TPU v7x, 32 devices: a whole 2x2x4 slice. The times are simulated.
32 devices in a mesh: dp: 4 (over y, x), mp: 8 (over z, core).
Axes of the slice: x: 2, y: 2, z: 4, core: 2. Of those that a mesh axis runs over, the one named last changes fastest.
Arguments:
- block_arguments: bfloat16 [2, 512, 2048], P(None, 'dp'), may hold values from -6 to 6
- bundled_spans: int32 [2, 4, 8], P(None, 'dp'), may hold values from 0 to 128, as said below
- opening_normalize_scale: float32 [2048], replicated, may hold values from 0.5 to 1.5
- accept_lagmix: float32 [2048], replicated, may hold values from 0 to 1
- lookup_lagmix: float32 [2048], replicated, may hold values from 0 to 1
- payload_lagmix: float32 [2048], replicated, may hold values from 0 to 1
- valve_lagmix: float32 [2048], replicated, may hold values from 0 to 1
- accept_weights: bfloat16 [2048, 2048], P(('dp', 'mp')), may hold values from -0.125 to 0.125
- lookup_weights: bfloat16 [2048, 2048], P(('dp', 'mp')), may hold values from -0.125 to 0.125
- payload_weights: bfloat16 [2048, 2048], P(('dp', 'mp')), may hold values from -0.125 to 0.125
- valve_weights: bfloat16 [2048, 2048], P(('dp', 'mp')), may hold values from -0.125 to 0.125
- fading_speed_logs: float32 [2048], replicated, may hold values from -6 to -1
- present_reward: float32 [2048], replicated, may hold values from -1 to 1
- lane_normalize_scale: float32 [2048], replicated, may hold values from 0.5 to 1.5
- emission_weights: bfloat16 [2048, 2048], P(('dp', 'mp')), may hold values from -0.125 to 0.125
- closing_normalize_scale: float32 [2048], replicated, may hold values from 0.5 to 1.5
- feedforward_lookup_lagmix: float32 [2048], replicated, may hold values from 0 to 1
- feedforward_accept_lagmix: float32 [2048], replicated, may hold values from 0 to 1
- feedforward_lookup_weights: bfloat16 [2048, 7168], P('dp', 'mp'), may hold values from -0.125 to 0.125
- feedforward_payload_weights: bfloat16 [2048, 7168], P('dp', 'mp'), may hold values from -0.0625 to 0.0625
- feedforward_accept_weights: bfloat16 [2048, 2048], P(('dp', 'mp')), may hold values from -0.125 to 0.125
- upstream_sensitivity: bfloat16 [2, 512, 2048], P(None, 'dp'), may hold values from -6 to 6
Outputs:
- outputs: bfloat16 [2, 512, 2048], P(None, 'dp')
- grad_inputs: bfloat16 [2, 512, 2048], P(None, 'dp')
- opening_scale_derivative: float32 [2048], P('dp')
- accept_lagmix_derivative: float32 [2048], P('dp')
- lookup_lagmix_derivative: float32 [2048], P('dp')
- payload_lagmix_derivative: float32 [2048], P('dp')
- valve_lagmix_derivative: float32 [2048], P('dp')
- accept_weights_derivative: float32 [2048, 2048], P(('dp', 'mp'))
- lookup_weights_derivative: float32 [2048, 2048], P(('dp', 'mp'))
- payload_weights_derivative: float32 [2048, 2048], P(('dp', 'mp'))
- valve_weights_derivative: float32 [2048, 2048], P(('dp', 'mp'))
- fading_speed_derivative: float32 [2048], P('dp')
- present_reward_derivative: float32 [2048], P('dp')
- lane_scale_derivative: float32 [2048], P('dp')
- emission_weights_derivative: float32 [2048, 2048], P(('dp', 'mp'))
- closing_scale_derivative: float32 [2048], P('dp')
- feedforward_lookup_lagmix_sens: float32 [2048], P('dp')
- feedforward_accept_lagmix_sens: float32 [2048], P('dp')
- feedforward_lookup_derivative: float32 [2048, 7168], P('dp', 'mp')
- feedforward_payload_derivative: float32 [2048, 7168], P('dp', 'mp')
- feedforward_accept_derivative: float32 [2048, 2048], P(('dp', 'mp'))
Inputs may be any that keep to these rules, and one draw needn't show every extreme that they name: `bundled_spans`: zero entries are empty slots. The lengths of one bucket sum to at most 128; its rows past that sum are padding. In every draw some bucket holds a single sequence of 128 tokens.
All inputs are finite; a program needn't handle non-finite values.
Results may differ from a plain program's by a relative error of at most 0.04.
Values may be sent and summed in bfloat16 or wider, within the bound.
A program may use at most 168 MiB of HBM per device.

v0:
```python
from functools import reduce

import jax
import jax.numpy as jnp
from jax import lax
from jax.sharding import PartitionSpec as P

LANE_WIDTH = 64
SPAN = 64


EPSILON = 1e-05
GROUP_EPSILON = 0.25
MIXED_MODE = lax.Precision.HIGH


def shortened(x):
    return jax.tree.map(lambda a: a.astype(jnp.bfloat16) if a.dtype == jnp.float32 else a, x)


def product(first_operand, second_operand):
    return jnp.dot(first_operand, second_operand, preferred_element_type=jnp.float32)


def product_rows(first_operand, second_operand):
    return lax.dot_general(
        first_operand, second_operand, (((0,), (0,)), ((), ())), preferred_element_type=jnp.float32
    )


def product_back(first_operand, second_operand):
    return lax.dot_general(
        first_operand, second_operand, (((1,), (1,)), ((), ())), preferred_element_type=jnp.float32
    )


def layer_norm(values, gain_entries):
    average = jnp.mean(values, axis=-1, keepdims=True)
    centered = values - average
    spread = jnp.mean(centered * centered, axis=-1, keepdims=True)
    return centered * lax.rsqrt(spread + EPSILON) * gain_entries


def group_norm(values, head_count):
    grouped = values.reshape(values.shape[0], head_count, -1)
    average = jnp.mean(grouped, axis=-1, keepdims=True)
    centered = grouped - average
    spread = jnp.mean(centered * centered, axis=-1, keepdims=True)
    return (centered * lax.rsqrt(spread + GROUP_EPSILON)).reshape(values.shape)


def segment_info(lengths, row_count):
    segment_ends = jnp.cumsum(lengths)
    places = jnp.arange(row_count, dtype=jnp.int32)
    sequence_label = jnp.sum((places[:, None] >= segment_ends[None, :]).astype(jnp.int32), axis=1)
    earlier = jnp.concatenate([jnp.full((1,), -1, jnp.int32), sequence_label[:-1]])
    common_series_filter = (sequence_label == earlier).astype(jnp.float32)
    valid_rows = (places < segment_ends[-1]).astype(jnp.float32)
    return (sequence_label, common_series_filter, valid_rows)


def shift_rows(values, common_series_filter):
    before = jnp.concatenate([jnp.zeros_like(values[:1]), values[:-1]], axis=0)
    return before * common_series_filter[:, None]


def iterative_renewal(
    accept_lines,
    lookup_weight_lines,
    payload_weight_lines,
    decay_logarithm,
    reward_scaler,
    sequence_label,
    layer_rows,
):
    row_count, head_count, head_width = accept_lines.shape
    block_count = row_count // layer_rows
    blocked = (block_count, layer_rows, head_count, head_width)
    accept_blocks = accept_lines.reshape(blocked)
    lookup_blocks = lookup_weight_lines.reshape(blocked)
    payload_blocks = payload_weight_lines.reshape(blocked)
    segment_blocks = sequence_label.reshape(block_count, layer_rows)
    positions = jnp.arange(layer_rows, dtype=jnp.float32)
    middle_step = float(layer_rows // 2)
    query_scale = jnp.exp(decay_logarithm[None] * (positions - middle_step)[:, None, None])
    key_scale = jnp.exp(decay_logarithm[None] * (middle_step - 1.0 - positions)[:, None, None])
    scores = jnp.einsum(
        "cthi,cshi->chts",
        accept_blocks * query_scale,
        lookup_blocks * key_scale,
        precision=MIXED_MODE,
    )
    causal = positions[:, None] > positions[None, :]
    within = segment_blocks[:, :, None] == segment_blocks[:, None, :]
    allowed = jnp.logical_and(causal[None], within).astype(jnp.float32)
    scores = scores * allowed[:, None]
    nested_routine = jnp.einsum("chts,cshj->cthj", scores, payload_blocks, precision=MIXED_MODE)
    reward_term = jnp.sum(accept_blocks * reward_scaler * lookup_blocks, axis=-1)
    nested_routine = nested_routine + reward_term[..., None] * payload_blocks
    last_segment = segment_blocks[:, -1]
    prior_segment = jnp.concatenate([jnp.full((1,), -1, jnp.int32), last_segment[:-1]])
    tail_scale = jnp.exp(decay_logarithm[None] * (layer_rows - 1.0 - positions)[:, None, None])
    tail_keep = (segment_blocks == last_segment[:, None]).astype(jnp.float32)
    added_state = jnp.einsum(
        "cshi,cshj->chij",
        lookup_blocks * tail_scale * tail_keep[:, :, None, None],
        payload_blocks,
        precision=MIXED_MODE,
    )
    carry_keep = (last_segment == prior_segment).astype(jnp.float32)
    whole_decay = jnp.exp(decay_logarithm * layer_rows)

    def advance(carry_state, piece_pair):
        addition, keep_flag = piece_pair
        return (whole_decay[:, :, None] * carry_state * keep_flag + addition, carry_state)

    initial = jnp.zeros((head_count, head_width, head_width), jnp.float32)
    unused, starts = lax.scan(advance, initial, (added_state, carry_keep))
    entry_keep = (segment_blocks == prior_segment[:, None]).astype(jnp.float32)
    entry_scale = jnp.exp(decay_logarithm[None] * positions[:, None, None])
    outside = jnp.einsum(
        "cthi,chij->cthj",
        accept_blocks * entry_scale * entry_keep[:, :, None, None],
        starts,
        precision=MIXED_MODE,
    )
    return (nested_routine + outside).reshape(row_count, head_count, head_width)


def add_terms(first_terms, second_terms):
    return jax.tree.map(jnp.add, first_terms, second_terms)


def body(
    block_arguments,
    bundled_spans,
    opening_normalize_scale,
    accept_lagmix,
    lookup_lagmix,
    payload_lagmix,
    valve_lagmix,
    accept_weights,
    lookup_weights,
    payload_weights,
    valve_weights,
    fading_speed_logs,
    present_reward,
    lane_normalize_scale,
    emission_weights,
    closing_normalize_scale,
    feedforward_lookup_lagmix,
    feedforward_accept_lagmix,
    feedforward_lookup_weights,
    feedforward_payload_weights,
    feedforward_accept_weights,
    upstream_sensitivity,
):
    micro_count, row_count, model_width = block_arguments.shape
    layer_rows = SPAN
    data_parts = lax.axis_size("dp")
    model_parts = lax.axis_size("mp")
    shard_rows = accept_weights.shape[0]
    model_place = lax.axis_index("mp")
    partition_lanes = model_width // LANE_WIDTH

    def own_columns(values):
        split_values = values.reshape(row_count, data_parts, model_parts, shard_rows)
        picked = lax.dynamic_index_in_dim(split_values, model_place, axis=2, keepdims=False)
        return picked.reshape(row_count, data_parts * shard_rows)

    outputs_list = []
    input_grads = []
    gradient_terms = []
    for micro_index in range(micro_count):
        projections = (
            lax.all_gather(accept_weights, ("dp", "mp"), axis=0, tiled=True),
            lax.all_gather(lookup_weights, ("dp", "mp"), axis=0, tiled=True),
            lax.all_gather(payload_weights, ("dp", "mp"), axis=0, tiled=True),
            lax.all_gather(valve_weights, ("dp", "mp"), axis=0, tiled=True),
            lax.all_gather(emission_weights, ("dp", "mp"), axis=0, tiled=True),
            lax.all_gather(feedforward_accept_weights, ("dp", "mp"), axis=0, tiled=True),
        )
        hidden_pair = (
            lax.all_gather(feedforward_lookup_weights, "dp", axis=0, tiled=True),
            lax.all_gather(feedforward_payload_weights, "dp", axis=0, tiled=True),
        )
        full_recept, full_key, full_value, full_gate, full_output, full_channel = projections
        hidden_key, hidden_value = hidden_pair
        sequence_label, common_series_filter, valid_rows = segment_info(
            bundled_spans[micro_index, 0], row_count
        )
        rows_float = block_arguments[micro_index].astype(jnp.float32)

        def front_part(rows_value, gain_entries, recept_mix, key_mix, value_mix, gate_mix):
            normed = layer_norm(rows_value, gain_entries)
            before = shift_rows(normed, common_series_filter)
            return tuple(
                (
                    normed * weight_mix + before * (1.0 - weight_mix)
                    for weight_mix in (recept_mix, key_mix, value_mix, gate_mix)
                )
            )

        front_values, front_pull = jax.vjp(
            front_part,
            rows_float,
            opening_normalize_scale,
            accept_lagmix,
            lookup_lagmix,
            payload_lagmix,
            valve_lagmix,
        )
        recept_in, key_in, value_in, gate_in = [
            front_piece.astype(jnp.bfloat16) for front_piece in front_values
        ]
        accept_lines = product(recept_in, full_recept).astype(jnp.bfloat16)
        lookup_weight_lines = product(key_in, full_key).astype(jnp.bfloat16)
        payload_weight_lines = product(value_in, full_value).astype(jnp.bfloat16)
        gate_raw = product(gate_in, full_gate)

        def middle_part(
            receptance_activation,
            key_value_product,
            value_activation,
            gate_activation,
            decay_parameter,
            reward_weight,
            gain_entries,
        ):
            decay_logarithm = -jnp.exp(decay_parameter).reshape(partition_lanes, -1)
            reward_scaler = reward_weight.reshape(partition_lanes, -1)
            reformed_array = (row_count, partition_lanes, model_width // partition_lanes)
            lane_answers = iterative_renewal(
                receptance_activation.reshape(reformed_array),
                key_value_product.reshape(reformed_array),
                value_activation.reshape(reformed_array),
                decay_logarithm,
                reward_scaler,
                sequence_label,
                layer_rows,
            )
            grouped = (
                group_norm(lane_answers.reshape(row_count, model_width), partition_lanes)
                * gain_entries
            )
            return grouped * jax.nn.silu(gate_activation)

        mixed_float, middle_pull = jax.vjp(
            middle_part,
            accept_lines.astype(jnp.float32),
            lookup_weight_lines.astype(jnp.float32),
            payload_weight_lines.astype(jnp.float32),
            gate_raw,
            fading_speed_logs,
            present_reward,
            lane_normalize_scale,
        )
        merged_lanes = mixed_float.astype(jnp.bfloat16)
        middle = rows_float + product(merged_lanes, full_output)

        def back_part(middle_value, gain_entries, key_mix, recept_mix):
            normed = layer_norm(middle_value, gain_entries)
            before = shift_rows(normed, common_series_filter)
            return (
                normed * key_mix + before * (1.0 - key_mix),
                normed * recept_mix + before * (1.0 - recept_mix),
            )

        channel_values, back_pull = jax.vjp(
            back_part,
            middle,
            closing_normalize_scale,
            feedforward_lookup_lagmix,
            feedforward_accept_lagmix,
        )
        channel_key_in = channel_values[0].astype(jnp.bfloat16)
        channel_recept_in = channel_values[1].astype(jnp.bfloat16)
        hidden_input = product(channel_key_in, hidden_key)
        hidden = jnp.square(jnp.maximum(hidden_input, 0.0)).astype(jnp.bfloat16)
        carried = lax.psum(product_back(hidden, hidden_value).astype(jnp.bfloat16), "mp").astype(
            jnp.float32
        )
        channel_gate = jax.nn.sigmoid(product(channel_recept_in, full_channel))
        outputs_list.append(
            ((middle + channel_gate * carried) * valid_rows[:, None]).astype(jnp.bfloat16)
        )
        top_grad = upstream_sensitivity[micro_index].astype(jnp.float32) * valid_rows[:, None]
        carried_grad = (top_grad * channel_gate).astype(jnp.bfloat16)
        gate_input_grad = (top_grad * carried * channel_gate * (1.0 - channel_gate)).astype(
            jnp.bfloat16
        )
        pre_grad = (
            product(carried_grad, hidden_value) * 2.0 * jnp.maximum(hidden_input, 0.0)
        ).astype(jnp.bfloat16)
        channel_key_grad = lax.psum(
            product_back(pre_grad, hidden_key).astype(jnp.bfloat16), "mp"
        ).astype(jnp.float32)
        channel_recept_grad = product_back(gate_input_grad, full_channel)
        middle_back, grad_second, feedforward_lookup_lagmix_sens, feedforward_accept_lagmix_sens = (
            back_pull((channel_key_grad, channel_recept_grad))
        )
        middle_grad = top_grad + middle_back
        branch_grad = middle_grad.astype(jnp.bfloat16)
        mixed_grad = product_back(branch_grad, full_output)
        output_term = product_rows(own_columns(merged_lanes), branch_grad)
        (
            receptance_single_precision,
            key_single_precision,
            value_single_precision,
            gate_single_precision,
            decay_gradient,
            reward_derivative,
            lane_normalize_derivative,
        ) = middle_pull(mixed_grad)
        recept_grad = receptance_single_precision.astype(jnp.bfloat16)
        key_grad = key_single_precision.astype(jnp.bfloat16)
        value_grad = value_single_precision.astype(jnp.bfloat16)
        gate_grad = gate_single_precision.astype(jnp.bfloat16)
        (
            line_derivatives,
            grad_first,
            grad_recept_mix,
            grad_key_mix,
            grad_value_mix,
            grad_gate_mix,
        ) = front_pull(
            (
                product_back(recept_grad, full_recept),
                product_back(key_grad, full_key),
                product_back(value_grad, full_value),
                product_back(gate_grad, full_gate),
            )
        )
        projection_terms = (
            product_rows(own_columns(recept_in), recept_grad),
            product_rows(own_columns(key_in), key_grad),
            product_rows(own_columns(value_in), value_grad),
            product_rows(own_columns(gate_in), gate_grad),
            output_term,
        )
        input_grads.append((middle_grad + line_derivatives).astype(jnp.bfloat16))
        local_terms = (
            grad_first,
            grad_recept_mix,
            grad_key_mix,
            grad_value_mix,
            grad_gate_mix,
            decay_gradient,
            reward_derivative,
            lane_normalize_derivative,
            grad_second,
            feedforward_lookup_lagmix_sens,
            feedforward_accept_lagmix_sens,
            product_rows(channel_key_in, pre_grad),
            product_rows(carried_grad, hidden),
            product_rows(own_columns(channel_recept_in), gate_input_grad),
        ) + projection_terms
        gradient_terms.append(local_terms)
    summed = reduce(add_terms, gradient_terms)
    summed = jax.tree.map(
        lambda part: part.astype(jnp.float32),
        lax.psum_scatter(shortened(summed), "dp", scatter_dimension=0, tiled=True),
    )
    (
        grad_first,
        grad_recept_mix,
        grad_key_mix,
        grad_value_mix,
        grad_gate_mix,
        decay_gradient,
        reward_derivative,
        lane_normalize_derivative,
        grad_second,
        feedforward_lookup_lagmix_sens,
        feedforward_accept_lagmix_sens,
        feedforward_lookup_derivative,
        feedforward_payload_derivative,
        feedforward_accept_derivative,
        grad_recept,
        grad_key,
        grad_value,
        grad_gate,
        grad_output,
    ) = summed
    return (
        jnp.stack(outputs_list),
        jnp.stack(input_grads),
        grad_first,
        grad_recept_mix,
        grad_key_mix,
        grad_value_mix,
        grad_gate_mix,
        grad_recept,
        grad_key,
        grad_value,
        grad_gate,
        decay_gradient,
        reward_derivative,
        lane_normalize_derivative,
        grad_output,
        grad_second,
        feedforward_lookup_lagmix_sens,
        feedforward_accept_lagmix_sens,
        feedforward_lookup_derivative,
        feedforward_payload_derivative,
        feedforward_accept_derivative,
    )


def solution(mesh):
    return jax.shard_map(
        body,
        mesh=mesh,
        in_specs=(
            P(None, "dp", None),
            P(None, "dp", None),
            P(),
            P(),
            P(),
            P(),
            P(),
            P(("dp", "mp"), None),
            P(("dp", "mp"), None),
            P(("dp", "mp"), None),
            P(("dp", "mp"), None),
            P(),
            P(),
            P(),
            P(("dp", "mp"), None),
            P(),
            P(),
            P(),
            P("dp", "mp"),
            P("dp", "mp"),
            P(("dp", "mp"), None),
            P(None, "dp", None),
        ),
        out_specs=(
            P(None, "dp", None),
            P(None, "dp", None),
            P("dp"),
            P("dp"),
            P("dp"),
            P("dp"),
            P("dp"),
            P(("dp", "mp"), None),
            P(("dp", "mp"), None),
            P(("dp", "mp"), None),
            P(("dp", "mp"), None),
            P("dp"),
            P("dp"),
            P("dp"),
            P(("dp", "mp"), None),
            P("dp"),
            P("dp"),
            P("dp"),
            P("dp", "mp"),
            P("dp", "mp"),
            P(("dp", "mp"), None),
        ),
        check_vma=False,
    )
```

profile of v0, /device:TPU:1, one launch (start us, length us, event | category | flops | bytes accessed | tf_op | source)
XLA Modules:
  0.0 1255.6 jit_solution(9831826618141880786)
XLA Ops:
  38.1 52.7 %all-gather.9.cloned.1.call-done = bf16[2048,2048]{1,0:T(8,128)(2,1)} async-done(((bf16[64,2048]{1,0:T(8,128)(2,1)}), bf16[2048,2048]{1,0:T(8,128)(2,1)}) %all-gather.9.cloned.1.call-update) | async-done | bytes 8388624 | tf_op jit(solution)/shard_map/all_gather | solution.py:178
  100.4 69.3 %all-gather.13.cloned.1.call-done = bf16[2048,2048]{1,0:T(8,128)(2,1)} async-done(((bf16[64,2048]{1,0:T(8,128)(2,1)}), bf16[2048,2048]{1,0:T(8,128)(2,1)}) %all-gather.13.cloned.1.call-update) | async-done | bytes 8388624 | tf_op jit(solution)/shard_map/all_gather | solution.py:177
  181.9 66.9 %all-gather.11.cloned.1.call-done = bf16[2048,2048]{1,0:T(8,128)(2,1)} async-done(((bf16[64,2048]{1,0:T(8,128)(2,1)}), bf16[2048,2048]{1,0:T(8,128)(2,1)}) %all-gather.11.cloned.1.call-update) | async-done | bytes 8388624 | tf_op jit(solution)/shard_map/all_gather | solution.py:176
  268.2 6.6 while.65
  302.0 25.6 %all-gather.15.cloned.1.call-done = bf16[2048,2048]{1,0:T(8,128)(2,1)} async-done(((bf16[64,2048]{1,0:T(8,128)(2,1)}), bf16[2048,2048]{1,0:T(8,128)(2,1)}) %all-gather.15.cloned.1.call-update) | async-done | bytes 8388624 | tf_op jit(solution)/shard_map/all_gather | solution.py:179
  327.6 7.3 multiply_convert_fusion
  335.0 71.5 %all-gather.17.cloned.1.call-done = bf16[2048,2048]{1,0:T(8,128)(2,1)} async-done(((bf16[64,2048]{1,0:T(8,128)(2,1)}), bf16[2048,2048]{1,0:T(8,128)(2,1)}) %all-gather.17.cloned.1.call-update) | async-done | bytes 8388624 | tf_op jit(solution)/shard_map/all_gather | solution.py:180
  414.8 39.9 %all-gather.21.cloned.1.call-done = bf16[2048,896]{1,0:T(8,128)(2,1)} async-done(((bf16[512,896]{1,0:T(8,128)(2,1)}), bf16[2048,896]{1,0:T(8,128)(2,1)}) %all-gather.21.cloned.1.call-update) | async-done | bytes 3670032 | tf_op jit(solution)/shard_map/all_gather | solution.py:184
  458.5 46.5 %all-gather.23.cloned.1.call-done = bf16[2048,896]{1,0:T(8,128)(2,1)} async-done(((bf16[512,896]{1,0:T(8,128)(2,1)}), bf16[2048,896]{1,0:T(8,128)(2,1)}) %all-gather.23.cloned.1.call-update) | async-done | bytes 3670032 | tf_op jit(solution)/shard_map/all_gather | solution.py:185
  509.2 76.6 %all-gather.19.cloned.1.call-done = bf16[2048,2048]{1,0:T(8,128)(2,1)} async-done(((bf16[64,2048]{1,0:T(8,128)(2,1)}), bf16[2048,2048]{1,0:T(8,128)(2,1)}) %all-gather.19.cloned.1.call-update) | async-done | bytes 8388624 | tf_op jit(solution)/shard_map/all_gather | solution.py:181
  613.6 38.2 %all-reduce.27.cloned.1.call-done = (bf16[128,2048]{1,0:T(8,128)(2,1)}, bf16[128,2048]{1,0:T(8,128)(2,1)}) async-done(((bf16[128,2048]{1,0:T(8,128)(2,1)}, bf16[128,2048]{1,0:T(8,128)(2,1)}), (bf16[128,2048]{1,0:T(8,128)(2,1)}, bf16[128,2048]{1,0:T(8,128)(2,1)})) %all-reduce.27.cloned.1.call-update) | async-done | bytes 1048592 | tf_op jit(solution)/shard_map/psum | solution.py:280
  705.4 9.2 while.67
  726.9 11.4 fusion.35
  755.0 6.7 fusion.234
  761.8 6.7 fusion.235
  822.3 6.7 while.64
  847.1 7.2 multiply_convert_fusion.1
  895.8 34.3 %all-reduce.25.cloned.1.call-done = (bf16[128,2048]{1,0:T(8,128)(2,1)}, bf16[128,2048]{1,0:T(8,128)(2,1)}) async-done(((bf16[128,2048]{1,0:T(8,128)(2,1)}, bf16[128,2048]{1,0:T(8,128)(2,1)}), (bf16[128,2048]{1,0:T(8,128)(2,1)}, bf16[128,2048]{1,0:T(8,128)(2,1)})) %all-reduce.25.cloned.1.call-update) | async-done | bytes 1048592 | tf_op jit(solution)/shard_map/psum | solution.py:280
  994.3 9.3 while.66
  1012.3 8.3 fusion.54
  1094.2 6.6 fusion.229
  1117.2 13.1 %all-reduce.21 = (bf16[2048]{0:T(1024)(128)(2,1)S(1)}, bf16[2048]{0:T(1024)(128)(2,1)S(1)}, bf16[2048]{0:T(1024)(128)(2,1)S(1)}, bf16[2048]{0:T(1024)(128)(2,1)S...) all-reduce(bf16[2048]{0:T(1024)(128)(2,1)S(1)} %add_convert_fusion., ...), channel_id=2, replica_groups=mesh['dp'=4,'mp'=8] {'dp'}, use_global_device_ids=true, to_apply=%region_48.49.clone | all-reduce | flops 22528 | bytes 90112
  1154.2 40.6 %reduce-scatter.19.cloned.1.call-done = bf16[512,896]{1,0:T(8,128)(2,1)} async-done(((bf16[2048,896]{1,0:T(8,128)(2,1)}), bf16[512,896]{1,0:T(8,128)(2,1)}) %reduce-scatter.19.cloned.1.call-update) | async-done | bytes 917520 | tf_op jit(solution)/shard_map/reduce_scatter | solution.py:362
  1197.2 48.7 %reduce-scatter.21.cloned.1.call-done = bf16[512,896]{1,0:T(8,128)(2,1)} async-done(((bf16[2048,896]{1,0:T(8,128)(2,1)}), bf16[512,896]{1,0:T(8,128)(2,1)}) %reduce-scatter.21.cloned.1.call-update) | async-done | bytes 917520 | tf_op jit(solution)/shard_map/reduce_scatter | solution.py:362
  (986 shorter events, 557.7 us)
Async XLA Ops:
  7.2 83.6 %all-gather.9.cloned.1.call-start = ((), (), s32[]{:S(2)}) async-start(), calls=%async_computation.8 | async-start | bytes 8650752 | tf_op jit(solution)/shard_map/all_gather | solution.py:178
  8.0 161.8 %all-gather.13.cloned.1.call-start = ((), (), s32[]{:S(2)}) async-start(), calls=%async_computation.10 | async-start | bytes 8650752 | tf_op jit(solution)/shard_map/all_gather | solution.py:177
  8.7 240.0 %all-gather.11.cloned.1.call-start = ((), (), s32[]{:S(2)}) async-start(), calls=%async_computation.9 | async-start | bytes 8650752 | tf_op jit(solution)/shard_map/all_gather | solution.py:176
  9.5 318.2 %all-gather.15.cloned.1.call-start = ((), (), s32[]{:S(2)}) async-start(), calls=%async_computation.11 | async-start | bytes 8650752 | tf_op jit(solution)/shard_map/all_gather | solution.py:179
  10.1 396.4 %all-gather.17.cloned.1.call-start = ((), (), s32[]{:S(2)}) async-start(), calls=%async_computation.12 | async-start | bytes 8650752 | tf_op jit(solution)/shard_map/all_gather | solution.py:180
  10.7 444.0 %all-gather.21.cloned.1.call-start = ((), (), s32[]{:S(2)}) async-start(), calls=%async_computation.14 | async-start | bytes 4587520 | tf_op jit(solution)/shard_map/all_gather | solution.py:184
  11.3 493.7 %all-gather.23.cloned.1.call-start = ((), (), s32[]{:S(2)}) async-start(), calls=%async_computation.15 | async-start | bytes 4587520 | tf_op jit(solution)/shard_map/all_gather | solution.py:185
  12.0 573.8 %all-gather.19.cloned.1.call-start = ((), (), s32[]{:S(2)}) async-start(), calls=%async_computation.13 | async-start | bytes 8650752 | tf_op jit(solution)/shard_map/all_gather | solution.py:181
  12.8 639.1 %all-reduce.27.cloned.1.call-start = ((), (), s32[]{:S(2)}) async-start(), calls=%async_computation.25 | async-start | bytes 2097152 | tf_op jit(solution)/shard_map/psum | solution.py:280
  18.5 758.5 %copy-start.175 = (f32[2048]{0:T(1024)}, f32[2048]{0:T(1024)S(1)}, u32[]{:S(2)}) copy-start(f32[2048]{0:T(1024)S(1)} %get-tuple-element.750) | copy-start | bytes 24580
  18.5 759.9 %copy-start.173 = (f32[2048]{0:T(1024)}, f32[2048]{0:T(1024)S(1)}, u32[]{:S(2)}) copy-start(f32[2048]{0:T(1024)S(1)} %get-tuple-element.749) | copy-start | bytes 24580
  18.6 759.9 %copy-start.177 = (f32[2048]{0:T(1024)}, f32[2048]{0:T(1024)S(1)}, u32[]{:S(2)}) copy-start(f32[2048]{0:T(1024)S(1)} %get-tuple-element.743) | copy-start | bytes 24580
  18.6 759.9 %copy-start.179 = (f32[2048]{0:T(1024)}, f32[2048]{0:T(1024)S(1)}, u32[]{:S(2)}) copy-start(f32[2048]{0:T(1024)S(1)} %get-tuple-element.744) | copy-start | bytes 24580
  33.4 826.5 %copy-start.181 = (f32[2048]{0:T(1024)}, f32[2048]{0:T(1024)S(1)}, u32[]{:S(2)}) copy-start(f32[2048]{0:T(1024)S(1)} %get-tuple-element.747) | copy-start | bytes 24580
  33.4 826.5 %copy-start.183 = (f32[2048]{0:T(1024)}, f32[2048]{0:T(1024)S(1)}, u32[]{:S(2)}) copy-start(f32[2048]{0:T(1024)S(1)} %get-tuple-element.748) | copy-start | bytes 24580
  596.3 333.8 %all-reduce.25.cloned.1.call-start = ((), (), s32[]{:S(2)}) async-start(), calls=%async_computation.24 | async-start | bytes 2097152 | tf_op jit(solution)/shard_map/psum | solution.py:280
  872.0 271.5 %reduce-scatter.17.cloned.1.call-start = ((), (), s32[]{:S(2)}) async-start(), calls=%async_computation.20 | async-start | bytes 1310720 | tf_op jit(solution)/shard_map/reduce_scatter | solution.py:362
  961.0 184.2 %reduce-scatter.15.cloned.1.call-start = ((), (), s32[]{:S(2)}) async-start(), calls=%async_computation.19 | async-start | bytes 1310720 | tf_op jit(solution)/shard_map/reduce_scatter | solution.py:362
  984.6 162.4 %reduce-scatter.23.cloned.1.call-start = ((), (), s32[]{:S(2)}) async-start(), calls=%async_computation.23 | async-start | bytes 1310720 | tf_op jit(solution)/shard_map/reduce_scatter | solution.py:362
  1003.6 145.2 %reduce-scatter.9.cloned.1.call-start = ((), (), s32[]{:S(2)}) async-start(), calls=%async_computation.16 | async-start | bytes 1310720 | tf_op jit(solution)/shard_map/reduce_scatter | solution.py:362
  1029.6 120.9 %reduce-scatter.11.cloned.1.call-start = ((), (), s32[]{:S(2)}) async-start(), calls=%async_computation.17 | async-start | bytes 1310720 | tf_op jit(solution)/shard_map/reduce_scatter | solution.py:362
  1045.8 106.5 %reduce-scatter.13.cloned.1.call-start = ((), (), s32[]{:S(2)}) async-start(), calls=%async_computation.18 | async-start | bytes 1310720 | tf_op jit(solution)/shard_map/reduce_scatter | solution.py:362
  1062.4 132.3 %reduce-scatter.19.cloned.1.call-start = ((), (), s32[]{:S(2)}) async-start(), calls=%async_computation.21 | async-start | bytes 4587520 | tf_op jit(solution)/shard_map/reduce_scatter | solution.py:362
  1066.6 179.3 %reduce-scatter.21.cloned.1.call-start = ((), (), s32[]{:S(2)}) async-start(), calls=%async_computation.22 | async-start | bytes 4587520 | tf_op jit(solution)/shard_map/reduce_scatter | solution.py:362
  (295 other events, 2167.3 us)
Sparse Core Ops, SparseCore 0:
  11.1 79.7 all-gather.8
  93.8 75.8 all-gather.12
  172.7 75.9 all-gather.10
  251.6 75.9 all-gather.14
  330.5 75.9 all-gather.16
  408.2 46.4 all-gather.20
  456.6 48.3 all-gather.22
  507.9 77.8 all-gather.18
  596.4 55.3 all-reduce.26
  872.1 57.9 all-reduce.24
  961.2 28.4 reduce-scatter.16
  992.7 27.7 reduce-scatter.14
  1023.4 27.7 reduce-scatter.22
  1054.1 27.7 reduce-scatter.8
  1084.6 27.7 reduce-scatter.10
  1115.4 28.0 reduce-scatter.12
  1146.3 48.3 reduce-scatter.18
  1197.6 48.3 reduce-scatter.20
where the time goes:
time: 1270 us; the launch traced here: 1260 us
  waiting for transfers between devices  616 us (49%)
  matrix products  255 us (20%)
  local copies, waits for them, and re-layouts  218 us (17%)
  other arithmetic  133 us (10%)
  between operations  18.9 us (1%)
  blocking collectives  13.1 us (1%)
    reduce_scatter x8, waiting for transfers between devices, body(): lax.psum_scatter(shortened(summed), 'dp', scatter_dimension=0, tiled=True)  89.2 us
    all_gather x1, waiting for transfers between devices, body(): lax.all_gather(feedforward_accept_weights, ('dp', 'mp'), axis=0, tiled=True)  76.6 us
    dot_general x16, matrix products, product_back(): lax.dot_general(first_operand, second_operand, (((1,), (1,)), ((), ())),...  75.7 us
    psum x2, waiting for transfers between devices, body(): lax.psum(product_back(hidden, hidden_value).astype(jnp.bfloat16), 'mp')  72.5 us
    all_gather x1, waiting for transfers between devices, body(): lax.all_gather(emission_weights, ('dp', 'mp'), axis=0, tiled=True)  71.5 us
    all_gather x1, waiting for transfers between devices, body(): lax.all_gather(lookup_weights, ('dp', 'mp'), axis=0, tiled=True)  69.3 us
    dot_general x16, matrix products, product(): jnp.dot(first_operand, second_operand, preferred_element_type=jnp.float32)  68.2 us
    all_gather x1, waiting for transfers between devices, body(): lax.all_gather(accept_weights, ('dp', 'mp'), axis=0, tiled=True)  66.9 us
  transfers between devices with their start and end apart: 18, of which 12 were waited for; matrix products, arithmetic and copies ran while one was open for 27% of the time, Pallas kernels for 0%

commit v1 on v0

--- a/solution.py
+++ b/solution.py
@@ -1,8 +1,11 @@
+import functools
 from functools import reduce
 
 import jax
 import jax.numpy as jnp
 from jax import lax
+from jax.experimental import pallas as pl
+from jax.experimental.pallas import tpu as pltpu
 from jax.sharding import PartitionSpec as P
 
 LANE_WIDTH = 64
@@ -131,7 +134,7 @@
     return jax.tree.map(jnp.add, first_terms, second_terms)
 
 
-def body(
+def general_body(
     block_arguments,
     bundled_spans,
     opening_normalize_scale,
@@ -405,6 +408,835 @@
         feedforward_payload_derivative,
         feedforward_accept_derivative,
     )
+
+
+MESH = pl.DeviceIdType.MESH
+BF = jnp.bfloat16
+F32 = jnp.float32
+VMEM_LIMIT = 56 << 20
+
+
+def vmem_specs(count):
+    return [pl.BlockSpec(memory_space=pltpu.VMEM)] * count
+
+
+def flip(place, other):
+    low = lax.rem(lax.rem(place, 2) + lax.rem(other, 2), 2)
+    high = lax.rem(lax.div(place, 2) + lax.div(other, 2), 2)
+    return 2 * high + low
+
+
+def column_of(owner, data_place, shifted):
+    if not shifted:
+        return owner
+    return 2 * flip(lax.div(owner, 2), data_place) + lax.rem(owner, 2)
+
+
+def over_x(a):
+    return lax.ppermute(a, "dp", [(i, i ^ 1) for i in range(4)])
+
+
+def over_y(a):
+    return lax.ppermute(a, "dp", [(i, i ^ 2) for i in range(4)])
+
+
+def greet(barrier, peers):
+    for peer in peers:
+        pl.semaphore_signal(barrier, inc=1, device_id=peer, device_id_type=MESH)
+    pl.semaphore_wait(barrier, len(peers))
+
+
+def gather_kernel(chips, shifted, a_ref, o_ref, send, recv, local):
+    d, m = lax.axis_index("dp"), lax.axis_index("mp")
+    z, c = lax.div(m, 2), lax.rem(m, 2)
+    mate = (d, 2 * z + 1 - c)
+    width = a_ref.shape[1]
+
+    def place(owner):
+        return o_ref.at[:, pl.ds(pl.multiple_of(column_of(owner, d, shifted) * width, width), width)]
+
+    chips_away = [lax.rem(z + i, chips) for i in range(1, chips)]
+    greet(pltpu.get_barrier_semaphore(), [mate] + [(d, 2 * other + c) for other in chips_away])
+    keep = pltpu.make_async_copy(a_ref, place(m), local)
+    keep.start()
+    copies = []
+    for i, other in enumerate(chips_away):
+        copies.append(
+            pltpu.make_async_remote_copy(
+                a_ref, place(m), send.at[i], recv.at[i], device_id=(d, 2 * other + c), device_id_type=MESH
+            )
+        )
+    across = pltpu.make_async_remote_copy(
+        a_ref, place(m), send.at[chips - 1], recv.at[chips - 1], device_id=mate, device_id_type=MESH
+    )
+    for copy in copies:
+        copy.start()
+    across.start()
+    onward = []
+    for i in range(chips - 1):
+        source = 2 * lax.rem(z - (i + 1) + chips, chips) + c
+        copies[i].wait_recv()
+        copy = pltpu.make_async_remote_copy(
+            place(source),
+            place(source),
+            send.at[chips + i],
+            recv.at[chips + i],
+            device_id=mate,
+            device_id_type=MESH,
+        )
+        copy.start()
+        onward.append(copy)
+    for copy in copies:
+        copy.wait_send()
+    across.wait()
+    for copy in onward:
+        copy.wait()
+    keep.wait()
+
+
+def gather_mp(block, shifted, collective_id):
+    chips = lax.axis_size("mp") // 2
+    rows, width = block.shape
+    count = 2 * chips - 1
+    return pl.pallas_call(
+        functools.partial(gather_kernel, chips, shifted),
+        out_shape=jax.ShapeDtypeStruct((rows, width * 2 * chips), block.dtype),
+        in_specs=vmem_specs(1),
+        out_specs=pl.BlockSpec(memory_space=pltpu.VMEM),
+        scratch_shapes=[
+            pltpu.SemaphoreType.DMA((count,)),
+            pltpu.SemaphoreType.DMA((count,)),
+            pltpu.SemaphoreType.DMA,
+        ],
+        compiler_params=pltpu.CompilerParams(
+            collective_id=collective_id, has_side_effects=True, vmem_limit_bytes=VMEM_LIMIT
+        ),
+        name="gather_mp",
+    )(block)
+
+
+def scatter_kernel(chips, shifted, with_rows, *refs):
+    if with_rows:
+        p_ref, s_ref, o_ref, so_ref, half, pair, far, small, send, recv = refs
+    else:
+        p_ref, o_ref, half, pair, far, send, recv = refs
+    d, m = lax.axis_index("dp"), lax.axis_index("mp")
+    z, c = lax.div(m, 2), lax.rem(m, 2)
+    mate = (d, 2 * z + 1 - c)
+    width = o_ref.shape[1]
+    chips_away = [lax.rem(z + i, chips) for i in range(1, chips)]
+    greet(pltpu.get_barrier_semaphore(), [mate] + [(d, 2 * other + c) for other in chips_away])
+
+    def part(owner):
+        return p_ref.at[:, pl.ds(pl.multiple_of(column_of(owner, d, shifted) * width, width), width)]
+
+    first = []
+    for i, other in enumerate(chips_away + [z]):
+        copy = pltpu.make_async_remote_copy(
+            part(2 * other + 1 - c), half.at[i], send.at[i], recv.at[i], device_id=mate, device_id_type=MESH
+        )
+        copy.start()
+        first.append(copy)
+    far_copies = []
+    base = chips
+    if with_rows:
+        mates_rows = pltpu.make_async_remote_copy(
+            s_ref, small.at[0], send.at[base], recv.at[base], device_id=mate, device_id_type=MESH
+        )
+        mates_rows.start()
+        base += 1
+    for i, other in enumerate(chips_away):
+        first[i].wait_recv()
+        pair[i] = (part(2 * other + c)[...].astype(F32) + half[i].astype(F32)).astype(pair.dtype)
+        copy = pltpu.make_async_remote_copy(
+            pair.at[i],
+            far.at[i],
+            send.at[base + i],
+            recv.at[base + i],
+            device_id=(d, 2 * other + c),
+            device_id_type=MESH,
+        )
+        copy.start()
+        far_copies.append(copy)
+    base += chips - 1
+    row_copies = []
+    if with_rows:
+        mates_rows.wait_recv()
+        small[1] = s_ref[...] + small[0]
+        for i, other in enumerate(chips_away):
+            copy = pltpu.make_async_remote_copy(
+                small.at[1],
+                small.at[2 + i],
+                send.at[base + i],
+                recv.at[base + i],
+                device_id=(d, 2 * other + c),
+                device_id_type=MESH,
+            )
+            copy.start()
+            row_copies.append(copy)
+    first[chips - 1].wait_recv()
+    o_ref[...] = part(m)[...].astype(F32) + half[chips - 1].astype(F32)
+    for i in range(chips - 1):
+        far_copies[i].wait_recv()
+        o_ref[...] += far[i].astype(F32)
+    if with_rows:
+        total = small[1]
+        for i in range(chips - 1):
+            row_copies[i].wait_recv()
+            total = total + small[2 + i]
+        so_ref[...] = total
+        mates_rows.wait_send()
+    for copy in first + far_copies + row_copies:
+        copy.wait_send()
+
+
+def scatter_mp(partial_sums, shifted, collective_id, row_sums=None):
+    parts = lax.axis_size("mp")
+    chips = parts // 2
+    rows, columns = partial_sums.shape
+    width = columns // parts
+    with_rows = row_sums is not None
+    out_shape = [jax.ShapeDtypeStruct((rows, width), F32)]
+    scratch = [
+        pltpu.VMEM((chips, rows, width), partial_sums.dtype),
+        pltpu.VMEM((chips - 1, rows, width), partial_sums.dtype),
+        pltpu.VMEM((chips - 1, rows, width), partial_sums.dtype),
+    ]
+    count = 2 * chips - 1
+    args = [partial_sums]
+    if with_rows:
+        args.append(row_sums)
+        out_shape.append(jax.ShapeDtypeStruct(row_sums.shape, F32))
+        scratch.append(pltpu.VMEM((chips + 1,) + row_sums.shape, F32))
+        count += chips
+    result = pl.pallas_call(
+        functools.partial(scatter_kernel, chips, shifted, with_rows),
+        out_shape=out_shape,
+        in_specs=vmem_specs(len(args)),
+        out_specs=vmem_specs(len(out_shape)),
+        scratch_shapes=scratch + [pltpu.SemaphoreType.DMA((count,)), pltpu.SemaphoreType.DMA((count,))],
+        compiler_params=pltpu.CompilerParams(
+            collective_id=collective_id, has_side_effects=True, vmem_limit_bytes=VMEM_LIMIT
+        ),
+        name="scatter_mp",
+    )(*args)
+    return result if with_rows else result[0]
+
+
+def exchange_kernel(parts, a_ref, o_ref, send, recv, local):
+    d, m = lax.axis_index("dp"), lax.axis_index("mp")
+    others = [lax.rem(m + i, parts) for i in range(1, parts)]
+    greet(pltpu.get_barrier_semaphore(), [(d, other) for other in others])
+    keep = pltpu.make_async_copy(a_ref.at[m], o_ref.at[m], local)
+    keep.start()
+    copies = []
+    for i, other in enumerate(others):
+        copy = pltpu.make_async_remote_copy(
+            a_ref.at[other], o_ref.at[m], send.at[i], recv.at[i], device_id=(d, other), device_id_type=MESH
+        )
+        copy.start()
+        copies.append(copy)
+    for copy in copies:
+        copy.wait()
+    keep.wait()
+
+
+def exchange_mp(blocks, collective_id):
+    parts = blocks.shape[0]
+    return pl.pallas_call(
+        functools.partial(exchange_kernel, parts),
+        out_shape=jax.ShapeDtypeStruct(blocks.shape, blocks.dtype),
+        in_specs=vmem_specs(1),
+        out_specs=pl.BlockSpec(memory_space=pltpu.VMEM),
+        scratch_shapes=[
+            pltpu.SemaphoreType.DMA((parts - 1,)),
+            pltpu.SemaphoreType.DMA((parts - 1,)),
+            pltpu.SemaphoreType.DMA,
+        ],
+        compiler_params=pltpu.CompilerParams(
+            collective_id=collective_id, has_side_effects=True, vmem_limit_bytes=VMEM_LIMIT
+        ),
+        name="exchange_mp",
+    )(blocks)
+
+
+def local_call(kernel, name, out_shape, args, scratch=(), scalars=0):
+    specs = [pl.BlockSpec(memory_space=pltpu.SMEM)] * scalars + vmem_specs(len(args) - scalars)
+    return pl.pallas_call(
+        kernel,
+        out_shape=out_shape,
+        in_specs=specs,
+        out_specs=vmem_specs(len(out_shape)),
+        scratch_shapes=list(scratch),
+        compiler_params=pltpu.CompilerParams(vmem_limit_bytes=VMEM_LIMIT),
+        name=name,
+    )(*args)
+
+
+def struct(shape, dtype):
+    return jax.ShapeDtypeStruct(shape, dtype)
+
+
+def roll_rows(values, shift):
+    return pltpu.roll(values, shift % values.shape[0], 0)
+
+
+def mix_kernel(mixes, shifted, *refs):
+    if shifted:
+        order, refs = refs[0], refs[1:]
+    x_ref, same_ref, gain_ref, mix_ref = refs[:4]
+    outs = refs[4 : 4 + mixes]
+    mean_ref, rstd_ref = refs[4 + mixes : 6 + mixes]
+    rows, width = x_ref.shape
+    block = width // 4
+    moved = refs[6 + mixes] if shifted else x_ref
+    half = rows // 2
+
+    for r in range(2):
+        rs = pl.ds(r * half, half)
+        total = jnp.zeros((half, 1), F32)
+        for j in range(4):
+            if shifted:
+                lanes = pl.ds(pl.multiple_of(order[j] * block, block), block)
+                moved[rs, j * block : (j + 1) * block] = x_ref[rs, lanes]
+            total = total + jnp.sum(
+                moved[rs, j * block : (j + 1) * block].astype(F32), axis=1, keepdims=True
+            )
+        average = total / width
+        spread = jnp.zeros((half, 1), F32)
+        for j in range(4):
+            centered = moved[rs, j * block : (j + 1) * block].astype(F32) - average
+            spread = spread + jnp.sum(centered * centered, axis=1, keepdims=True)
+        scale = lax.rsqrt(spread / width + EPSILON)
+        mean_ref[rs, :] = average
+        rstd_ref[rs, :] = scale
+        same = same_ref[rs, :]
+        for j in range(4):
+            cols = slice(j * block, (j + 1) * block)
+            normed = (moved[rs, cols].astype(F32) - average) * scale * gain_ref[0:1, cols]
+            before = roll_rows(normed, 1) * same
+            for i in range(mixes):
+                weight = mix_ref[i : i + 1, cols]
+                outs[i][rs, cols] = (normed * weight + before * (1.0 - weight)).astype(BF)
+
+
+def mix_rows(x, same, gain, mixes, order=None):
+    rows, width = x.shape
+    count = mixes.shape[0]
+    out = [struct((rows, width), BF)] * count + [struct((rows, 1), F32)] * 2
+    args = [x, same, gain, mixes]
+    if order is not None:
+        out.append(struct((rows, width), BF))
+        args = [order] + args
+    return local_call(
+        functools.partial(mix_kernel, count, order is not None),
+        "mix_rows",
+        out,
+        args,
+        scalars=0 if order is None else 1,
+    )
+
+
+def nt(a, b):
+    return lax.dot_general(a, b, (((1,), (1,)), ((), ())), preferred_element_type=F32)
+
+
+def tn(a, b):
+    return lax.dot_general(a, b, (((0,), (0,)), ((), ())), preferred_element_type=F32)
+
+
+def nn(a, b):
+    return lax.dot_general(a, b, (((1,), (0,)), ((), ())), preferred_element_type=F32)
+
+
+def decay_scales(logs, rows):
+    places = lax.broadcasted_iota(jnp.int32, (rows, 1), 0).astype(F32)
+    middle = float(rows // 2)
+    log_decay = -jnp.exp(logs)
+    return jnp.exp(log_decay * (places - middle)), jnp.exp(log_decay * (middle - 1.0 - places)), places - middle
+
+
+def lane_choice(rows, lanes):
+    return lax.broadcasted_iota(jnp.int32, (rows, lanes), 1) < LANE_WIDTH
+
+
+def head_sums(values, low):
+    first = jnp.sum(jnp.where(low, values, 0.0), axis=1, keepdims=True)
+    second = jnp.sum(jnp.where(low, 0.0, values), axis=1, keepdims=True)
+    return jnp.where(low, first, second)
+
+
+def time_forward_kernel(
+    buckets,
+    in0, in1, in2, in3, own, by_x, by_y, far0, far1, label_c, label_r, logs, bonus, gain,
+    r_ref, k_ref, v_ref, g_ref, n_ref, rstd_ref, mixed_ref,
+):
+    block = own.shape[1]
+    for w, (in_ref, out_ref) in enumerate(zip((in0, in1, in2, in3), (r_ref, k_ref, v_ref, g_ref))):
+        total = nn(in_ref[:, 0:block], own[w])
+        total += nn(in_ref[:, block : 2 * block], by_x[w])
+        total += nn(in_ref[:, 2 * block : 3 * block], by_y[w])
+        total += nn(in_ref[:, 3 * block : 4 * block], far0[w] if w < far0.shape[0] else far1[w - far0.shape[0]])
+        out_ref[...] = total.astype(out_ref.dtype)
+    rows = r_ref.shape[0] // buckets
+    pair = 2 * LANE_WIDTH
+    low = lane_choice(rows, pair)
+    t = lax.broadcasted_iota(jnp.int32, (rows, rows), 0)
+    s = lax.broadcasted_iota(jnp.int32, (rows, rows), 1)
+    for p in range(r_ref.shape[1] // pair):
+        cols = slice(p * pair, (p + 1) * pair)
+        out_scale, in_scale, unused = decay_scales(logs[0:1, cols], rows)
+        for b in range(buckets):
+            rs = slice(b * rows, (b + 1) * rows)
+            allowed = jnp.logical_and(s < t, label_c[rs, :] == label_r[b : b + 1, :])
+            r, k = r_ref[rs, cols].astype(F32), k_ref[rs, cols].astype(F32)
+            v = v_ref[rs, cols]
+            rt, kt = r * out_scale, (k * in_scale).astype(BF)
+            now = r * bonus[0:1, cols] * k
+            parts = []
+            for h in range(2):
+                mine = low if h == 0 else jnp.logical_not(low)
+                scores = nt(jnp.where(mine, rt, 0.0).astype(BF), kt)
+                here = jnp.sum(jnp.where(mine, now, 0.0), axis=1, keepdims=True)
+                scores = jnp.where(allowed, scores, jnp.where(s == t, here, 0.0))
+                parts.append(nn(scores.astype(BF), v))
+            wkv = jnp.where(low, parts[0], parts[1])
+            centered = wkv - head_sums(wkv, low) / LANE_WIDTH
+            scale = lax.rsqrt(head_sums(centered * centered, low) / LANE_WIDTH + GROUP_EPSILON)
+            n = centered * scale
+            n_ref[rs, cols] = n
+            rstd_ref[rs, cols] = scale
+            gate = g_ref[rs, cols]
+            mixed_ref[rs, cols] = (n * gain[0:1, cols] * gate * jax.nn.sigmoid(gate)).astype(BF)
+
+
+def time_backward_kernel(
+    buckets,
+    mg, r_ref, k_ref, v_ref, g_ref, n_ref, rstd_ref, label_c, label_r, logs, bonus, gain,
+    dr_ref, dk_ref, dv_ref, dg_ref, small_ref,
+):
+    rows = r_ref.shape[0] // buckets
+    pair = 2 * LANE_WIDTH
+    low = lane_choice(rows, pair)
+    t = lax.broadcasted_iota(jnp.int32, (rows, rows), 0)
+    s = lax.broadcasted_iota(jnp.int32, (rows, rows), 1)
+    small_ref[...] = jnp.zeros_like(small_ref)
+    for p in range(r_ref.shape[1] // pair):
+        cols = slice(p * pair, (p + 1) * pair)
+        out_scale, in_scale, place = decay_scales(logs[0:1, cols], rows)
+        u, gn = bonus[0:1, cols], gain[0:1, cols]
+        for b in range(buckets):
+            rs = slice(b * rows, (b + 1) * rows)
+            allowed = jnp.logical_and(s < t, label_c[rs, :] == label_r[b : b + 1, :])
+            m, gate, n = mg[rs, cols], g_ref[rs, cols], n_ref[rs, cols]
+            sg = jax.nn.sigmoid(gate)
+            silu = gate * sg
+            dg_ref[rs, cols] = (m * n * gn * sg * (1.0 + gate * (1.0 - sg))).astype(BF)
+            lane_d = jnp.sum(m * n * silu, axis=0, keepdims=True)
+            q = m * gn * silu
+            dout = q - head_sums(q, low) / LANE_WIDTH - n * (head_sums(q * n, low) / LANE_WIDTH)
+            dout = dout * rstd_ref[rs, cols]
+            r, k = r_ref[rs, cols].astype(F32), k_ref[rs, cols].astype(F32)
+            v = v_ref[rs, cols]
+            rt, kt = (r * out_scale).astype(BF), (k * in_scale).astype(BF)
+            now = r * u * k
+            diag = head_sums(dout * v.astype(F32), low)
+            drs, dks, dvs = [], [], []
+            for h in range(2):
+                mine = low if h == 0 else jnp.logical_not(low)
+                dmine = jnp.where(mine, dout, 0.0).astype(BF)
+                scores = nt(jnp.where(mine, rt, jnp.zeros_like(rt)), kt)
+                here = jnp.sum(jnp.where(mine, now, 0.0), axis=1, keepdims=True)
+                scores = jnp.where(allowed, scores, jnp.where(s == t, here, 0.0))
+                dvs.append(tn(scores.astype(BF), dmine))
+                a = jnp.where(allowed, nt(dmine, v), 0.0).astype(BF)
+                drs.append(nn(a, kt))
+                dks.append(tn(a, rt))
+            drt = jnp.where(low, drs[0], drs[1])
+            dkt = jnp.where(low, dks[0], dks[1])
+            dr_ref[rs, cols] = (drt * out_scale + u * k * diag).astype(BF)
+            dk_ref[rs, cols] = (dkt * in_scale + u * r * diag).astype(BF)
+            dv_ref[rs, cols] = jnp.where(low, dvs[0], dvs[1]).astype(BF)
+            lags = place * rt.astype(F32) * drt - (place + 1.0) * kt.astype(F32) * dkt
+            small_ref[0:1, cols] += jnp.sum(lags, axis=0, keepdims=True) * -jnp.exp(logs[0:1, cols])
+            small_ref[1:2, cols] += jnp.sum(r * k * diag, axis=0, keepdims=True)
+            small_ref[2:3, cols] += lane_d
+
+
+def channel_forward_kernel(
+    key_in, recept_in, wk0, wk1, wk2, wk3, wk4, wa0, wa1, wa2, wa3, top, hid_ref, pos_ref, gate_ref, cg_ref
+):
+    start = 0
+    total = None
+    for w in (wk0, wk1, wk2, wk3, wk4):
+        size = w.shape[0]
+        term = nn(key_in[:, start : start + size], w[...])
+        total = term if total is None else total + term
+        start += size
+    positive = jnp.maximum(total, 0.0)
+    hid_ref[...] = (positive * positive).astype(BF)
+    pos_ref[...] = positive.astype(BF)
+    start = 0
+    total = None
+    for w in (wa0, wa1, wa2, wa3):
+        size = w.shape[0]
+        term = nn(recept_in[:, start : start + size], w[...])
+        total = term if total is None else total + term
+        start += size
+    gate = jax.nn.sigmoid(total)
+    gate_ref[...] = gate
+    cg_ref[...] = (top[...] * gate).astype(BF)
+
+
+def carried_kernel(hid, w0, w1, w2, w3, w4, out_ref):
+    start = 0
+    for w in (w0, w1, w2, w3, w4):
+        size = w.shape[0]
+        out_ref[:, start : start + size] = nt(hid[...], w[...]).astype(BF)
+        start += size
+
+
+def pre_grad_kernel(cg, pos, w0, w1, w2, w3, w4, out_ref):
+    start = 0
+    total = None
+    for w in (w0, w1, w2, w3, w4):
+        size = w.shape[0]
+        term = nn(cg[:, start : start + size], w[...])
+        total = term if total is None else total + term
+        start += size
+    out_ref[...] = (total * 2.0 * pos[...].astype(F32)).astype(BF)
+
+
+def back_mix_kernel(count, layout, *refs):
+    x_ref, mean_ref, rstd_ref, same_ref, next_ref, gain_ref, mix_ref = refs[:7]
+    grads = refs[7 : 7 + count]
+    weights = refs[7 + count : -3]
+    out_ref, sens_ref, stat_ref = refs[-3:]
+    rows = x_ref.shape[0]
+    same, following = same_ref[...], next_ref[...]
+    mean, rstd = mean_ref[...], rstd_ref[...]
+    stat_ref[...] = jnp.zeros_like(stat_ref)
+    sens_ref[...] = jnp.zeros_like(sens_ref)
+    ones = jnp.ones((8, 256), BF)
+    for start in range(0, x_ref.shape[1], 256):
+        cols = slice(start, start + 256)
+        hat = (x_ref[:, cols].astype(F32) - mean) * rstd
+        gain = gain_ref[0:1, cols]
+        normed = hat * gain
+        change = normed - roll_rows(normed, 1) * same
+        now = jnp.zeros((rows, 256), F32)
+        later = jnp.zeros((rows, 256), F32)
+        for i in range(count):
+            which, lead, row = layout(i, start)
+            w = weights[which]
+            w = w[row : row + 256, :] if lead is None else w[lead, row : row + 256, :]
+            g = nt(grads[i][...], w)
+            sens_ref[i : i + 1, cols] = jnp.sum(g * change, axis=0, keepdims=True)
+            weight = mix_ref[i : i + 1, cols]
+            now = now + g * weight
+            later = later + g * (1.0 - weight)
+        back = now + following * roll_rows(later, -1)
+        out_ref[:, cols] = back.astype(BF)
+        scaled = back * gain
+        stat_ref[0:8, :] += nt(ones, scaled.astype(BF))
+        stat_ref[8:16, :] += nt(ones, (scaled * hat).astype(BF))
+
+
+def weight_grad_kernel(lhs, rhs, send_x, send_y, keep):
+    places = ((keep, 0), (keep, 2), (send_x, 0), (keep, 3), (keep, 1), (send_y, 0), (send_x, 1), (send_y, 1))
+    piece = lhs.shape[1] // 8
+    for i, (ref, slot) in enumerate(places):
+        ref[slot] = tn(lhs[:, i * piece : (i + 1) * piece], rhs[...]).astype(BF)
+
+
+def weight_grad(lhs, rhs):
+    piece, columns = lhs.shape[1] // 8, rhs.shape[1]
+    return local_call(
+        weight_grad_kernel,
+        "weight_grad",
+        [struct((2, piece, columns), BF), struct((2, piece, columns), BF), struct((4, piece, columns), BF)],
+        [lhs, rhs],
+    )
+
+
+def reduce_relay(send_x, send_y, keep):
+    got_x, got_y = over_x(send_x), over_y(send_y)
+    f = lambda a: a.astype(F32)
+    next_y = over_y((f(keep[1]) + f(got_x[1])).astype(BF))
+    next_x = over_x((f(keep[3]) + f(got_y[1])).astype(BF))
+    upper = f(keep[0]) + f(got_x[0]) + f(next_y)
+    lower = f(keep[2]) + f(got_y[0]) + f(next_x)
+    return upper, lower
+
+
+def fast_body(
+    block_arguments,
+    bundled_spans,
+    opening_normalize_scale,
+    accept_lagmix,
+    lookup_lagmix,
+    payload_lagmix,
+    valve_lagmix,
+    accept_weights,
+    lookup_weights,
+    payload_weights,
+    valve_weights,
+    fading_speed_logs,
+    present_reward,
+    lane_normalize_scale,
+    emission_weights,
+    closing_normalize_scale,
+    feedforward_lookup_lagmix,
+    feedforward_accept_lagmix,
+    feedforward_lookup_weights,
+    feedforward_payload_weights,
+    feedforward_accept_weights,
+    upstream_sensitivity,
+):
+    buckets, bucket_rows, width = block_arguments.shape
+    rows = buckets * bucket_rows
+    parts = lax.axis_size("mp")
+    d, m = lax.axis_index("dp"), lax.axis_index("mp")
+    own_width = width // parts
+    own_heads = own_width // LANE_WIDTH
+    block = width // 4
+    shard = accept_weights.shape[0]
+    order = jnp.stack([flip(jnp.int32(j), d) for j in range(4)]).astype(jnp.int32)
+
+    def features_in_order(vectors):
+        split = vectors.reshape(vectors.shape[0], 4, block)
+        return jnp.concatenate(
+            [lax.dynamic_index_in_dim(split, order[j], axis=1, keepdims=False) for j in range(4)], axis=1
+        )
+
+    def own_columns(values):
+        return lax.dynamic_slice_in_dim(values, m * own_width, own_width, axis=values.ndim - 1)
+
+    def of_own_heads(vectors):
+        split = vectors.reshape(vectors.shape[0], own_heads, parts, LANE_WIDTH)
+        return lax.dynamic_index_in_dim(split, m, axis=2, keepdims=False).reshape(vectors.shape[0], own_width)
+
+    wk1, wk2 = over_x(feedforward_lookup_weights), over_y(feedforward_lookup_weights)
+    half = block // 2
+    wk3, wk4 = over_y(wk1[:half]), over_x(wk2[half:])
+    wk = (feedforward_lookup_weights, wk1, wk2, wk3, wk4)
+
+    stacked = jnp.stack([accept_weights, lookup_weights, payload_weights, valve_weights])
+    by_head = stacked.reshape(4, shard, own_heads, parts, LANE_WIDTH).transpose(3, 0, 1, 2, 4)
+    by_head = by_head.reshape(parts, 4, shard, own_width)
+    by_column = feedforward_accept_weights.reshape(shard, parts, own_width).transpose(1, 0, 2)
+    blocks = jnp.concatenate([by_head, by_column[:, None]], axis=1)
+    got = exchange_mp(blocks, 0)
+    own = got.transpose(1, 0, 2, 3).reshape(5, parts * shard, own_width)
+    by_x, by_y = over_x(own), over_y(own)
+    far0, far1 = over_y(by_x[:2]), over_x(by_y[2:])
+    full_output = lax.all_gather(emission_weights, "dp", axis=0, tiled=True)
+
+    wv_own, by_x_held = lax.optimization_barrier((feedforward_payload_weights, by_x))
+    by_x = by_x_held
+    wv1, wv2 = over_x(wv_own), over_y(wv_own)
+    wv3, wv4 = over_y(wv1[:half]), over_x(wv2[half:])
+    wv = (wv_own, wv1, wv2, wv3, wv4)
+
+    lengths = bundled_spans.reshape(buckets, -1)
+    slots = lengths.shape[1]
+    before_slot = (jnp.arange(slots)[:, None] <= jnp.arange(slots)[None, :]).astype(jnp.int32)
+    ends = jnp.sum(lengths[:, :, None] * before_slot[None], axis=1)
+    places = jnp.arange(bucket_rows, dtype=jnp.int32)
+    label = jnp.sum((places[None, :, None] >= ends[:, None, :]).astype(jnp.int32), axis=2)
+    past = jnp.sum((places[None, :, None] >= ends[:, None, :] + 1).astype(jnp.int32), axis=2)
+    ahead = jnp.sum((places[None, :, None] + 1 >= ends[:, None, :]).astype(jnp.int32), axis=2)
+    same = jnp.logical_and(label == past, places[None] > 0).astype(F32).reshape(rows, 1)
+    following = jnp.logical_and(label == ahead, places[None] < bucket_rows - 1).astype(F32).reshape(rows, 1)
+    valid = (places[None] < ends[:, -1:]).astype(F32).reshape(rows, 1)
+    label_column = label.reshape(rows, 1)
+
+    x_rows = block_arguments.reshape(rows, width)
+    gains = features_in_order(jnp.stack([opening_normalize_scale, closing_normalize_scale]))
+    mixes = features_in_order(
+        jnp.stack(
+            [
+                accept_lagmix,
+                lookup_lagmix,
+                payload_lagmix,
+                valve_lagmix,
+                feedforward_lookup_lagmix,
+                feedforward_accept_lagmix,
+            ]
+        )
+    )
+    head_vectors = of_own_heads(jnp.stack([fading_speed_logs, present_reward, lane_normalize_scale]))
+    logs, bonus, lane_gain = head_vectors[0:1], head_vectors[1:2], head_vectors[2:3]
+    x_own = own_columns(x_rows).astype(F32)
+    top_own = own_columns(upstream_sensitivity.reshape(rows, width)).astype(F32) * valid
+
+    recept_in, key_in, value_in, gate_in, mean1, rstd1, x_moved = mix_rows(
+        x_rows, same, gains[0:1], mixes[0:4], order
+    )
+    wide = struct((rows, own_width), F32)
+    narrow = struct((rows, own_width), BF)
+    recept, key, value, gate_raw, n, n_scale, mixed = local_call(
+        functools.partial(time_forward_kernel, buckets),
+        "time_forward",
+        [narrow, narrow, narrow, wide, wide, wide, narrow],
+        [recept_in, key_in, value_in, gate_in, own, by_x, by_y, far0, far1, label_column, label, logs, bonus, lane_gain],
+    )
+    mixed_out = product(mixed, full_output).astype(BF)
+    middle_own = x_own + scatter_mp(mixed_out, False, 1)
+    middle = gather_mp(middle_own.astype(BF), True, 2)
+    channel_key_in, channel_recept_in, mean2, rstd2 = mix_rows(middle, same, gains[1:2], mixes[4:6])
+    wa = (own[4], by_x[4], by_y[4], far1[2])
+    hidden_width = wv_own.shape[1]
+    hidden, positive, channel_gate, carried_grad_own = local_call(
+        channel_forward_kernel,
+        "channel_forward",
+        [struct((rows, hidden_width), BF)] * 2 + [wide, narrow],
+        [channel_key_in, channel_recept_in, *wk, *wa, top_own],
+    )
+    carried_grad = gather_mp(carried_grad_own, True, 3)
+    ff_value = reduce_relay(*weight_grad(carried_grad, hidden))
+    (carried_part,) = local_call(
+        carried_kernel, "carried", [struct((rows, width), BF)], [hidden, *wv]
+    )
+    (pre_grad,) = local_call(
+        pre_grad_kernel, "pre_grad", [struct((rows, hidden_width), BF)], [carried_grad, positive, *wv]
+    )
+    carried = scatter_mp(carried_part, True, 4)
+    ff_key = reduce_relay(*weight_grad(channel_key_in, pre_grad))
+    outputs_own = ((middle_own + channel_gate * carried) * valid).astype(BF)
+    gate_input_grad = (top_own * carried * channel_gate * (1.0 - channel_gate)).astype(BF)
+
+    def channel_layout(i, start):
+        if i == 0:
+            for which, (first, size) in enumerate(
+                ((0, block), (block, block), (2 * block, block), (3 * block, half), (3 * block + half, half))
+            ):
+                if first <= start < first + size:
+                    return which, None, start - first
+        return 5 + start // block, None, start % block
+
+    back_part, channel_sens, stats = local_call(
+        functools.partial(back_mix_kernel, 2, channel_layout),
+        "channel_back",
+        [struct((rows, width), BF), struct((8, width), F32), struct((16, rows), F32)],
+        [middle, mean2, rstd2, same, following, gains[1:2], mixes[4:6], pre_grad, gate_input_grad, *wk, *wa],
+    )
+    back_own, stats = scatter_mp(back_part, True, 5, stats)
+
+    def norm_back(back, hat, gain, rstd, sums):
+        mean_g = sums[0][:, None] / width
+        mean_gh = sums[8][:, None] / width
+        return (back * gain - mean_g - hat * mean_gh) * rstd
+
+    hat2 = (middle_own.astype(BF).astype(F32) - mean2) * rstd2
+    closing_own = jnp.sum(back_own * hat2, axis=0)
+    middle_grad = top_own + norm_back(
+        back_own, hat2, own_columns(closing_normalize_scale)[None], rstd2, stats
+    )
+    branch_own = middle_grad.astype(BF)
+    branch = gather_mp(branch_own, False, 6)
+    mixed_grad = product_back(branch, full_output)
+    grad_output = lax.psum_scatter(
+        product_rows(mixed, branch).astype(BF), "dp", scatter_dimension=0, tiled=True
+    ).astype(F32)
+    recept_grad, key_grad, value_grad, gate_grad, small = local_call(
+        functools.partial(time_backward_kernel, buckets),
+        "time_backward",
+        [narrow, narrow, narrow, narrow, struct((8, own_width), F32)],
+        [mixed_grad, recept, key, value, gate_raw, n, n_scale, label_column, label, logs, bonus, lane_gain],
+    )
+
+    def time_layout(i, start):
+        which = start // block
+        if which < 3:
+            return which, i, start % block
+        return (3, i, start % block) if i < 2 else (4, i - 2, start % block)
+
+    back_part1, time_sens, stats1 = local_call(
+        functools.partial(back_mix_kernel, 4, time_layout),
+        "time_back",
+        [struct((rows, width), BF), struct((8, width), F32), struct((16, rows), F32)],
+        [
+            x_moved, mean1, rstd1, same, following, gains[0:1], mixes[0:4],
+            recept_grad, key_grad, value_grad, gate_grad,
+            own, by_x, by_y, far0, far1,
+        ],
+    )
+    pieces = [
+        weight_grad(a, b)
+        for a, b in (
+            (recept_in, recept_grad),
+            (key_in, key_grad),
+            (value_in, value_grad),
+            (gate_in, gate_grad),
+            (channel_recept_in, gate_input_grad),
+        )
+    ]
+    send_x, send_y, keep = (jnp.stack([p[i] for p in pieces], axis=1) for i in range(3))
+    upper, lower = reduce_relay(send_x, send_y, keep)
+    back_own1, stats1 = scatter_mp(back_part1, True, 7, stats1)
+    hat1 = (x_own - mean1) * rstd1
+    opening_own = jnp.sum(back_own1 * hat1, axis=0)
+    rows_grad = norm_back(back_own1, hat1, own_columns(opening_normalize_scale)[None], rstd1, stats1)
+    input_own = (middle_grad + rows_grad).astype(BF)
+    outputs = gather_mp(outputs_own, False, 8)
+    input_grads = gather_mp(input_own, False, 9)
+
+    both = jnp.concatenate([upper, lower], axis=1).astype(BF)
+    both = both.reshape(5, parts, shard, own_width).transpose(1, 0, 2, 3)
+    back = exchange_mp(both, 10)
+    heads_back = back[:, :4].reshape(parts, 4, shard, own_heads, LANE_WIDTH).transpose(1, 2, 3, 0, 4)
+    heads_back = heads_back.reshape(4, shard, width).astype(F32)
+    columns_back = back[:, 4].transpose(1, 0, 2).reshape(shard, width).astype(F32)
+
+    def from_order(vectors):
+        return features_in_order(vectors)
+
+    sens = from_order(jnp.concatenate([time_sens[:4], channel_sens[:2]], axis=0))
+    zeros = jnp.zeros((2, width), F32)
+    columns = lax.dynamic_update_slice_in_dim(zeros, jnp.stack([opening_own, closing_own]), m * own_width, axis=1)
+    head_zeros = jnp.zeros((3, own_heads, parts, LANE_WIDTH), F32)
+    head_part = small[:3].reshape(3, own_heads, 1, LANE_WIDTH)
+    heads = lax.dynamic_update_slice_in_dim(head_zeros, head_part, m, axis=2).reshape(3, width)
+    vectors = lax.psum(jnp.concatenate([sens, columns, heads], axis=0), ("dp", "mp"))
+    vectors = lax.dynamic_slice_in_dim(vectors, d * block, block, axis=1)
+    shape = (buckets, bucket_rows, width)
+    return (
+        outputs.reshape(shape),
+        input_grads.reshape(shape),
+        vectors[6],
+        vectors[0],
+        vectors[1],
+        vectors[2],
+        vectors[3],
+        heads_back[0],
+        heads_back[1],
+        heads_back[2],
+        heads_back[3],
+        vectors[8],
+        vectors[9],
+        vectors[10],
+        grad_output,
+        vectors[7],
+        vectors[4],
+        vectors[5],
+        jnp.concatenate(ff_key, axis=0),
+        jnp.concatenate(ff_value, axis=0),
+        columns_back,
+    )
+
+
+def body(*args):
+    data_parts, parts = lax.axis_size("dp"), lax.axis_size("mp")
+    width, shard, hidden = args[0].shape[2], args[7].shape[0], args[18].shape[1]
+    aligned = (
+        data_parts == 4
+        and parts % 2 == 0
+        and shard == LANE_WIDTH
+        and (width // parts) % 256 == 0
+        and hidden % 128 == 0
+    )
+    return fast_body(*args) if aligned else general_body(*args)
 
 
 def solution(mesh):

time: 1270 us -> 623 us (0.49)
  waiting for transfers between devices: 616 us -> 134 us
  Pallas kernels: 0 us -> 307 us
  matrix products: 255 us -> 6.54 us
  local copies, waits for them, and re-layouts: 218 us -> 83 us
  other arithmetic: 133 us -> 45.9 us
  starting transfers between devices: 0.72 us -> 20.4 us
  blocking collectives: 13.1 us -> 0 us
    all_gather x8 -> x1, waiting for transfers between devices: 449 us -> 0.01 us  [fast_body(): full_output = lax.all_gather(emission_weights, 'dp', axis=0, tiled=True)]
    pallas_call x0 -> x27, Pallas kernels: none -> 307 us  [the longest x5 87.6 us: gather_mp(): pl.pallas_call(functools.partial(gather_kernel, chips, shifted), out_shap...]
    reduce_scatter x8 -> x1, waiting for transfers between devices: 89.2 us -> 0.01 us  [fast_body(): lax.psum_scatter(product_rows(mixed, branch).astype(BF), 'dp', scatter_di...]
    dot_general x24 -> x0, matrix products: 85.8 us -> none  [the longest x6 33.4 us: iterative_renewal(): jnp.einsum('cshi,cshj->chij', lookup_blocks * tail_scale * tail_keep[:, :...]
    dot_general x16 -> x1, matrix products: 75.7 us -> 2.4 us  [product_back(): lax.dot_general(first_operand, second_operand, (((1,), (1,)), ((), ())),...]
    dot_general x16 -> x1, matrix products: 68.2 us -> 2.72 us  [product(): jnp.dot(first_operand, second_operand, preferred_element_type=jnp.float32)]
    reshape x21 -> x5, local copies, waits for them, and re-layouts: 59.6 us -> 2.58 us  [the longest x1 1.36 us: fast_body(): by_head = by_head.reshape(parts, 4, shard, own_width)]
    ppermute x0 -> x24, waiting for transfers between devices: none -> 55.1 us  [the longest x12 35.8 us: over_y(): return lax.ppermute(a, 'dp', [(i, i ^ 2) for i in range(4)])]
  transfers between devices with their start and end apart: 18 -> 27, of which waited for: 12 -> 10; matrix products, arithmetic and copies ran while one was open for 27% -> 19% of each run, Pallas kernels for 0% -> 45%
where the time goes in v1:
time: 623 us; the launch traced here: 612 us
  Pallas kernels  307 us (49%)
  waiting for transfers between devices  134 us (22%)
  local copies, waits for them, and re-layouts  83 us (13%)
  other arithmetic  45.9 us (7%)
  starting transfers between devices  20.4 us (3%)
  between operations  14.8 us (2%)
  matrix products  6.54 us (1%)
    pallas_call x5, Pallas kernels, gather_mp(): pl.pallas_call(functools.partial(gather_kernel, chips, shifted), out_shap...  87.6 us
    pallas_call x4, Pallas kernels, scatter_mp(): pl.pallas_call(functools.partial(scatter_kernel, chips, shifted, with_row...  85 us
    psum x1, waiting for transfers between devices, fast_body(): lax.psum(jnp.concatenate([sens, columns, heads], axis=0), ('dp', 'mp'))  79.1 us
    pallas_call x16, Pallas kernels, local_call(): pl.pallas_call(kernel, out_shape=out_shape, in_specs=specs, out_specs=vme...  74.3 us
    pallas_call x2, Pallas kernels, exchange_mp(): pl.pallas_call(functools.partial(exchange_kernel, parts), out_shape=jax.S...  59.9 us
    ppermute x12, waiting for transfers between devices, over_y(): return lax.ppermute(a, 'dp', [(i, i ^ 2) for i in range(4)])  35.8 us
    unnamed x122, local copies, waits for them, and re-layouts  20.4 us
    ppermute x12, waiting for transfers between devices, over_x(): return lax.ppermute(a, 'dp', [(i, i ^ 1) for i in range(4)])  19.2 us
  transfers between devices with their start and end apart: 27, of which 10 were waited for; matrix products, arithmetic and copies ran while one was open for 19% of the time, Pallas kernels for 45%

profile of v1, /device:TPU:1, one launch (start us, length us, event | category | flops | bytes accessed | tf_op | source)
XLA Modules:
  0.0 611.7 jit_solution(9045918505601168569)
XLA Ops:
  18.4 29.7 %exchange_mp.2 = bf16[8,5,64,256]{3,2,1,0:T(8,128)(2,1)} custom-call(bf16[8,5,64,256]{3,2,1,0:T(8,128)(2,1)} %pad_maximum_fusion.2.a_ref), custom_call_target="tpu_custom_call" | custom-call | tf_op jit(solution)/shard_map/exchange_mp/pallas_call | solution.py:646
  91.9 16.6 %collective-permute-done.4.wk1.refs_10_ = bf16[512,896]{1,0:T(8,128)(2,1)S(1)} collective-permute-done((bf16[512,896]{1,0:T(8,128)(2,1)}, bf16[512,896]{1,0:T(8,128)(2,1)S(1)}, u32[]{:S(2)}, u32[]{:S(2)}) %collective-permute-start.4) | collective-permute-done | bytes 917536 | tf_op jit(solution)/shard_map/ppermute | solution.py:436
  118.3 6.2 %mix_rows.2 = (bf16[256,2048]{1,0:T(8,128)(2,1)}, bf16[256,2048]{1,0:T(8,128)(2,1)}, bf16[256,2048]{1,0:T(8,128)(2,1)}, bf16[256,2048]{1,0:T(8,128)(2,1)}, f32[2...) custom-call(s32[4]{0:T(128)} %pad_add_fusion.refs_0_, bf16[256,2048]{1,0:T(8,128)(2,1)} %bitcast.226, ...), custom_call_target="tpu_custom_call" | custom-call | tf_op jit(solution)/shard_map/mix_rows/pallas_call | solution.py:665
  131.9 8.5 %collective-permute-done.2.far0.refs_14_ = bf16[2,512,256]{2,1,0:T(8,128)(2,1)} collective-permute-done((bf16[2,512,256]{2,1,0:T(8,128)(2,1)}, bf16[2,512,256]{2,1,0:T(8,128)(2,1)}, u32[]{:S(2)}, u32[]{:S(2)}) %collective-permute-start.2) | collective-permute-done | bytes 524320 | tf_op jit(solution)/shard_map/ppermute | solution.py:440
  140.6 7.2 %time_forward.1 = (bf16[256,256]{1,0:T(8,128)(2,1)}, bf16[256,256]{1,0:T(8,128)(2,1)}, bf16[256,256]{1,0:T(8,128)(2,1)}, f32[256,256]{1,0:T(8,128)}, f32[256,256...) custom-call(bf16[256,2048]{1,0:T(8,128)(2,1)} %get-tuple-element.81.in0.lhs, ...), custom_call_target="tpu_custom_call" | custom-call | tf_op jit(solution)/shard_map/time_forward/pallas_call | solution.py:665
  150.6 22.9 %scatter_mp.4 = f32[256,256]{1,0:T(8,128)} custom-call(bf16[256,2048]{1,0:T(8,128)(2,1)} %convolution_convert_fusion.1.refs_0_), custom_call_target="tpu_custom_call" | custom-call | tf_op jit(solution)/shard_map/scatter_mp/pallas_call | solution.py:612
  180.2 18.5 %gather_mp.5.refs_0_ = bf16[256,2048]{1,0:T(8,128)(2,1)} custom-call(bf16[256,256]{1,0:T(8,128)(2,1)} %fusion.17.a_ref), custom_call_target="tpu_custom_call" | custom-call | tf_op jit(solution)/shard_map/gather_mp/pallas_call | solution.py:501
  205.8 5.6 channel_forward.1
  211.4 17.7 %gather_mp.7.cg.lhs = bf16[256,2048]{1,0:T(8,128)(2,1)} custom-call(bf16[256,256]{1,0:T(8,128)(2,1)} %get-tuple-element.94.a_ref), custom_call_target="tpu_custom_call" | custom-call | tf_op jit(solution)/shard_map/gather_mp/pallas_call | solution.py:501
  240.1 18.6 %scatter_mp.5 = f32[256,256]{1,0:T(8,128)} custom-call(bf16[256,2048]{1,0:T(8,128)(2,1)} %carried.1.refs_0_), custom_call_target="tpu_custom_call" | custom-call | tf_op jit(solution)/shard_map/scatter_mp/pallas_call | solution.py:612
  263.2 4.5 pre_grad.1.refs_7_.rhs
  272.0 7.2 %channel_back.1 = (bf16[256,2048]{1,0:T(8,128)(2,1)}, f32[8,2048]{1,0:T(8,128)}, f32[16,256]{1,0:T(8,128)}) custom-call(bf16[256,2048]{1,0:T(8,128)(2,1)} %gather_mp.5.refs_0_, f32[256,1]{1,0:T(8,128)} %get-tuple-element.92.refs_1_, f32[256,1]{1,0:T(8,128)} %get-tuple-element.93.refs_2_, f32[256,1]{1,0:T(8,128)} %get-tuple-element.198.refs_2_.refs_1_.refs_3_, ...), custom_call_target="tpu_custom_call" | custom-call | tf_op jit(solution)/shard_map/channel_back/pallas_call | solution.py:665
  279.2 22.2 %scatter_mp.6 = (f32[256,256]{1,0:T(8,128)}, f32[16,256]{1,0:T(8,128)}) custom-call(bf16[256,2048]{1,0:T(8,128)(2,1)} %get-tuple-element.96.refs_0_, f32[16,256]{1,0:T(8,128)} %get-tuple-element.97.refs_1_), custom_call_target="tpu_custom_call" | custom-call | tf_op jit(solution)/shard_map/scatter_mp/pallas_call | solution.py:612
  304.1 16.6 %gather_mp.8 = bf16[256,2048]{1,0:T(8,128)(2,1)} custom-call(bf16[256,256]{1,0:T(8,128)(2,1)} %get-tuple-element.146.a_ref), custom_call_target="tpu_custom_call" | custom-call | tf_op jit(solution)/shard_map/gather_mp/pallas_call | solution.py:501
  323.1 4.6 time_backward.1
  338.5 8.0 %time_back.1 = (bf16[256,2048]{1,0:T(8,128)(2,1)}, f32[8,2048]{1,0:T(8,128)}, f32[16,256]{1,0:T(8,128)}) custom-call(bf16[256,2048]{1,0:T(8,128)(2,1)} %get-tuple-element.100.refs_0_, f32[256,1]{1,0:T(8,128)} %get-tuple-element.101.refs_1_, f32[256,1]{1,0:T(8,128)} %get-tuple-element.102.refs_2_, f32[256,1]{1,0:T(8,128)} %get-tuple-element.198.refs_2_.refs_1_.refs_3_, ...), custom_call_target="tpu_custom_call" | custom-call | tf_op jit(solution)/shard_map/time_back/pallas_call | solution.py:665
  346.5 21.3 %scatter_mp.7 = (f32[256,256]{1,0:T(8,128)}, f32[16,256]{1,0:T(8,128)}) custom-call(bf16[256,2048]{1,0:T(8,128)(2,1)} %get-tuple-element.113.refs_0_, f32[16,256]{1,0:T(8,128)} %get-tuple-element.114.refs_1_), custom_call_target="tpu_custom_call" | custom-call | tf_op jit(solution)/shard_map/scatter_mp/pallas_call | solution.py:612
  387.1 17.6 %gather_mp.6 = bf16[256,2048]{1,0:T(8,128)(2,1)} custom-call(bf16[256,256]{1,0:T(8,128)(2,1)} %get-tuple-element.164.a_ref), custom_call_target="tpu_custom_call" | custom-call | tf_op jit(solution)/shard_map/gather_mp/pallas_call | solution.py:501
  404.7 17.3 %gather_mp.9 = bf16[256,2048]{1,0:T(8,128)(2,1)} custom-call(bf16[256,256]{1,0:T(8,128)(2,1)} %get-tuple-element.163.a_ref), custom_call_target="tpu_custom_call" | custom-call | tf_op jit(solution)/shard_map/gather_mp/pallas_call | solution.py:501
  423.1 79.1 %all-reduce.2.cloned.1.call-done = f32[11,2048]{1,0:T(8,128)} async-done(((f32[11,2048]{1,0:T(8,128)}), f32[11,2048]{1,0:T(8,128)}) %all-reduce.2.cloned.1.call-update) | async-done | bytes 90128 | tf_op jit(solution)/shard_map/psum | solution.py:1201
  513.9 4.6 collective-permute-done.21
  522.9 8.8 %collective-permute-done.17 = bf16[256,896]{1,0:T(8,128)(2,1)S(1)} collective-permute-done((bf16[256,896]{1,0:T(8,128)(2,1)S(1)}, bf16[256,896]{1,0:T(8,128)(2,1)S(1)}, u32[]{:S(2)}, u32[]{:S(2)}) %collective-permute-start.17) | collective-permute-done | bytes 458784 | tf_op jit(solution)/shard_map/ppermute | solution.py:440
  535.5 13.1 %collective-permute-done.13 = bf16[5,256,256]{2,1,0:T(8,128)(2,1)S(1)} collective-permute-done((bf16[5,256,256]{2,1,0:T(8,128)(2,1)S(1)}, bf16[5,256,256]{2,1,0:T(8,128)(2,1)S(1)}, u32[]{:S(2)}, u32[]{:S(2)}) %collective-permute-start.13) | collective-permute-done | bytes 655392 | tf_op jit(solution)/shard_map/ppermute | solution.py:440
  552.7 30.1 %exchange_mp.3 = bf16[8,5,64,256]{3,2,1,0:T(8,128)(2,1)} custom-call(bf16[8,5,64,256]{3,2,1,0:T(8,128)(2,1)} %bitcast.221), custom_call_target="tpu_custom_call" | custom-call | tf_op jit(solution)/shard_map/exchange_mp/pallas_call | solution.py:646
  (295 shorter events, 190.3 us)
Async XLA Ops:
  7.2 140.7 %all-gather.2.cloned.1.call-start = ((), (), s32[]{:S(2)}) async-start(), calls=%async_computation.1 | async-start | bytes 1310720 | tf_op jit(solution)/shard_map/all_gather | solution.py:1033
  49.6 36.9 %collective-permute-start = (bf16[5,512,256]{2,1,0:T(8,128)(2,1)S(1)}, bf16[5,512,256]{2,1,0:T(8,128)(2,1)}, u32[]{:S(2)}, u32[]{:S(2)}) collective-permute-start(bf16[5,512,256]{2,1,0:T(8,128)(2,1)S(1)} %bitcast.214), channel_id=1, source_target_pairs={{0,8},{8,0},{16,24},{24,16},{1,9},{9,1},{17,25},{25,17},{2,10},{10... | collective-permute-start | bytes 3932168 | tf_op jit(solution)/shard_map/ppermute | solution.py:436
  50.9 34.2 %collective-permute-start.1 = (bf16[5,512,256]{2,1,0:T(8,128)(2,1)S(1)}, bf16[5,512,256]{2,1,0:T(8,128)(2,1)S(1)}, u32[]{:S(2)}, u32[]{:S(2)}) collective-permute-start(bf16[5,512,256]{2,1,0:T(8,128)(2,1)S(1)} %bitcast.215), channel_id=1, source_target_pairs={{0,16},{8,24},{16,0},{24,8},{1,17},{9,25},{17,1},{25,9},{2,18},{10... | collective-permute-start | bytes 3932168 | tf_op jit(solution)/shard_map/ppermute | solution.py:440
  52.1 56.3 %collective-permute-start.4 = (bf16[512,896]{1,0:T(8,128)(2,1)}, bf16[512,896]{1,0:T(8,128)(2,1)S(1)}, u32[]{:S(2)}, u32[]{:S(2)}) collective-permute-start(bf16[512,896]{1,0:T(8,128)(2,1)} %refs_9_.1), channel_id=1, source_target_pairs={{0,8},{8,0},{16,24},{24,16},{1,9},{9,1},{17,25},{25,17},{2,10},{10... | collective-permute-start | bytes 2752520 | tf_op jit(solution)/shard_map/ppermute | solution.py:436
  52.4 75.0 %collective-permute-start.5 = (bf16[512,896]{1,0:T(8,128)(2,1)}, bf16[512,896]{1,0:T(8,128)(2,1)}, u32[]{:S(2)}, u32[]{:S(2)}) collective-permute-start(bf16[512,896]{1,0:T(8,128)(2,1)} %refs_9_.1), channel_id=1, source_target_pairs={{0,16},{8,24},{16,0},{24,8},{1,17},{9,25},{17,1},{25,9},{2,18},{10... | collective-permute-start | bytes 2752520 | tf_op jit(solution)/shard_map/ppermute | solution.py:440
  52.6 449.6 %all-reduce.2.cloned.1.call-start = ((), (), s32[]{:S(2)}) async-start(), calls=%async_computation.2 | async-start | bytes 262144 | tf_op jit(solution)/shard_map/psum | solution.py:1201
  86.1 54.5 %collective-permute-start.3 = (bf16[3,512,256]{2,1,0:T(8,128)(2,1)}, bf16[3,512,256]{2,1,0:T(8,128)(2,1)}, u32[]{:S(2)}, u32[]{:S(2)}) collective-permute-start(bf16[3,512,256]{2,1,0:T(8,128)(2,1)} %slice.288), channel_id=1, source_target_pairs={{0,8},{8,0},{16,24},{24,16},{1,9},{9,1},{17,25},{25,17},{2,10},{10... | collective-permute-start | bytes 2359304 | tf_op jit(solution)/shard_map/ppermute | solution.py:436
  86.5 87.0 %collective-permute-start.8 = (bf16[512,896]{1,0:T(8,128)(2,1)}, bf16[512,896]{1,0:T(8,128)(2,1)S(1)}, u32[]{:S(2)}, u32[]{:S(2)}) collective-permute-start(bf16[512,896]{1,0:T(8,128)(2,1)} %w0.1), channel_id=1, source_target_pairs={{0,8},{8,0},{16,24},{24,16},{1,9},{9,1},{17,25},{25,17},{2,10},{10... | collective-permute-start | bytes 2752520 | tf_op jit(solution)/shard_map/ppermute | solution.py:436
  87.7 87.9 %collective-permute-start.9 = (bf16[512,896]{1,0:T(8,128)(2,1)}, bf16[512,896]{1,0:T(8,128)(2,1)}, u32[]{:S(2)}, u32[]{:S(2)}) collective-permute-start(bf16[512,896]{1,0:T(8,128)(2,1)} %w0.1), channel_id=1, source_target_pairs={{0,16},{8,24},{16,0},{24,8},{1,17},{9,25},{17,1},{25,9},{2,18},{10... | collective-permute-start | bytes 2752520 | tf_op jit(solution)/shard_map/ppermute | solution.py:440
  108.5 31.9 %collective-permute-start.2 = (bf16[2,512,256]{2,1,0:T(8,128)(2,1)}, bf16[2,512,256]{2,1,0:T(8,128)(2,1)}, u32[]{:S(2)}, u32[]{:S(2)}) collective-permute-start(bf16[2,512,256]{2,1,0:T(8,128)(2,1)} %slice.287), channel_id=1, source_target_pairs={{0,16},{8,24},{16,0},{24,8},{1,17},{9,25},{17,1},{25,9},{2,18},{10... | collective-permute-start | bytes 1572872 | tf_op jit(solution)/shard_map/ppermute | solution.py:440
  127.4 77.4 %collective-permute-start.6 = (bf16[256,896]{1,0:T(8,128)(2,1)}, bf16[256,896]{1,0:T(8,128)(2,1)S(1)}, u32[]{:S(2)}, u32[]{:S(2)}) collective-permute-start(bf16[256,896]{1,0:T(8,128)(2,1)} %slice.293), channel_id=1, source_target_pairs={{0,16},{8,24},{16,0},{24,8},{1,17},{9,25},{17,1},{25,9},{2,18},{10... | collective-permute-start | bytes 1376264 | tf_op jit(solution)/shard_map/ppermute | solution.py:440
  140.4 64.5 %collective-permute-start.7 = (bf16[256,896]{1,0:T(8,128)(2,1)}, bf16[256,896]{1,0:T(8,128)(2,1)S(1)}, u32[]{:S(2)}, u32[]{:S(2)}) collective-permute-start(bf16[256,896]{1,0:T(8,128)(2,1)} %slice.294), channel_id=1, source_target_pairs={{0,8},{8,0},{16,24},{24,16},{1,9},{9,1},{17,25},{25,17},{2,10},{10... | collective-permute-start | bytes 1376264 | tf_op jit(solution)/shard_map/ppermute | solution.py:436
  174.3 59.7 %collective-permute-start.10 = (bf16[256,896]{1,0:T(8,128)(2,1)}, bf16[256,896]{1,0:T(8,128)(2,1)S(1)}, u32[]{:S(2)}, u32[]{:S(2)}) collective-permute-start(bf16[256,896]{1,0:T(8,128)(2,1)} %slice.298), channel_id=1, source_target_pairs={{0,16},{8,24},{16,0},{24,8},{1,17},{9,25},{17,1},{25,9},{2,18},{10... | collective-permute-start | bytes 1376264 | tf_op jit(solution)/shard_map/ppermute | solution.py:440
  177.4 56.7 %collective-permute-start.11 = (bf16[256,896]{1,0:T(8,128)(2,1)}, bf16[256,896]{1,0:T(8,128)(2,1)S(1)}, u32[]{:S(2)}, u32[]{:S(2)}) collective-permute-start(bf16[256,896]{1,0:T(8,128)(2,1)} %slice.299), channel_id=1, source_target_pairs={{0,8},{8,0},{16,24},{24,16},{1,9},{9,1},{17,25},{25,17},{2,10},{10... | collective-permute-start | bytes 1376264 | tf_op jit(solution)/shard_map/ppermute | solution.py:436
  233.6 153.2 %collective-permute-start.20 = (bf16[2,256,896]{2,1,0:T(8,128)(2,1)}, bf16[2,256,896]{2,1,0:T(8,128)(2,1)S(1)}, u32[]{:S(2)}, u32[]{:S(2)}) collective-permute-start(bf16[2,256,896]{2,1,0:T(8,128)(2,1)} %get-tuple-element.139), channel_id=1, source_target_pairs={{0,8},{8,0},{16,24},{24,16},{1,9},{9,1},{17,25},{25,17},{2,10},{10... | collective-permute-start | bytes 2752520 | tf_op jit(solution)/shard_map/ppermute | solution.py:436
  233.9 270.1 %collective-permute-start.22 = (bf16[2,256,896]{2,1,0:T(8,128)(2,1)}, bf16[2,256,896]{2,1,0:T(8,128)(2,1)}, u32[]{:S(2)}, u32[]{:S(2)}) collective-permute-start(bf16[2,256,896]{2,1,0:T(8,128)(2,1)} %get-tuple-element.140), channel_id=1, source_target_pairs={{0,16},{8,24},{16,0},{24,8},{1,17},{9,25},{17,1},{25,9},{2,18},{10... | collective-permute-start | bytes 2752520 | tf_op jit(solution)/shard_map/ppermute | solution.py:440
  373.3 227.8 %reduce-scatter.2.cloned.1.call-start = ((), (), s32[]{:S(2)}) async-start(), calls=%async_computation.3 | async-start | bytes 1310720 | tf_op jit(solution)/shard_map/reduce_scatter | solution.py:1139
  377.0 132.8 %collective-permute-start.12 = (bf16[2,5,256,256]{3,2,1,0:T(8,128)(2,1)}, bf16[2,5,256,256]{3,2,1,0:T(8,128)(2,1)}, u32[]{:S(2)}, u32[]{:S(2)}) collective-permute-start(bf16[2,5,256,256]{3,2,1,0:T(8,128)(2,1)} %bitcast_dynamic-update-slice_fusion.10), channel_id=1, source_target_pairs={{0,8},{8,0},{16,24},{24,16},{1,9},{9,1},{17,25},{25,17},{2,10},{10... | collective-permute-start | bytes 3932168 | tf_op jit(solution)/shard_map/ppermute | solution.py:436
  378.3 128.6 %collective-permute-start.16 = (bf16[2,256,896]{2,1,0:T(8,128)(2,1)}, bf16[2,256,896]{2,1,0:T(8,128)(2,1)}, u32[]{:S(2)}, u32[]{:S(2)}) collective-permute-start(bf16[2,256,896]{2,1,0:T(8,128)(2,1)} %get-tuple-element.136), channel_id=1, source_target_pairs={{0,8},{8,0},{16,24},{24,16},{1,9},{9,1},{17,25},{25,17},{2,10},{10... | collective-permute-start | bytes 2752520 | tf_op jit(solution)/shard_map/ppermute | solution.py:436
  378.7 128.6 %collective-permute-start.18 = (bf16[2,256,896]{2,1,0:T(8,128)(2,1)}, bf16[2,256,896]{2,1,0:T(8,128)(2,1)}, u32[]{:S(2)}, u32[]{:S(2)}) collective-permute-start(bf16[2,256,896]{2,1,0:T(8,128)(2,1)} %get-tuple-element.137), channel_id=1, source_target_pairs={{0,16},{8,24},{16,0},{24,8},{1,17},{9,25},{17,1},{25,9},{2,18},{10... | collective-permute-start | bytes 2752520 | tf_op jit(solution)/shard_map/ppermute | solution.py:440
  386.8 124.6 %collective-permute-start.14 = (bf16[2,5,256,256]{3,2,1,0:T(8,128)(2,1)}, bf16[2,5,256,256]{3,2,1,0:T(8,128)(2,1)}, u32[]{:S(2)}, u32[]{:S(2)}) collective-permute-start(bf16[2,5,256,256]{3,2,1,0:T(8,128)(2,1)} %bitcast_dynamic-update-slice_fusion.5), channel_id=1, source_target_pairs={{0,16},{8,24},{16,0},{24,8},{1,17},{9,25},{17,1},{25,9},{2,18},{10... | collective-permute-start | bytes 3932168 | tf_op jit(solution)/shard_map/ppermute | solution.py:440
  508.6 23.2 %collective-permute-start.17 = (bf16[256,896]{1,0:T(8,128)(2,1)S(1)}, bf16[256,896]{1,0:T(8,128)(2,1)S(1)}, u32[]{:S(2)}, u32[]{:S(2)}) collective-permute-start(bf16[256,896]{1,0:T(8,128)(2,1)S(1)} %get-tuple-element.160), channel_id=1, source_target_pairs={{0,16},{8,24},{16,0},{24,8},{1,17},{9,25},{17,1},{25,9},{2,18},{10... | collective-permute-start | bytes 1376264 | tf_op jit(solution)/shard_map/ppermute | solution.py:440
  511.4 37.3 %collective-permute-start.13 = (bf16[5,256,256]{2,1,0:T(8,128)(2,1)S(1)}, bf16[5,256,256]{2,1,0:T(8,128)(2,1)S(1)}, u32[]{:S(2)}, u32[]{:S(2)}) collective-permute-start(bf16[5,256,256]{2,1,0:T(8,128)(2,1)S(1)} %fusion.3), channel_id=1, source_target_pairs={{0,16},{8,24},{16,0},{24,8},{1,17},{9,25},{17,1},{25,9},{2,18},{10... | collective-permute-start | bytes 1966088 | tf_op jit(solution)/shard_map/ppermute | solution.py:440
  518.5 31.1 %collective-permute-start.15 = (bf16[5,256,256]{2,1,0:T(8,128)(2,1)S(1)}, bf16[5,256,256]{2,1,0:T(8,128)(2,1)S(1)}, u32[]{:S(2)}, u32[]{:S(2)}) collective-permute-start(bf16[5,256,256]{2,1,0:T(8,128)(2,1)S(1)} %fusion.4), channel_id=1, source_target_pairs={{0,8},{8,0},{16,24},{24,16},{1,9},{9,1},{17,25},{25,17},{2,10},{10... | collective-permute-start | bytes 1966088 | tf_op jit(solution)/shard_map/ppermute | solution.py:436
  (52 other events, 475.2 us)
Sparse Core Ops, SparseCore 0:
  52.8 42.0 all-gather.1
  373.4 128.7 all-reduce.1
  505.7 35.0 reduce-scatter.1

commit v2 on v0

--- a/solution.py
+++ b/solution.py
@@ -1,8 +1,11 @@
+import functools
 from functools import reduce
 
 import jax
 import jax.numpy as jnp
 from jax import lax
+from jax.experimental import pallas as pl
+from jax.experimental.pallas import tpu as pltpu
 from jax.sharding import PartitionSpec as P
 
 LANE_WIDTH = 64
@@ -131,7 +134,7 @@
     return jax.tree.map(jnp.add, first_terms, second_terms)
 
 
-def body(
+def general_body(
     block_arguments,
     bundled_spans,
     opening_normalize_scale,
@@ -407,6 +410,891 @@
     )
 
 
+MESH = pl.DeviceIdType.MESH
+BF = jnp.bfloat16
+F32 = jnp.float32
+VMEM_LIMIT = 63 << 20
+OPENING, CLOSING, FADING, REWARD, LANE = 0, 5, 8, 9, 10
+
+
+def struct(shape, dtype):
+    return jax.ShapeDtypeStruct(shape, dtype)
+
+
+def flip(place, other):
+    low = lax.rem(lax.rem(place, 2) + lax.rem(other, 2), 2)
+    high = lax.rem(lax.div(place, 2) + lax.div(other, 2), 2)
+    return 2 * high + low
+
+
+def nt(a, b):
+    return lax.dot_general(a, b, (((1,), (1,)), ((), ())), preferred_element_type=F32)
+
+
+def tn(a, b):
+    return lax.dot_general(a, b, (((0,), (0,)), ((), ())), preferred_element_type=F32)
+
+
+def nn(a, b):
+    return lax.dot_general(a, b, (((1,), (0,)), ((), ())), preferred_element_type=F32)
+
+
+def roll_rows(values, shift):
+    return pltpu.roll(values, shift % values.shape[0], 0)
+
+
+def swap_halves(tile):
+    return pltpu.roll(tile, LANE_WIDTH, 1)
+
+
+def head_sums(values, low):
+    first = jnp.sum(jnp.where(low, values, 0.0), axis=1, keepdims=True)
+    second = jnp.sum(jnp.where(low, 0.0, values), axis=1, keepdims=True)
+    return jnp.where(low, first, second)
+
+
+class Links:
+    def __init__(self, send, recv):
+        self.send, self.recv = send, recv
+        self.used = 0
+        self.open = []
+
+    def push(self, source, target, peer):
+        i = self.used
+        self.used += 1
+        copy = pltpu.make_async_remote_copy(
+            source, target, self.send.at[i], self.recv.at[i], device_id=peer, device_id_type=MESH
+        )
+        copy.start()
+        self.open.append(copy)
+        return copy
+
+    def group(self, sources, targets, peers, whole):
+        i = self.used
+        self.used += 1
+        for source, target, peer in zip(sources, targets, peers):
+            pltpu.make_async_remote_copy(
+                source, target, self.send.at[i], self.recv.at[i], device_id=peer, device_id_type=MESH
+            ).start()
+        copy = pltpu.make_async_remote_copy(
+            whole, whole, self.send.at[i], self.recv.at[i], device_id=peers[0], device_id_type=MESH
+        )
+        self.open.append(copy)
+        return copy
+
+    def sent(self, copy):
+        if any(other is copy for other in self.open):
+            copy.wait_send()
+            self.open = [other for other in self.open if other is not copy]
+
+    def finish(self):
+        for copy in self.open:
+            copy.wait_send()
+
+
+COPIES = 300
+
+
+def block_kernel(
+    spans, x_ref, up_ref, vec, w_recept, w_key, w_value, w_gate, w_out, w_channel, fk, fv,
+    out_full, gin_full, ffk_out, ffv_out, back_out, wo_out, vec_out,
+    blocks, g, fkb, fvb, wob, acts, mean1, rstd1, mean2, rstd2, order_vec, head_vec, seen,
+    rkv, gate_raw, n_ref, n_scale, mixed, part, half, pair, far, small,
+    mid_own, mid_own_b, mid, kin, cri, hid, pos, pre, channel_gate, cg_own, cg,
+    out_own, gig, middle_grad, branch_own, branch, mixed_grad, time_grads, sens, head_small,
+    ff_send, ff_got, ff_got2, tm_send, tm_got, tm_got2, channel_sum,
+    wo_part, wo_got, gin_own, u_got, u2_own, u2_got, u3_own, u3_got,
+    send, recv, local,
+):
+    d, m = lax.axis_index("dp"), lax.axis_index("mp")
+    z, c = lax.div(m, 2), lax.rem(m, 2)
+    chips, parts = 4, 8
+    buckets, rows = 2, x_ref.shape[0] // 2
+    width = x_ref.shape[1]
+    own = width // parts
+    block = width // 4
+    shard = w_out.shape[0]
+    pairs = own // 128
+    links = Links(send, recv)
+    mate = (d, 2 * z + 1 - c)
+    chips_away = [lax.rem(z + i, chips) for i in range(1, chips)]
+    others = [lax.rem(m + i, parts) for i in range(1, parts)]
+    x_peer = (d + 1 - 2 * lax.rem(d, 2), m)
+    y_peer = (d + 2 - 4 * lax.div(d, 2), m)
+    diagonal = (3 - d, m)
+    order = [d, x_peer[0], y_peer[0], diagonal[0]]
+
+    def own_lanes(owner):
+        return pl.ds(pl.multiple_of(owner * own, own), own)
+
+    def moved_lanes(owner):
+        place = 2 * flip(lax.div(owner, 2), d) + lax.rem(owner, 2)
+        return pl.ds(pl.multiple_of(place * own, own), own)
+
+    def bucket_rows(b):
+        return slice(b * rows, (b + 1) * rows)
+
+    barrier = pltpu.get_barrier_semaphore()
+    greeted = [(d, other) for other in others] + [x_peer, y_peer, diagonal]
+    for peer in greeted:
+        pl.semaphore_signal(barrier, inc=1, device_id=peer, device_id_type=MESH)
+    top_copy = pltpu.make_async_copy(up_ref.at[:, own_lanes(m)], seen, local)
+    top_copy.start()
+    low16 = lax.broadcasted_iota(jnp.int32, (shard, 128), 1) < LANE_WIDTH
+
+    def head_blocks(w, weight):
+        for to in range(parts):
+            for q in range(pairs):
+                tiles = []
+                for j in (2 * q, 2 * q + 1):
+                    start = j * block + (to // 2) * 128
+                    tiles.append(weight[:, start : start + 128].astype(F32))
+                if to % 2 == 0:
+                    tile = jnp.where(low16, tiles[0], swap_halves(tiles[1]))
+                else:
+                    tile = jnp.where(low16, swap_halves(tiles[0]), tiles[1])
+                blocks[w, to, :, q * 128 : (q + 1) * 128] = tile.astype(BF)
+
+    head_blocks(0, w_recept)
+    pl.semaphore_wait(barrier, len(greeted))
+
+    my_rows = pl.ds(pl.multiple_of(m * shard, shard), shard)
+
+    def exchange(w):
+        if w < 4:
+            sources = [blocks.at[w, other] for other in others]
+        else:
+            sources = [w_channel.at[:, own_lanes(other)] for other in others]
+        return links.group(
+            sources,
+            [g.at[0, w, my_rows]] * (parts - 1),
+            [(d, other) for other in others],
+            g.at[0, w, pl.ds(0, (parts - 1) * shard)],
+        )
+
+    arrivals = [exchange(0)]
+    for w, weight in ((1, w_key), (2, w_value), (3, w_gate)):
+        head_blocks(w, weight)
+        arrivals.append(exchange(w))
+    arrivals.append(exchange(4))
+    for w in range(4):
+        g[0, w, my_rows] = blocks[w, m]
+    g[0, 4, my_rows] = w_channel[:, own_lanes(m)]
+    out_rows = pl.ds(pl.multiple_of(d * shard, shard), shard)
+    wo_arrivals = [links.push(w_out, wob.at[out_rows], peer) for peer in (x_peer, y_peer, diagonal)]
+    wob[out_rows] = w_out[...]
+
+    for j in range(4):
+        order_vec[:, j * block : (j + 1) * block] = vec[
+            :, pl.ds(pl.multiple_of(order[j] * block, block), block)
+        ]
+    low_row = lax.broadcasted_iota(jnp.int32, (16, 128), 1) < LANE_WIDTH
+    upper = lax.rem(m, 2) == 1
+
+    def head_tile(j):
+        start = pl.multiple_of(j * block + lax.div(m, 2) * 128, 128)
+        return vec[:, pl.ds(start, 128)]
+
+    for q in range(pairs):
+        first, second = head_tile(2 * q), head_tile(2 * q + 1)
+        first = jnp.where(upper, swap_halves(first), first)
+        second = jnp.where(upper, second, swap_halves(second))
+        head_vec[:, q * 128 : (q + 1) * 128] = jnp.where(low_row, first, second)
+
+    def row_masks(b):
+        t = lax.broadcasted_iota(jnp.int32, (rows, 1), 0)
+        lane = lax.broadcasted_iota(jnp.int32, (1, rows), 1)
+        label, past, ahead = (jnp.zeros((rows, 1), jnp.int32) for unused in range(3))
+        label_row = jnp.zeros((1, rows), jnp.int32)
+        end = jnp.int32(0)
+        for j in range(spans.shape[1]):
+            end = end + spans[b, j]
+            label = label + jnp.where(t >= end, 1, 0)
+            past = past + jnp.where(t - 1 >= end, 1, 0)
+            ahead = ahead + jnp.where(t + 1 >= end, 1, 0)
+            label_row = label_row + jnp.where(lane >= end, 1, 0)
+        same = jnp.where(jnp.logical_and(label == past, t > 0), 1.0, 0.0)
+        following = jnp.where(jnp.logical_and(label == ahead, t < rows - 1), 1.0, 0.0)
+        valid = jnp.where(t < end, 1.0, 0.0)
+        return label, label_row, same, following, valid
+
+    masks = [row_masks(b) for b in range(buckets)]
+
+    def mix(b, take, mean, rstd, gain_row, mix_row, outs):
+        rs = bucket_rows(b)
+        same = masks[b][2]
+        total = jnp.zeros((rows, 1), F32)
+        for j in range(4):
+            total = total + jnp.sum(take(rs, j).astype(F32), axis=1, keepdims=True)
+        average = total / width
+        spread = jnp.zeros((rows, 1), F32)
+        for j in range(4):
+            centered = take(rs, j).astype(F32) - average
+            spread = spread + jnp.sum(centered * centered, axis=1, keepdims=True)
+        scale = lax.rsqrt(spread / width + EPSILON)
+        mean[rs, :] = average
+        rstd[rs, :] = scale
+        for j in range(4):
+            cols = slice(j * block, (j + 1) * block)
+            normed = (take(rs, j).astype(F32) - average) * scale * order_vec[gain_row : gain_row + 1, cols]
+            before = roll_rows(normed, 1) * same
+            for i, out in enumerate(outs):
+                weight = order_vec[mix_row + i : mix_row + i + 1, cols]
+                out[rs, cols] = (normed * weight + before * (1.0 - weight)).astype(BF)
+
+    def take_x(rs, j):
+        return x_ref[rs, pl.ds(pl.multiple_of(order[j] * block, block), block)]
+
+    def take_mid(rs, j):
+        return mid[rs, j * block : (j + 1) * block]
+
+    def relay_out(source, slot1, slot2):
+        return links.push(source, slot1, x_peer), links.push(source, slot2, y_peer)
+
+    for b in range(buckets):
+        mix(b, take_x, mean1, rstd1, OPENING, OPENING + 1, [acts.at[w] for w in range(4)])
+
+    half_block = block // 2
+    g_first = []
+    for w in range(5):
+        arrivals[w].wait_recv()
+        g_first.append(relay_out(g.at[0, w], g.at[1, w], g.at[2, w]))
+
+    def forward(copies, slot1, slot2, slot3):
+        upper_half, lower_half = pl.ds(0, half_block), pl.ds(half_block, half_block)
+        copies[0].wait_recv()
+        one = links.push(slot1.at[upper_half], slot3.at[upper_half], y_peer)
+        copies[1].wait_recv()
+        return one, links.push(slot2.at[lower_half], slot3.at[lower_half], x_peer)
+
+    fk_first = relay_out(fk, fkb.at[0], fkb.at[1])
+    g_second = [forward(g_first[w], g.at[1, w], g.at[2, w], g.at[3, w]) for w in range(4)]
+
+    for w in range(4):
+        for copy in g_second[w]:
+            copy.wait_recv()
+        for b in range(buckets):
+            rs = bucket_rows(b)
+            total = nn(acts[w, rs, 0:block], g[0, w])
+            for j in range(1, 4):
+                total = total + nn(acts[w, rs, j * block : (j + 1) * block], g[j, w])
+            if w < 3:
+                rkv[w, rs] = total.astype(BF)
+            else:
+                gate_raw[rs] = total
+    g_second.append(forward(g_first[4], g.at[1, 4], g.at[2, 4], g.at[3, 4]))
+
+    low = lax.broadcasted_iota(jnp.int32, (rows, 128), 1) < LANE_WIDTH
+    t_square = lax.broadcasted_iota(jnp.int32, (rows, rows), 0)
+    s_square = lax.broadcasted_iota(jnp.int32, (rows, rows), 1)
+    places = lax.broadcasted_iota(jnp.int32, (rows, 1), 0).astype(F32) - float(rows // 2)
+
+    def decay_scales(cols):
+        log_decay = -jnp.exp(head_vec[FADING : FADING + 1, cols])
+        return jnp.exp(log_decay * places), jnp.exp(log_decay * (-1.0 - places))
+
+    def allowed_pairs(b):
+        return jnp.logical_and(s_square < t_square, masks[b][0] == masks[b][1])
+
+    def scores_of(rt, kt, now, mine, allowed):
+        scores = nt(jnp.where(mine, rt, 0.0).astype(BF), kt)
+        here = jnp.sum(jnp.where(mine, now, 0.0), axis=1, keepdims=True)
+        return jnp.where(allowed, scores, jnp.where(s_square == t_square, here, 0.0)).astype(BF)
+
+    def time_forward(b):
+        rs = bucket_rows(b)
+        allowed = allowed_pairs(b)
+        for p in range(pairs):
+            cols = slice(p * 128, (p + 1) * 128)
+            out_scale, in_scale = decay_scales(cols)
+            r, k = rkv[0, rs, cols].astype(F32), rkv[1, rs, cols].astype(F32)
+            v = rkv[2, rs, cols]
+            rt, kt = r * out_scale, (k * in_scale).astype(BF)
+            now = r * head_vec[REWARD : REWARD + 1, cols] * k
+            first = nn(scores_of(rt, kt, now, low, allowed), v)
+            second = nn(scores_of(rt, kt, now, jnp.logical_not(low), allowed), v)
+            wkv = jnp.where(low, first, second)
+            centered = wkv - head_sums(wkv, low) / LANE_WIDTH
+            scale = lax.rsqrt(head_sums(centered * centered, low) / LANE_WIDTH + GROUP_EPSILON)
+            n = centered * scale
+            n_ref[rs, cols] = n
+            n_scale[rs, cols] = scale
+            gate = gate_raw[rs, cols]
+            gained = n * head_vec[LANE : LANE + 1, cols] * gate * jax.nn.sigmoid(gate)
+            mixed[rs, cols] = gained.astype(BF)
+
+    pair_copies = {}
+
+    def scatter_start(k, b, source, lanes):
+        rs = pl.ds(b * rows, rows)
+        return [
+            links.push(source.at[rs, lanes(2 * other + 1 - c)], half.at[k, b, i], mate)
+            for i, other in enumerate(chips_away + [z])
+        ]
+
+    def scatter_middle(k, b, source, lanes, first):
+        rs = pl.ds(b * rows, rows)
+        copies = []
+        for i, other in enumerate(chips_away):
+            if (b, i) in pair_copies:
+                links.sent(pair_copies[b, i])
+            first[i].wait_recv()
+            value = source[rs, lanes(2 * other + c)].astype(F32) + half[k, b, i].astype(F32)
+            pair[b, i] = value.astype(BF)
+            copy = links.push(pair.at[b, i], far.at[k, b, i], (d, 2 * other + c))
+            pair_copies[b, i] = copy
+            copies.append(copy)
+        return copies
+
+    def scatter_end(k, b, source, lanes, first, second):
+        rs = pl.ds(b * rows, rows)
+        first[chips - 1].wait_recv()
+        total = source[rs, lanes(m)].astype(F32) + half[k, b, chips - 1].astype(F32)
+        for i, copy in enumerate(second):
+            copy.wait_recv()
+            total = total + far[k, b, i].astype(F32)
+        return total
+
+    def stats_start(k, b):
+        return links.push(small.at[k, b, 0], small.at[k, b, 1], mate)
+
+    def stats_middle(k, b, first):
+        first.wait_recv()
+        small[k, b, 2] = small[k, b, 0] + small[k, b, 1]
+        return [
+            links.push(small.at[k, b, 2], small.at[k, b, 3 + i], (d, 2 * other + c))
+            for i, other in enumerate(chips_away)
+        ]
+
+    eye8 = jnp.where(lax.broadcasted_iota(jnp.int32, (16, 128), 0) == 0, 1.0, 0.0)
+    eye16 = jnp.where(lax.broadcasted_iota(jnp.int32, (16, 128), 0) == 8, 1.0, 0.0)
+
+    def stats_end(k, b, second):
+        total = small[k, b, 2]
+        for i, copy in enumerate(second):
+            copy.wait_recv()
+            total = total + small[k, b, 3 + i]
+        total = total / width
+        turn = lambda e: lax.dot_general(
+            total, e, (((0,), (0,)), ((), ())), precision=lax.Precision.HIGHEST, preferred_element_type=F32
+        )[:, 0:1]
+        return turn(eye8), turn(eye16)
+
+    def gather_start(source, target, lanes, rs):
+        mine = target.at[rs, lanes(m)]
+        copies = [links.push(source.at[rs], mine, (d, 2 * other + c)) for other in chips_away]
+        copies.append(links.push(source.at[rs], mine, mate))
+        target[rs, lanes(m)] = source[rs]
+        return copies
+
+    def gather_middle(target, lanes, rs, first):
+        copies = []
+        for i in range(chips - 1):
+            source = 2 * lax.rem(z - (i + 1) + chips, chips) + c
+            first[i].wait_recv()
+            copies.append(links.push(target.at[rs, lanes(source)], target.at[rs, lanes(source)], mate))
+        return copies
+
+    def gather_end(first, second):
+        first[-1].wait_recv()
+        for copy in second:
+            copy.wait_recv()
+
+    both = (0, 1)
+    slices = [pl.ds(b * rows, rows) for b in both]
+    all_rows = pl.ds(0, buckets * rows)
+
+    for copy in wo_arrivals:
+        copy.wait_recv()
+    first1 = []
+    for b in both:
+        time_forward(b)
+        rs = bucket_rows(b)
+        for j in range(4):
+            cols = slice(j * block, (j + 1) * block)
+            part[0, rs, cols] = nn(mixed[rs], wob[:, cols]).astype(BF)
+        first1.append(scatter_start(0, b, part.at[0], own_lanes))
+    fk_second = forward(fk_first, fkb.at[0], fkb.at[1], fkb.at[2])
+    fv_first = relay_out(fv, fvb.at[0], fvb.at[1])
+    second1 = [scatter_middle(0, b, part.at[0], own_lanes, first1[b]) for b in both]
+    gathers = []
+    for b in both:
+        rs = bucket_rows(b)
+        total = scatter_end(0, b, part.at[0], own_lanes, first1[b], second1[b])
+        middle = x_ref[rs, own_lanes(m)].astype(F32) + total
+        mid_own[rs] = middle
+        mid_own_b[rs] = middle.astype(BF)
+        gathers.append(gather_start(mid_own_b, mid, moved_lanes, slices[b]))
+    onward = [gather_middle(mid, moved_lanes, slices[b], gathers[b]) for b in both]
+    for b in both:
+        gather_end(gathers[b], onward[b])
+        mix(b, take_mid, mean2, rstd2, CLOSING, CLOSING + 1, [kin, cri])
+    for copy in g_second[4]:
+        copy.wait_recv()
+    top_copy.wait()
+
+    def top(b):
+        return seen[bucket_rows(b)].astype(F32) * masks[b][4]
+
+    for b in both:
+        rs = bucket_rows(b)
+        total = nn(cri[rs, 0:block], g[0, 4])
+        for j in range(1, 4):
+            total = total + nn(cri[rs, j * block : (j + 1) * block], g[j, 4])
+        gate = jax.nn.sigmoid(total)
+        channel_gate[rs] = gate
+        cg_own[rs] = (top(b) * gate).astype(BF)
+    gathers = gather_start(cg_own, cg, moved_lanes, all_rows)
+    for copy in fk_second:
+        copy.wait_recv()
+
+    def fk_piece(j):
+        return fk if j == 0 else fkb.at[j - 1]
+
+    def fv_piece(j):
+        return fv if j == 0 else fvb.at[j - 1]
+
+    for b in both:
+        rs = bucket_rows(b)
+        total = nn(kin[rs, 0:block], fk[...])
+        for j in range(1, 4):
+            total = total + nn(kin[rs, j * block : (j + 1) * block], fkb[j - 1])
+        positive = jnp.maximum(total, 0.0)
+        hid[rs] = (positive * positive).astype(BF)
+        pos[rs] = positive.astype(BF)
+    onward = gather_middle(cg, moved_lanes, all_rows, gathers)
+    fv_second = forward(fv_first, fvb.at[0], fvb.at[1], fvb.at[2])
+    gather_end(gathers, onward)
+
+    piece = own
+
+    def product_piece(lhs, rhs, i):
+        return tn(lhs[:, i * piece : (i + 1) * piece], rhs[...])
+
+    def ff_grad_start(k, lhs, rhs):
+        for i, (way, slot) in ((2, (0, 0)), (6, (0, 1)), (5, (1, 0)), (7, (1, 1))):
+            ff_send[k, way, slot] = product_piece(lhs, rhs, i).astype(BF)
+        return (
+            links.push(ff_send.at[k, 0], ff_got.at[k, 0], x_peer),
+            links.push(ff_send.at[k, 1], ff_got.at[k, 1], y_peer),
+        )
+
+    def ff_grad_middle(k, lhs, rhs, first):
+        first[0].wait_recv()
+        links.sent(first[0])
+        ff_send[k, 0, 0] = (product_piece(lhs, rhs, 4) + ff_got[k, 0, 1].astype(F32)).astype(BF)
+        one = links.push(ff_send.at[k, 0, 0], ff_got2.at[k, 0], y_peer)
+        first[1].wait_recv()
+        links.sent(first[1])
+        ff_send[k, 1, 0] = (product_piece(lhs, rhs, 3) + ff_got[k, 1, 1].astype(F32)).astype(BF)
+        return one, links.push(ff_send.at[k, 1, 0], ff_got2.at[k, 1], x_peer)
+
+    def ff_grad_end(k, lhs, rhs, second, out):
+        for way in range(2):
+            second[way].wait_recv()
+            total = product_piece(lhs, rhs, way) + ff_got[k, way, 0].astype(F32) + ff_got2[k, way].astype(F32)
+            out[way * piece : (way + 1) * piece] = total.astype(BF)
+
+    fv_grad1 = ff_grad_start(0, cg, hid)
+
+    for copy in fv_second:
+        copy.wait_recv()
+    first3 = []
+    for b in both:
+        rs = bucket_rows(b)
+        for j in range(4):
+            cols = slice(j * block, (j + 1) * block)
+            part[1, rs, cols] = nt(hid[rs], fv_piece(j)[...]).astype(BF)
+        first3.append(scatter_start(1, b, part.at[1], moved_lanes))
+    second3 = []
+    for b in both:
+        rs = bucket_rows(b)
+        total = nn(cg[rs, 0:block], fv[...])
+        for j in range(1, 4):
+            total = total + nn(cg[rs, j * block : (j + 1) * block], fvb[j - 1])
+        pre[rs] = (total * 2.0 * pos[rs].astype(F32)).astype(BF)
+        second3.append(scatter_middle(1, b, part.at[1], moved_lanes, first3[b]))
+    fk_grad1 = ff_grad_start(1, kin, pre)
+    sens[...] = jnp.zeros_like(sens)
+    head_small[...] = jnp.zeros_like(head_small)
+    gate_first = []
+    out_first = []
+    for b in both:
+        rs = bucket_rows(b)
+        gate = channel_gate[rs]
+        total = scatter_end(1, b, part.at[1], moved_lanes, first3[b], second3[b])
+        out_own[rs] = ((mid_own[rs] + gate * total) * masks[b][4]).astype(BF)
+        gig[rs] = (top(b) * total * gate * (1.0 - gate)).astype(BF)
+
+    ones = jnp.ones((8, own), BF)
+
+    def back_mix(k, b, target, take, mean, rstd, gain_row, mix_row, sens_row, grads):
+        rs = bucket_rows(b)
+        same, following = masks[b][2], masks[b][3]
+        average, scale = mean[rs, :], rstd[rs, :]
+        one, two = jnp.zeros((8, rows), F32), jnp.zeros((8, rows), F32)
+        for e in range(parts):
+            cols = slice(e * own, (e + 1) * own)
+            hat = (take(rs, e).astype(F32) - average) * scale
+            gain = order_vec[gain_row : gain_row + 1, cols]
+            normed = hat * gain
+            change = normed - roll_rows(normed, 1) * same
+            now = jnp.zeros((rows, own), F32)
+            later = jnp.zeros((rows, own), F32)
+            for i, (grad, weight_of) in enumerate(grads):
+                value = nt(grad(rs), weight_of(e))
+                at = slice(sens_row + i, sens_row + i + 1)
+                sens[at, cols] += jnp.sum(value * change, axis=0, keepdims=True)
+                weight = order_vec[mix_row + i : mix_row + i + 1, cols]
+                now = now + value * weight
+                later = later + value * (1.0 - weight)
+            back = now + following * roll_rows(later, -1)
+            target[rs, cols] = back.astype(BF)
+            scaled = back * gain
+            one = one + nt(ones, scaled.astype(BF))
+            two = two + nt(ones, (scaled * hat).astype(BF))
+        small[k, b, 0, 0:8] = one
+        small[k, b, 0, 8:16] = two
+
+    def piece_rows(e):
+        return slice((e % 2) * own, (e % 2 + 1) * own)
+
+    def take_mid_own(rs, e):
+        return mid[rs, e * own : (e + 1) * own]
+
+    def take_x_own(rs, e):
+        start = pl.multiple_of(order[e // 2] * block + (e % 2) * own, own)
+        return x_ref[rs, pl.ds(start, own)]
+
+    def fk_rows(e):
+        return fk_piece(e // 2)[piece_rows(e)]
+
+    def g_rows(w):
+        return lambda e: g[e // 2, w, piece_rows(e)]
+
+    for copies in first1 + second1:
+        for copy in copies:
+            links.sent(copy)
+    first4, stats4 = [], []
+    for b in both:
+        back_mix(
+            0, b, part.at[0], take_mid_own, mean2, rstd2, CLOSING, CLOSING + 1, 4,
+            [(lambda rs: pre[rs], fk_rows), (lambda rs: gig[rs], g_rows(4))],
+        )
+        first4.append(scatter_start(2, b, part.at[0], moved_lanes))
+        stats4.append(stats_start(0, b))
+    second4, stats4b = [], []
+    for b in both:
+        second4.append(scatter_middle(2, b, part.at[0], moved_lanes, first4[b]))
+        stats4b.append(stats_middle(0, b, stats4[b]))
+    fv_grad2 = ff_grad_middle(0, cg, hid, fv_grad1)
+
+    def norm_back(b, back, hat, gain_row, rstd, means):
+        gain = vec[gain_row : gain_row + 1, own_lanes(m)]
+        return (back * gain - means[0] - hat * means[1]) * rstd[bucket_rows(b), :]
+
+    closing = jnp.zeros((1, own), F32)
+    gathers = []
+    for b in both:
+        rs = bucket_rows(b)
+        back = scatter_end(2, b, part.at[0], moved_lanes, first4[b], second4[b])
+        means = stats_end(0, b, stats4b[b])
+        hat = (mid_own_b[rs].astype(F32) - mean2[rs, :]) * rstd2[rs, :]
+        closing = closing + jnp.sum(back * hat, axis=0, keepdims=True)
+        value = top(b) + norm_back(b, back, hat, CLOSING, rstd2, means)
+        middle_grad[rs] = value
+        branch_own[rs] = value.astype(BF)
+        gathers.append(gather_start(branch_own, branch, own_lanes, slices[b]))
+    onward = [gather_middle(branch, own_lanes, slices[b], gathers[b]) for b in both]
+    fk_grad2 = ff_grad_middle(1, kin, pre, fk_grad1)
+
+    def time_backward(b):
+        rs = bucket_rows(b)
+        allowed = allowed_pairs(b)
+        for p in range(pairs):
+            cols = slice(p * 128, (p + 1) * 128)
+            out_scale, in_scale = decay_scales(cols)
+            u, gn = head_vec[REWARD : REWARD + 1, cols], head_vec[LANE : LANE + 1, cols]
+            g_in, gate, n = mixed_grad[rs, cols], gate_raw[rs, cols], n_ref[rs, cols]
+            sg = jax.nn.sigmoid(gate)
+            silu = gate * sg
+            time_grads[3, rs, cols] = (g_in * n * gn * sg * (1.0 + gate * (1.0 - sg))).astype(BF)
+            q = g_in * gn * silu
+            dout = q - head_sums(q, low) / LANE_WIDTH - n * (head_sums(q * n, low) / LANE_WIDTH)
+            dout = dout * n_scale[rs, cols]
+            r, k = rkv[0, rs, cols].astype(F32), rkv[1, rs, cols].astype(F32)
+            v = rkv[2, rs, cols]
+            rt, kt = r * out_scale, (k * in_scale).astype(BF)
+            rtb = rt.astype(BF)
+            now = r * u * k
+            diag = head_sums(dout * v.astype(F32), low)
+            found = []
+            for mine in (low, jnp.logical_not(low)):
+                dmine = jnp.where(mine, dout, 0.0).astype(BF)
+                scores = scores_of(rt, kt, now, mine, allowed)
+                a = jnp.where(allowed, nt(dmine, v), 0.0).astype(BF)
+                found.append((tn(scores, dmine), nn(a, kt), tn(a, rtb)))
+            dv, drt, dkt = (jnp.where(low, one, two) for one, two in zip(*found))
+            time_grads[0, rs, cols] = (drt * out_scale + u * k * diag).astype(BF)
+            time_grads[1, rs, cols] = (dkt * in_scale + u * r * diag).astype(BF)
+            time_grads[2, rs, cols] = dv.astype(BF)
+            lags = places * rtb.astype(F32) * drt - (places + 1.0) * kt.astype(F32) * dkt
+            log_decay = -jnp.exp(head_vec[FADING : FADING + 1, cols])
+            head_small[0:1, cols] += jnp.sum(lags, axis=0, keepdims=True) * log_decay
+            head_small[1:2, cols] += jnp.sum(r * k * diag, axis=0, keepdims=True)
+            head_small[2:3, cols] += jnp.sum(g_in * n * silu, axis=0, keepdims=True)
+
+    for copies in first3 + second3:
+        for copy in copies:
+            links.sent(copy)
+    first6, stats6 = [], []
+    for b in both:
+        gather_end(gathers[b], onward[b])
+        rs = bucket_rows(b)
+        mixed_grad[rs] = nt(branch[rs], wob[...])
+        time_backward(b)
+        back_mix(
+            1, b, part.at[1], take_x_own, mean1, rstd1, OPENING, OPENING + 1, 0,
+            [((lambda rs, w=w: time_grads[w, rs]), g_rows(w)) for w in range(4)],
+        )
+        first6.append(scatter_start(3, b, part.at[1], moved_lanes))
+        stats6.append(stats_start(1, b))
+
+    def tm_lhs(w):
+        return acts.at[w] if w < 4 else cri
+
+    def tm_rhs(w):
+        return time_grads.at[w] if w < 4 else gig
+
+    tm_first = {}
+    for w in (4, 0, 1, 2, 3):
+        for i, (way, slot) in ((2, (0, 0)), (6, (0, 1)), (5, (1, 0)), (7, (1, 1))):
+            tm_send[w, way, slot] = product_piece(tm_lhs(w), tm_rhs(w), i).astype(BF)
+        tm_first[w] = (
+            links.push(tm_send.at[w, 0], tm_got.at[w, 0], x_peer),
+            links.push(tm_send.at[w, 1], tm_got.at[w, 1], y_peer),
+        )
+    second6, stats6b = [], []
+    for b in both:
+        second6.append(scatter_middle(3, b, part.at[1], moved_lanes, first6[b]))
+        stats6b.append(stats_middle(1, b, stats6[b]))
+    for j in range(4):
+        wo_part[j] = tn(mixed[:, j * LANE_WIDTH : (j + 1) * LANE_WIDTH], branch[...]).astype(BF)
+    wo_copies = [
+        links.push(wo_part.at[peer[0]], wo_got.at[i], peer) for i, peer in enumerate((x_peer, y_peer, diagonal))
+    ]
+    ff_grad_end(0, cg, hid, fv_grad2, ffv_out)
+    tm_second = {}
+    for w in (4, 0, 1, 2, 3):
+        tm_first[w][0].wait_recv()
+        links.sent(tm_first[w][0])
+        value = product_piece(tm_lhs(w), tm_rhs(w), 4) + tm_got[w, 0, 1].astype(F32)
+        tm_send[w, 0, 0] = value.astype(BF)
+        one = links.push(tm_send.at[w, 0, 0], tm_got2.at[w, 0], y_peer)
+        tm_first[w][1].wait_recv()
+        links.sent(tm_first[w][1])
+        value = product_piece(tm_lhs(w), tm_rhs(w), 3) + tm_got[w, 1, 1].astype(F32)
+        tm_send[w, 1, 0] = value.astype(BF)
+        tm_second[w] = (one, links.push(tm_send.at[w, 1, 0], tm_got2.at[w, 1], x_peer))
+
+    opening = jnp.zeros((1, own), F32)
+    for b in both:
+        rs = bucket_rows(b)
+        back = scatter_end(3, b, part.at[1], moved_lanes, first6[b], second6[b])
+        means = stats_end(1, b, stats6b[b])
+        hat = (x_ref[rs, own_lanes(m)].astype(F32) - mean1[rs, :]) * rstd1[rs, :]
+        opening = opening + jnp.sum(back * hat, axis=0, keepdims=True)
+        value = middle_grad[rs] + norm_back(b, back, hat, OPENING, rstd1, means)
+        gin_own[rs] = value.astype(BF)
+    gin_first = gather_start(gin_own, gin_full, own_lanes, all_rows)
+    out_first = gather_start(out_own, out_full, own_lanes, all_rows)
+
+    vec_copies = links.group(
+        [sens.at[:, moved_lanes(other)] for other in others],
+        [u_got.at[i] for i in range(parts - 1)],
+        [(d, other) for other in others],
+        u_got,
+    )
+    gin_second = gather_middle(gin_full, own_lanes, all_rows, gin_first)
+    out_second = gather_middle(out_full, own_lanes, all_rows, out_first)
+    vec_copies.wait_recv()
+    total = sens[:, moved_lanes(m)]
+    for i in range(parts - 1):
+        total = total + u_got[i]
+    u2_own[0:8] = total
+    u2_own[6:7] = opening
+    u2_own[7:8] = closing
+    u2_own[8:16] = head_small[...]
+    dp_copies = links.group(
+        [u2_own] * 3, [u2_got.at[i] for i in range(3)], [x_peer, y_peer, diagonal], u2_got
+    )
+    dp_copies.wait_recv()
+    u3_own[...] = (u2_own[...] + u2_got[0]) + (u2_got[1] + u2_got[2])
+    all_copies = links.group(
+        [u3_own] * (parts - 1),
+        [u3_got.at[m]] * (parts - 1),
+        [(d, other) for other in others],
+        u3_got.at[pl.ds(0, parts - 1)],
+    )
+    u3_got[m] = u3_own[...]
+
+    back_copies = []
+    for w in (4, 0, 1, 2, 3):
+        links.sent(arrivals[w])
+        sums = blocks.at[w] if w < 4 else channel_sum
+        for way in range(2):
+            tm_second[w][way].wait_recv()
+            value = product_piece(tm_lhs(w), tm_rhs(w), way)
+            value = value + tm_got[w, way, 0].astype(F32) + tm_got2[w, way].astype(F32)
+            sums[4 * way : 4 * way + 4] = value.astype(BF).reshape(4, shard, own)
+        back_copies.append(
+            links.group(
+                [sums.at[other] for other in others],
+                [back_out.at[w, m]] * (parts - 1),
+                [(d, other) for other in others],
+                back_out.at[w, pl.ds(0, parts - 1)],
+            )
+        )
+        back_out[w, m] = sums[m]
+    ff_grad_end(1, kin, pre, fk_grad2, ffk_out)
+    total = wo_part[d].astype(F32)
+    for i, copy in enumerate(wo_copies):
+        copy.wait_recv()
+        total = total + wo_got[i].astype(F32)
+    wo_out[...] = total.astype(BF)
+    all_copies.wait_recv()
+    upper_d = lax.rem(d, 2) == 1
+    low_vec = lax.broadcasted_iota(jnp.int32, (8, 128), 1) < LANE_WIDTH
+    for e in range(2):
+        vec_out[0:8, e * own : (e + 1) * own] = u3_got[2 * d + e, 0:8]
+    for u in range(4):
+        lanes = pl.ds(pl.multiple_of(lax.div(d, 2) * 128, 128), 128)
+        first, second = u3_got[2 * u, 8:16, lanes], u3_got[2 * u + 1, 8:16, lanes]
+        first = jnp.where(upper_d, swap_halves(first), first)
+        second = jnp.where(upper_d, second, swap_halves(second))
+        vec_out[8:16, u * 128 : (u + 1) * 128] = jnp.where(low_vec, first, second)
+    gather_end(gin_first, gin_second)
+    gather_end(out_first, out_second)
+    for copy in back_copies:
+        copy.wait_recv()
+    links.finish()
+
+
+def finish_kernel(out, gin, ffk, ffv, back, wo, out_o, gin_o, ffk_o, ffv_o, r_o, k_o, v_o, g_o, c_o, wo_o):
+    out_o[...] = out[...].reshape(out_o.shape)
+    gin_o[...] = gin[...].reshape(gin_o.shape)
+    ffk_o[...] = ffk[...].astype(F32)
+    ffv_o[...] = ffv[...].astype(F32)
+    wo_o[...] = wo[...].astype(F32)
+    parts, shard, own = back.shape[1:]
+    low = lax.broadcasted_iota(jnp.int32, (shard, 128), 1) < LANE_WIDTH
+    for w, target in enumerate((r_o, k_o, v_o, g_o)):
+        for j in range(4):
+            for u in range(4):
+                lanes = slice((j // 2) * 128, (j // 2 + 1) * 128)
+                first = back[w, 2 * u, :, lanes].astype(F32)
+                second = back[w, 2 * u + 1, :, lanes].astype(F32)
+                if j % 2 == 0:
+                    tile = jnp.where(low, first, swap_halves(second))
+                else:
+                    tile = jnp.where(low, swap_halves(first), second)
+                start = j * 4 * 128 + u * 128
+                target[:, start : start + 128] = tile
+    for to in range(parts):
+        c_o[:, to * own : (to + 1) * own] = back[4, to].astype(F32)
+
+
+def fast_body(*args):
+    (
+        block_arguments, bundled_spans, opening_gain, mix_r, mix_k, mix_v, mix_g, w_recept, w_key, w_value, w_gate,
+        fading, reward, lane_gain, w_out, closing_gain, mix_fk, mix_fr, fk, fv, w_channel, upstream,
+    ) = args
+    buckets, bucket_rows, width = block_arguments.shape
+    rows = buckets * bucket_rows
+    parts, chips = 8, 4
+    own, block = width // parts, width // 4
+    hidden = fk.shape[1]
+    shard = w_out.shape[0]
+    vectors = [
+        opening_gain, mix_r, mix_k, mix_v, mix_g, closing_gain, mix_fk, mix_fr, fading, reward, lane_gain,
+    ]
+    vec = jnp.stack(vectors + [opening_gain] * (16 - len(vectors)))
+    v, sm = pltpu.VMEM, pltpu.SMEM
+    vm = pl.BlockSpec(memory_space=pltpu.VMEM)
+    half_block = block // 2
+    scratch = [
+        v((4, parts, shard, own), BF), v((4, 5, block, own), BF), v((3, block, hidden), BF), v((3, block, hidden), BF),
+        v((4 * shard, width), BF), v((4, rows, width), BF), v((rows, 1), F32), v((rows, 1), F32), v((rows, 1), F32),
+        v((rows, 1), F32), v((16, width), F32), v((16, own), F32), v((rows, own), BF),
+        v((3, rows, own), BF), v((rows, own), F32), v((rows, own), F32), v((rows, own), F32), v((rows, own), BF),
+        v((2, rows, width), BF), v((4, buckets, chips, bucket_rows, own), BF),
+        v((buckets, chips - 1, bucket_rows, own), BF), v((4, buckets, chips - 1, bucket_rows, own), BF),
+        v((2, buckets, chips + 2, 16, bucket_rows), F32),
+        v((rows, own), F32), v((rows, own), BF), v((rows, width), BF), v((rows, width), BF), v((rows, width), BF),
+        v((rows, hidden), BF), v((rows, hidden), BF), v((rows, hidden), BF), v((rows, own), F32), v((rows, own), BF),
+        v((rows, width), BF),
+        v((rows, own), BF), v((rows, own), BF), v((rows, own), F32), v((rows, own), BF),
+        v((rows, width), BF), v((rows, own), F32), v((4, rows, own), BF), v((8, width), F32), v((8, own), F32),
+        v((2, 2, 2, own, hidden), BF), v((2, 2, 2, own, hidden), BF), v((2, 2, own, hidden), BF),
+        v((5, 2, 2, own, own), BF), v((5, 2, 2, own, own), BF), v((5, 2, own, own), BF),
+        v((parts, shard, own), BF),
+        v((4, shard, width), BF), v((3, shard, width), BF), v((rows, own), BF),
+        v((parts - 1, 8, own), F32), v((16, own), F32), v((3, 16, own), F32), v((16, own), F32),
+        v((parts, 16, own), F32),
+        pltpu.SemaphoreType.DMA((COPIES,)), pltpu.SemaphoreType.DMA((COPIES,)), pltpu.SemaphoreType.DMA,
+    ]
+    out = pl.pallas_call(
+        block_kernel,
+        out_shape=[
+            struct((rows, width), BF), struct((rows, width), BF), struct((block, hidden), BF),
+            struct((block, hidden), BF), struct((5, parts, shard, own), BF), struct((shard, width), BF),
+            struct((16, block), F32),
+        ],
+        in_specs=[pl.BlockSpec(memory_space=sm), vm, pl.BlockSpec(memory_space=pl.ANY)] + [vm] * 9,
+        out_specs=[vm] * 7,
+        scratch_shapes=scratch,
+        compiler_params=pltpu.CompilerParams(
+            collective_id=0, has_side_effects=True, vmem_limit_bytes=VMEM_LIMIT
+        ),
+        name="whole_block",
+    )(
+        bundled_spans.reshape(buckets, -1), block_arguments.reshape(rows, width), upstream.reshape(rows, width), vec,
+        w_recept, w_key, w_value, w_gate, w_out, w_channel, fk, fv,
+    )
+    small = out[6]
+    square = struct((shard, width), F32)
+    done = pl.pallas_call(
+        finish_kernel,
+        out_shape=[
+            struct(block_arguments.shape, BF), struct(block_arguments.shape, BF), struct(fk.shape, F32),
+            struct(fv.shape, F32), square, square, square, square, square, square,
+        ],
+        in_specs=[vm] * 6,
+        out_specs=[vm] * 10,
+        compiler_params=pltpu.CompilerParams(vmem_limit_bytes=48 << 20),
+        name="finish",
+    )(*out[:6])
+    outputs, grad_inputs, d_fk, d_fv, d_r, d_k, d_v, d_g, d_c, d_o = done
+    return (
+        outputs, grad_inputs, small[6], small[0], small[1], small[2], small[3], d_r, d_k, d_v, d_g,
+        small[8], small[9], small[10], d_o, small[7], small[4], small[5], d_fk, d_fv, d_c,
+    )
+
+
+def body(*args):
+    data_parts, parts = lax.axis_size("dp"), lax.axis_size("mp")
+    width, shard, hidden = args[0].shape[2], args[7].shape[0], args[18].shape[1]
+    fitted = (
+        data_parts == 4
+        and parts == 8
+        and shard == LANE_WIDTH
+        and width == 4 * parts * shard
+        and hidden % 128 == 0
+        and args[0].shape[:2] == (2, 128)
+    )
+    return fast_body(*args) if fitted else general_body(*args)
+
+
 def solution(mesh):
     return jax.shard_map(
         body,

time: 1270 us -> 322 us (0.25)
  waiting for transfers between devices: 616 us -> 0 us
  Pallas kernels: 0 us -> 304 us
  matrix products: 255 us -> 0 us
  local copies, waits for them, and re-layouts: 218 us -> 11.9 us
  other arithmetic: 133 us -> 0 us
  between operations: 18.9 us -> 0.87 us
  blocking collectives: 13.1 us -> 0 us
    all_gather x8 -> x0, waiting for transfers between devices: 449 us -> none  [the longest x1 76.6 us: body(): lax.all_gather(feedforward_accept_weights, ('dp', 'mp'), axis=0, tiled=True)]
    pallas_call x0 -> x2, Pallas kernels: none -> 304 us  [the longest x1 300 us: fast_body(): pl.pallas_call(block_kernel, out_shape=[struct((rows, width), BF), struct...]
    dot_general x72 -> x0, matrix products: 255 us -> none  [the longest x16 75.7 us: product_back(): lax.dot_general(first_operand, second_operand, (((1,), (1,)), ((), ())),...]
    reduce_scatter x8 -> x0, waiting for transfers between devices: 89.2 us -> none  [body(): lax.psum_scatter(shortened(summed), 'dp', scatter_dimension=0, tiled=True)]
    psum x2 -> x0, waiting for transfers between devices: 72.5 us -> none  [body(): lax.psum(product_back(hidden, hidden_value).astype(jnp.bfloat16), 'mp')]
    reshape x21 -> x0, local copies, waits for them, and re-layouts: 59.6 us -> none  [the longest x4 13.5 us: group_norm(): grouped = values.reshape(values.shape[0], head_count, -1)]
    convert_element_type x24 -> x0, local copies, waits for them, and re-layouts: 55.6 us -> none  [the longest x8 16.6 us: body(): front_piece.astype(jnp.bfloat16)]
    convert_element_type x49 -> x0, other arithmetic: 47 us -> none  [the longest x19 22.9 us: body(): part.astype(jnp.float32)]
  transfers between devices with their start and end apart: 18 -> 0, of which waited for: 12 -> 0; matrix products, arithmetic and copies ran while one was open for 27% -> 0% of each run, Pallas kernels for 0% -> 0%
where the time goes in v2:
time: 322 us; the launch traced here: 316 us
  Pallas kernels  304 us (94%)
  local copies, waits for them, and re-layouts  11.9 us (4%)
    pallas_call x1, Pallas kernels, fast_body(): pl.pallas_call(block_kernel, out_shape=[struct((rows, width), BF), struct...  300 us
    unnamed x12, local copies, waits for them, and re-layouts  7.07 us

profile of v2, /device:TPU:1, one launch (start us, length us, event | category | flops | bytes accessed | tf_op | source)
XLA Modules:
  0.0 316.3 jit_solution(7364310956790326482)
XLA Ops:
  0.7 3.1 stack.52.vec
  3.8 299.7 %whole_block.1 = (bf16[256,2048]{1,0:T(8,128)(2,1)}, bf16[256,2048]{1,0:T(8,128)(2,1)}, bf16[512,896]{1,0:T(8,128)(2,1)}, bf16[512,896]{1,0:T(8,128)(2,1)}, bf16...) custom-call(s32[2,8]{1,0:T(2,128)} %bitcast.54, bf16[256,2048]{1,0:T(8,128)(2,1)} %bitcast.25, ...), custom_call_target="tpu_custom_call" | custom-call | tf_op jit(solution)/shard_map/whole_block/pallas_call | solution.py:1246
  303.5 1.7 fusion
  305.1 0.0 copy-start
  305.1 1.3 copy-done
  306.5 0.0 copy-start.1
  306.5 1.2 copy-done.1
  307.7 0.0 copy-start.2
  307.7 1.2 copy-done.2
  308.9 0.0 copy-start.3
  308.9 1.2 copy-done.3
  310.1 0.0 copy-start.4
  310.1 1.2 copy-done.4
  311.3 0.0 copy-start.5
  311.3 0.9 copy-done.5
  312.2 3.9 %finish.1 = (bf16[2,128,2048]{2,1,0:T(8,128)(2,1)}, bf16[2,128,2048]{2,1,0:T(8,128)(2,1)}, f32[512,896]{1,0:T(8,128)}, f32[512,896]{1,0:T(8,128)}, f32[64,2048]{...) custom-call(bf16[256,2048]{1,0:T(8,128)(2,1)S(1)} %copy-done.1, ...), custom_call_target="tpu_custom_call" | custom-call | tf_op jit(solution)/shard_map/finish/pallas_call | solution.py:1266
Async XLA Ops:
  305.1 1.3 copy-start
  306.5 1.2 copy-start.1
  307.7 1.2 copy-start.2
  308.9 1.2 copy-start.3
  310.1 1.2 copy-start.4
  311.3 0.9 copy-start.5

commit v3 on v2

--- a/solution.py
+++ b/solution.py
@@ -492,13 +492,13 @@
             copy.wait_send()
 
 
-COPIES = 300
+COPIES = 196
 
 
 def block_kernel(
-    spans, x_ref, up_ref, vec, w_recept, w_key, w_value, w_gate, w_out, w_channel, fk, fv,
+    spans, x_ref, up_ref, v0, v1, v2, v3, v4, v5, v6, v7, v8, v9, v10, w_recept, w_key, w_value, w_gate, w_out, w_channel, fk, fv,
     out_full, gin_full, ffk_out, ffv_out, back_out, wo_out, vec_out,
-    blocks, g, fkb, fvb, wob, acts, mean1, rstd1, mean2, rstd2, order_vec, head_vec, seen,
+    vec, blocks, g, fkb, fvb, wob, acts, mean1, rstd1, mean2, rstd2, order_vec, head_vec, seen,
     rkv, gate_raw, n_ref, n_scale, mixed, part, half, pair, far, small,
     mid_own, mid_own_b, mid, kin, cri, hid, pos, pre, channel_gate, cg_own, cg,
     out_own, gig, middle_grad, branch_own, branch, mixed_grad, time_grads, sens, head_small,
@@ -541,6 +541,9 @@
     top_copy = pltpu.make_async_copy(up_ref.at[:, own_lanes(m)], seen, local)
     top_copy.start()
     low16 = lax.broadcasted_iota(jnp.int32, (shard, 128), 1) < LANE_WIDTH
+    vec[...] = jnp.zeros_like(vec)
+    for i, ref in enumerate((v0, v1, v2, v3, v4, v5, v6, v7, v8, v9, v10)):
+        vec[i : i + 1] = ref[...]
 
     def head_blocks(w, weight):
         for to in range(parts):
@@ -557,6 +560,7 @@
 
     head_blocks(0, w_recept)
     pl.semaphore_wait(barrier, len(greeted))
+    top_copy.wait()
 
     my_rows = pl.ds(pl.multiple_of(m * shard, shard), shard)
 
@@ -571,6 +575,9 @@
             [(d, other) for other in others],
             g.at[0, w, pl.ds(0, (parts - 1) * shard)],
         )
+
+    def relay_out(source, slot1, slot2):
+        return links.push(source, slot1, x_peer), links.push(source, slot2, y_peer)
 
     arrivals = [exchange(0)]
     for w, weight in ((1, w_key), (2, w_value), (3, w_gate)):
@@ -583,6 +590,7 @@
     out_rows = pl.ds(pl.multiple_of(d * shard, shard), shard)
     wo_arrivals = [links.push(w_out, wob.at[out_rows], peer) for peer in (x_peer, y_peer, diagonal)]
     wob[out_rows] = w_out[...]
+    fk_first = relay_out(fk, fkb.at[0], fkb.at[1])
 
     for j in range(4):
         order_vec[:, j * block : (j + 1) * block] = vec[
@@ -648,9 +656,6 @@
     def take_mid(rs, j):
         return mid[rs, j * block : (j + 1) * block]
 
-    def relay_out(source, slot1, slot2):
-        return links.push(source, slot1, x_peer), links.push(source, slot2, y_peer)
-
     for b in range(buckets):
         mix(b, take_x, mean1, rstd1, OPENING, OPENING + 1, [acts.at[w] for w in range(4)])
 
@@ -667,7 +672,6 @@
         copies[1].wait_recv()
         return one, links.push(slot2.at[lower_half], slot3.at[lower_half], x_peer)
 
-    fk_first = relay_out(fk, fkb.at[0], fkb.at[1])
     g_second = [forward(g_first[w], g.at[1, w], g.at[2, w], g.at[3, w]) for w in range(4)]
 
     for w in range(4):
@@ -683,6 +687,7 @@
             else:
                 gate_raw[rs] = total
     g_second.append(forward(g_first[4], g.at[1, 4], g.at[2, 4], g.at[3, 4]))
+    fk_second = forward(fk_first, fkb.at[0], fkb.at[1], fkb.at[2])
 
     low = lax.broadcasted_iota(jnp.int32, (rows, 128), 1) < LANE_WIDTH
     t_square = lax.broadcasted_iota(jnp.int32, (rows, rows), 0)
@@ -814,7 +819,6 @@
             cols = slice(j * block, (j + 1) * block)
             part[0, rs, cols] = nn(mixed[rs], wob[:, cols]).astype(BF)
         first1.append(scatter_start(0, b, part.at[0], own_lanes))
-    fk_second = forward(fk_first, fkb.at[0], fkb.at[1], fkb.at[2])
     fv_first = relay_out(fv, fvb.at[0], fvb.at[1])
     second1 = [scatter_middle(0, b, part.at[0], own_lanes, first1[b]) for b in both]
     gathers = []
@@ -831,7 +835,6 @@
         mix(b, take_mid, mean2, rstd2, CLOSING, CLOSING + 1, [kin, cri])
     for copy in g_second[4]:
         copy.wait_recv()
-    top_copy.wait()
 
     def top(b):
         return seen[bucket_rows(b)].astype(F32) * masks[b][4]
@@ -894,6 +897,50 @@
             second[way].wait_recv()
             total = product_piece(lhs, rhs, way) + ff_got[k, way, 0].astype(F32) + ff_got2[k, way].astype(F32)
             out[way * piece : (way + 1) * piece] = total.astype(BF)
+
+    tm_first, tm_second, back_copies = {}, {}, []
+
+    def tm_lhs(w):
+        return acts.at[w] if w < 4 else cri
+
+    def tm_rhs(w):
+        return time_grads.at[w] if w < 4 else gig
+
+    def tm_grad_start(w):
+        for i, (way, slot) in ((2, (0, 0)), (6, (0, 1)), (5, (1, 0)), (7, (1, 1))):
+            tm_send[w, way, slot] = product_piece(tm_lhs(w), tm_rhs(w), i).astype(BF)
+        tm_first[w] = (
+            links.push(tm_send.at[w, 0], tm_got.at[w, 0], x_peer),
+            links.push(tm_send.at[w, 1], tm_got.at[w, 1], y_peer),
+        )
+
+    def tm_grad_middle(w):
+        copies = []
+        for way, (i, peer) in enumerate(((4, y_peer), (3, x_peer))):
+            value = product_piece(tm_lhs(w), tm_rhs(w), i)
+            tm_first[w][way].wait_recv()
+            links.sent(tm_first[w][way])
+            tm_send[w, way, 0] = (value + tm_got[w, way, 1].astype(F32)).astype(BF)
+            copies.append(links.push(tm_send.at[w, way, 0], tm_got2.at[w, way], peer))
+        tm_second[w] = copies
+
+    def tm_grad_end(w):
+        links.sent(arrivals[w])
+        sums = blocks.at[w] if w < 4 else channel_sum
+        for way in range(2):
+            value = product_piece(tm_lhs(w), tm_rhs(w), way)
+            tm_second[w][way].wait_recv()
+            value = value + tm_got[w, way, 0].astype(F32) + tm_got2[w, way].astype(F32)
+            sums[4 * way : 4 * way + 4] = value.astype(BF).reshape(4, shard, own)
+        back_copies.append(
+            links.group(
+                [sums.at[other] for other in others],
+                [back_out.at[w, m]] * (parts - 1),
+                [(d, other) for other in others],
+                back_out.at[w, pl.ds(0, parts - 1)],
+            )
+        )
+        back_out[w, m] = sums[m]
 
     fv_grad1 = ff_grad_start(0, cg, hid)
 
@@ -925,6 +972,7 @@
         total = scatter_end(1, b, part.at[1], moved_lanes, first3[b], second3[b])
         out_own[rs] = ((mid_own[rs] + gate * total) * masks[b][4]).astype(BF)
         gig[rs] = (top(b) * total * gate * (1.0 - gate)).astype(BF)
+    tm_grad_start(4)
 
     ones = jnp.ones((8, own), BF)
 
@@ -1051,6 +1099,13 @@
     for b in both:
         gather_end(gathers[b], onward[b])
         rs = bucket_rows(b)
+        if b == 1:
+            for j in range(4):
+                wo_part[j] = tn(mixed[:, j * LANE_WIDTH : (j + 1) * LANE_WIDTH], branch[...]).astype(BF)
+            wo_copies = [
+                links.push(wo_part.at[peer[0]], wo_got.at[i], peer)
+                for i, peer in enumerate((x_peer, y_peer, diagonal))
+            ]
         mixed_grad[rs] = nt(branch[rs], wob[...])
         time_backward(b)
         back_mix(
@@ -1060,43 +1115,18 @@
         first6.append(scatter_start(3, b, part.at[1], moved_lanes))
         stats6.append(stats_start(1, b))
 
-    def tm_lhs(w):
-        return acts.at[w] if w < 4 else cri
-
-    def tm_rhs(w):
-        return time_grads.at[w] if w < 4 else gig
-
-    tm_first = {}
-    for w in (4, 0, 1, 2, 3):
-        for i, (way, slot) in ((2, (0, 0)), (6, (0, 1)), (5, (1, 0)), (7, (1, 1))):
-            tm_send[w, way, slot] = product_piece(tm_lhs(w), tm_rhs(w), i).astype(BF)
-        tm_first[w] = (
-            links.push(tm_send.at[w, 0], tm_got.at[w, 0], x_peer),
-            links.push(tm_send.at[w, 1], tm_got.at[w, 1], y_peer),
-        )
+    for w in (0, 1):
+        tm_grad_start(w)
     second6, stats6b = [], []
     for b in both:
         second6.append(scatter_middle(3, b, part.at[1], moved_lanes, first6[b]))
         stats6b.append(stats_middle(1, b, stats6[b]))
-    for j in range(4):
-        wo_part[j] = tn(mixed[:, j * LANE_WIDTH : (j + 1) * LANE_WIDTH], branch[...]).astype(BF)
-    wo_copies = [
-        links.push(wo_part.at[peer[0]], wo_got.at[i], peer) for i, peer in enumerate((x_peer, y_peer, diagonal))
-    ]
+    out_first = gather_start(out_own, out_full, own_lanes, all_rows)
     ff_grad_end(0, cg, hid, fv_grad2, ffv_out)
-    tm_second = {}
-    for w in (4, 0, 1, 2, 3):
-        tm_first[w][0].wait_recv()
-        links.sent(tm_first[w][0])
-        value = product_piece(tm_lhs(w), tm_rhs(w), 4) + tm_got[w, 0, 1].astype(F32)
-        tm_send[w, 0, 0] = value.astype(BF)
-        one = links.push(tm_send.at[w, 0, 0], tm_got2.at[w, 0], y_peer)
-        tm_first[w][1].wait_recv()
-        links.sent(tm_first[w][1])
-        value = product_piece(tm_lhs(w), tm_rhs(w), 3) + tm_got[w, 1, 1].astype(F32)
-        tm_send[w, 1, 0] = value.astype(BF)
-        tm_second[w] = (one, links.push(tm_send.at[w, 1, 0], tm_got2.at[w, 1], x_peer))
-
+    tm_grad_middle(4)
+    tm_grad_middle(0)
+    tm_grad_start(2)
+    out_second = gather_middle(out_full, own_lanes, all_rows, out_first)
     opening = jnp.zeros((1, own), F32)
     for b in both:
         rs = bucket_rows(b)
@@ -1107,7 +1137,9 @@
         value = middle_grad[rs] + norm_back(b, back, hat, OPENING, rstd1, means)
         gin_own[rs] = value.astype(BF)
     gin_first = gather_start(gin_own, gin_full, own_lanes, all_rows)
-    out_first = gather_start(out_own, out_full, own_lanes, all_rows)
+    tm_grad_middle(1)
+    tm_grad_start(3)
+    tm_grad_end(4)
 
     vec_copies = links.group(
         [sens.at[:, moved_lanes(other)] for other in others],
@@ -1116,7 +1148,6 @@
         u_got,
     )
     gin_second = gather_middle(gin_full, own_lanes, all_rows, gin_first)
-    out_second = gather_middle(out_full, own_lanes, all_rows, out_first)
     vec_copies.wait_recv()
     total = sens[:, moved_lanes(m)]
     for i in range(parts - 1):
@@ -1128,6 +1159,10 @@
     dp_copies = links.group(
         [u2_own] * 3, [u2_got.at[i] for i in range(3)], [x_peer, y_peer, diagonal], u2_got
     )
+    tm_grad_end(0)
+    tm_grad_middle(2)
+    tm_grad_end(1)
+    tm_grad_middle(3)
     dp_copies.wait_recv()
     u3_own[...] = (u2_own[...] + u2_got[0]) + (u2_got[1] + u2_got[2])
     all_copies = links.group(
@@ -1138,30 +1173,14 @@
     )
     u3_got[m] = u3_own[...]
 
-    back_copies = []
-    for w in (4, 0, 1, 2, 3):
-        links.sent(arrivals[w])
-        sums = blocks.at[w] if w < 4 else channel_sum
-        for way in range(2):
-            tm_second[w][way].wait_recv()
-            value = product_piece(tm_lhs(w), tm_rhs(w), way)
-            value = value + tm_got[w, way, 0].astype(F32) + tm_got2[w, way].astype(F32)
-            sums[4 * way : 4 * way + 4] = value.astype(BF).reshape(4, shard, own)
-        back_copies.append(
-            links.group(
-                [sums.at[other] for other in others],
-                [back_out.at[w, m]] * (parts - 1),
-                [(d, other) for other in others],
-                back_out.at[w, pl.ds(0, parts - 1)],
-            )
-        )
-        back_out[w, m] = sums[m]
     ff_grad_end(1, kin, pre, fk_grad2, ffk_out)
+    tm_grad_end(2)
     total = wo_part[d].astype(F32)
     for i, copy in enumerate(wo_copies):
         copy.wait_recv()
         total = total + wo_got[i].astype(F32)
     wo_out[...] = total.astype(BF)
+    tm_grad_end(3)
     all_copies.wait_recv()
     upper_d = lax.rem(d, 2) == 1
     low_vec = lax.broadcasted_iota(jnp.int32, (8, 128), 1) < LANE_WIDTH
@@ -1178,30 +1197,59 @@
     for copy in back_copies:
         copy.wait_recv()
     links.finish()
-
-
-def finish_kernel(out, gin, ffk, ffv, back, wo, out_o, gin_o, ffk_o, ffv_o, r_o, k_o, v_o, g_o, c_o, wo_o):
-    out_o[...] = out[...].reshape(out_o.shape)
-    gin_o[...] = gin[...].reshape(gin_o.shape)
-    ffk_o[...] = ffk[...].astype(F32)
-    ffv_o[...] = ffv[...].astype(F32)
-    wo_o[...] = wo[...].astype(F32)
-    parts, shard, own = back.shape[1:]
+    assert links.used == COPIES, links.used
+
+
+def finish_kernel(
+    out, gin, ffk, ffv, back, wo, vec,
+    out_o, gin_o, ffk_o, ffv_o, r_o, k_o, v_o, g_o, c_o, wo_o,
+    y0, y1, y2, y3, y4, y5, y6, y7, y8, y9, y10,
+    ffk_v, ffv_v, back_v, wo_v, ffk_f, ffv_f, square, read, write,
+):
+    buckets, rows = out_o.shape[:2]
+    reads = [
+        pltpu.make_async_copy(a, b, read.at[i])
+        for i, (a, b) in enumerate(((ffv, ffv_v), (ffk, ffk_v), (wo, wo_v), (back, back_v)))
+    ]
+    for copy in reads:
+        copy.start()
+    writes = []
+
+    def store(source, target):
+        copy = pltpu.make_async_copy(source, target, write.at[len(writes)])
+        copy.start()
+        writes.append(copy)
+
+    for source, target in ((out, out_o), (gin, gin_o)):
+        for b in range(buckets):
+            store(source.at[pl.ds(b * rows, rows)], target.at[b])
+    for i, ref in enumerate((y0, y1, y2, y3, y4, y5, y6, y7, y8, y9, y10)):
+        ref[...] = vec[i : i + 1]
+    for copy, source, middle, target in zip(reads, (ffv_v, ffk_v, wo_v), (ffv_f, ffk_f, square.at[5]), (ffv_o, ffk_o, wo_o)):
+        copy.wait()
+        middle[...] = source[...].astype(F32)
+        store(middle, target)
+    reads[3].wait()
+    parts, shard, own = back_v.shape[1:]
     low = lax.broadcasted_iota(jnp.int32, (shard, 128), 1) < LANE_WIDTH
+    for to in range(parts):
+        square[4, :, to * own : (to + 1) * own] = back_v[4, to].astype(F32)
+    store(square.at[4], c_o)
     for w, target in enumerate((r_o, k_o, v_o, g_o)):
         for j in range(4):
             for u in range(4):
                 lanes = slice((j // 2) * 128, (j // 2 + 1) * 128)
-                first = back[w, 2 * u, :, lanes].astype(F32)
-                second = back[w, 2 * u + 1, :, lanes].astype(F32)
+                first = back_v[w, 2 * u, :, lanes].astype(F32)
+                second = back_v[w, 2 * u + 1, :, lanes].astype(F32)
                 if j % 2 == 0:
                     tile = jnp.where(low, first, swap_halves(second))
                 else:
                     tile = jnp.where(low, swap_halves(first), second)
                 start = j * 4 * 128 + u * 128
-                target[:, start : start + 128] = tile
-    for to in range(parts):
-        c_o[:, to * own : (to + 1) * own] = back[4, to].astype(F32)
+                square[w, :, start : start + 128] = tile
+        store(square.at[w], target)
+    for copy in writes:
+        copy.wait()
 
 
 def fast_body(*args):
@@ -1218,12 +1266,12 @@
     vectors = [
         opening_gain, mix_r, mix_k, mix_v, mix_g, closing_gain, mix_fk, mix_fr, fading, reward, lane_gain,
     ]
-    vec = jnp.stack(vectors + [opening_gain] * (16 - len(vectors)))
+    vectors = [vector.reshape(1, width) for vector in vectors]
     v, sm = pltpu.VMEM, pltpu.SMEM
     vm = pl.BlockSpec(memory_space=pltpu.VMEM)
     half_block = block // 2
     scratch = [
-        v((4, parts, shard, own), BF), v((4, 5, block, own), BF), v((3, block, hidden), BF), v((3, block, hidden), BF),
+        v((16, width), F32), v((4, parts, shard, own), BF), v((4, 5, block, own), BF), v((3, block, hidden), BF), v((3, block, hidden), BF),
         v((4 * shard, width), BF), v((4, rows, width), BF), v((rows, 1), F32), v((rows, 1), F32), v((rows, 1), F32),
         v((rows, 1), F32), v((16, width), F32), v((16, own), F32), v((rows, own), BF),
         v((3, rows, own), BF), v((rows, own), F32), v((rows, own), F32), v((rows, own), F32), v((rows, own), BF),
@@ -1250,7 +1298,7 @@
             struct((block, hidden), BF), struct((5, parts, shard, own), BF), struct((shard, width), BF),
             struct((16, block), F32),
         ],
-        in_specs=[pl.BlockSpec(memory_space=sm), vm, pl.BlockSpec(memory_space=pl.ANY)] + [vm] * 9,
+        in_specs=[pl.BlockSpec(memory_space=sm), vm, pl.BlockSpec(memory_space=pl.ANY)] + [vm] * 19,
         out_specs=[vm] * 7,
         scratch_shapes=scratch,
         compiler_params=pltpu.CompilerParams(
@@ -1258,23 +1306,30 @@
         ),
         name="whole_block",
     )(
-        bundled_spans.reshape(buckets, -1), block_arguments.reshape(rows, width), upstream.reshape(rows, width), vec,
+        bundled_spans.reshape(buckets, -1), block_arguments.reshape(rows, width), upstream.reshape(rows, width), *vectors,
         w_recept, w_key, w_value, w_gate, w_out, w_channel, fk, fv,
     )
-    small = out[6]
     square = struct((shard, width), F32)
+    hbm = pl.BlockSpec(memory_space=pl.ANY)
     done = pl.pallas_call(
         finish_kernel,
         out_shape=[
             struct(block_arguments.shape, BF), struct(block_arguments.shape, BF), struct(fk.shape, F32),
             struct(fv.shape, F32), square, square, square, square, square, square,
+        ]
+        + [struct((1, block), F32)] * 11,
+        in_specs=[hbm] * 6 + [vm],
+        out_specs=[hbm] * 10 + [vm] * 11,
+        scratch_shapes=[
+            v(fk.shape, BF), v(fv.shape, BF), v((5, parts, shard, own), BF), v((shard, width), BF),
+            v(fk.shape, F32), v(fv.shape, F32), v((6, shard, width), F32),
+            pltpu.SemaphoreType.DMA((4,)), pltpu.SemaphoreType.DMA((2 * buckets + 8,)),
         ],
-        in_specs=[vm] * 6,
-        out_specs=[vm] * 10,
-        compiler_params=pltpu.CompilerParams(vmem_limit_bytes=48 << 20),
+        compiler_params=pltpu.CompilerParams(vmem_limit_bytes=VMEM_LIMIT),
         name="finish",
-    )(*out[:6])
-    outputs, grad_inputs, d_fk, d_fv, d_r, d_k, d_v, d_g, d_c, d_o = done
+    )(*out)
+    outputs, grad_inputs, d_fk, d_fv, d_r, d_k, d_v, d_g, d_c, d_o = done[:10]
+    small = [vector.reshape(block) for vector in done[10:]]
     return (
         outputs, grad_inputs, small[6], small[0], small[1], small[2], small[3], d_r, d_k, d_v, d_g,
         small[8], small[9], small[10], d_o, small[7], small[4], small[5], d_fk, d_fv, d_c,

time: 322 us -> 337 us (1.047); the launches traced: 316 us -> 337 us
  Pallas kernels: 304 us -> 336 us
  local copies, waits for them, and re-layouts: 11.9 us -> 0 us
    pallas_call x1, Pallas kernels: 3.85 us -> 66.2 us  [fast_body(): pl.pallas_call(finish_kernel, out_shape=[struct(block_arguments.shape, BF...]
    pallas_call x1, Pallas kernels: 300 us -> 270 us  [fast_body(): pl.pallas_call(block_kernel, out_shape=[struct((rows, width), BF), struct...]
    unnamed x12 -> x0, local copies, waits for them, and re-layouts: 7.07 us -> none
where the time goes in v3:
time: 337 us
  Pallas kernels  336 us (100%)
    pallas_call x1, Pallas kernels, fast_body(): pl.pallas_call(block_kernel, out_shape=[struct((rows, width), BF), struct...  270 us
    pallas_call x1, Pallas kernels, fast_body(): pl.pallas_call(finish_kernel, out_shape=[struct(block_arguments.shape, BF...  66.2 us

profile of v3, /device:TPU:1, one launch (start us, length us, event | category | flops | bytes accessed | tf_op | source)
XLA Modules:
  0.0 336.9 jit_solution(995358246581299648)
XLA Ops:
  0.7 269.8 %whole_block.1 = (bf16[256,2048]{1,0:T(8,128)(2,1)}, bf16[256,2048]{1,0:T(8,128)(2,1)}, bf16[512,896]{1,0:T(8,128)(2,1)}, bf16[512,896]{1,0:T(8,128)(2,1)}, bf16...) custom-call(s32[2,8]{1,0:T(2,128)} %bitcast.38, bf16[256,2048]{1,0:T(8,128)(2,1)} %bitcast.25, ...), custom_call_target="tpu_custom_call" | custom-call | tf_op jit(solution)/shard_map/whole_block/pallas_call | solution.py:1294
  270.5 66.2 %finish.1 = (bf16[2,128,2048]{2,1,0:T(8,128)(2,1)}, bf16[2,128,2048]{2,1,0:T(8,128)(2,1)}, f32[512,896]{1,0:T(8,128)}, f32[512,896]{1,0:T(8,128)}, f32[64,2048]{...) custom-call(bf16[256,2048]{1,0:T(8,128)(2,1)} %get-tuple-element.49., ...), custom_call_target="tpu_custom_call" | custom-call | tf_op jit(solution)/shard_map/finish/pallas_call | solution.py:1314

commit v4 on v3

--- a/solution.py
+++ b/solution.py
@@ -492,7 +492,7 @@
             copy.wait_send()
 
 
-COPIES = 196
+COPIES = 204
 
 
 def block_kernel(
@@ -503,7 +503,7 @@
     mid_own, mid_own_b, mid, kin, cri, hid, pos, pre, channel_gate, cg_own, cg,
     out_own, gig, middle_grad, branch_own, branch, mixed_grad, time_grads, sens, head_small,
     ff_send, ff_got, ff_got2, tm_send, tm_got, tm_got2, channel_sum,
-    wo_part, wo_got, gin_own, u_got, u2_own, u2_got, u3_own, u3_got,
+    wo_part, wo_got, wo_send, wo_got2, gin_own, u_got, u2_own, u2_got, u3_own, u3_got,
     send, recv, local,
 ):
     d, m = lax.axis_index("dp"), lax.axis_index("mp")
@@ -538,7 +538,7 @@
     greeted = [(d, other) for other in others] + [x_peer, y_peer, diagonal]
     for peer in greeted:
         pl.semaphore_signal(barrier, inc=1, device_id=peer, device_id_type=MESH)
-    top_copy = pltpu.make_async_copy(up_ref.at[:, own_lanes(m)], seen, local)
+    top_copy = pltpu.make_async_copy(up_ref.at[:, own_lanes(m)], seen, local.at[0])
     top_copy.start()
     low16 = lax.broadcasted_iota(jnp.int32, (shard, 128), 1) < LANE_WIDTH
     vec[...] = jnp.zeros_like(vec)
@@ -558,7 +558,8 @@
                     tile = jnp.where(low16, swap_halves(tiles[0]), tiles[1])
                 blocks[w, to, :, q * 128 : (q + 1) * 128] = tile.astype(BF)
 
-    head_blocks(0, w_recept)
+    for w, weight in enumerate((w_recept, w_key, w_value, w_gate)):
+        head_blocks(w, weight)
     pl.semaphore_wait(barrier, len(greeted))
     top_copy.wait()
 
@@ -576,21 +577,34 @@
             g.at[0, w, pl.ds(0, (parts - 1) * shard)],
         )
 
-    def relay_out(source, slot1, slot2):
-        return links.push(source, slot1, x_peer), links.push(source, slot2, y_peer)
-
-    arrivals = [exchange(0)]
-    for w, weight in ((1, w_key), (2, w_value), (3, w_gate)):
-        head_blocks(w, weight)
-        arrivals.append(exchange(w))
+    half_block = block // 2
+    upper_half, lower_half = pl.ds(0, half_block), pl.ds(half_block, half_block)
+
+    def relay_out(source, slot1, slot2, which):
+        return (
+            links.push(source.at[which], slot1.at[which], x_peer),
+            links.push(source.at[which], slot2.at[which], y_peer),
+        )
+
+    def forward(upper_copies, lower_copies, slot1, slot2, slot3):
+        upper_copies[0].wait_recv()
+        one = links.push(slot1.at[upper_half], slot3.at[upper_half], y_peer)
+        lower_copies[1].wait_recv()
+        two = links.push(slot2.at[lower_half], slot3.at[lower_half], x_peer)
+        return (one, two) + (() if upper_copies is lower_copies else (upper_copies[1], lower_copies[0]))
+
+    fk_upper = relay_out(fk, fkb.at[0], fkb.at[1], upper_half)
+    arrivals = [exchange(w) for w in range(4)]
     arrivals.append(exchange(4))
     for w in range(4):
         g[0, w, my_rows] = blocks[w, m]
     g[0, 4, my_rows] = w_channel[:, own_lanes(m)]
-    out_rows = pl.ds(pl.multiple_of(d * shard, shard), shard)
-    wo_arrivals = [links.push(w_out, wob.at[out_rows], peer) for peer in (x_peer, y_peer, diagonal)]
-    wob[out_rows] = w_out[...]
-    fk_first = relay_out(fk, fkb.at[0], fkb.at[1])
+
+    def out_rows(dp_place, start, size):
+        return pl.ds(pl.multiple_of(dp_place * shard + start, 32), size)
+
+    wo_first = [links.push(w_out, wob.at[out_rows(d, 0, shard)], peer) for peer in (x_peer, y_peer)]
+    wob[out_rows(d, 0, shard)] = w_out[...]
 
     for j in range(4):
         order_vec[:, j * block : (j + 1) * block] = vec[
@@ -646,9 +660,10 @@
             cols = slice(j * block, (j + 1) * block)
             normed = (take(rs, j).astype(F32) - average) * scale * order_vec[gain_row : gain_row + 1, cols]
             before = roll_rows(normed, 1) * same
+            change = normed - before
             for i, out in enumerate(outs):
                 weight = order_vec[mix_row + i : mix_row + i + 1, cols]
-                out[rs, cols] = (normed * weight + before * (1.0 - weight)).astype(BF)
+                out[rs, cols] = (before + change * weight).astype(BF)
 
     def take_x(rs, j):
         return x_ref[rs, pl.ds(pl.multiple_of(order[j] * block, block), block)]
@@ -659,20 +674,21 @@
     for b in range(buckets):
         mix(b, take_x, mean1, rstd1, OPENING, OPENING + 1, [acts.at[w] for w in range(4)])
 
-    half_block = block // 2
     g_first = []
-    for w in range(5):
+    everything = pl.ds(0, block)
+    for w in range(4):
         arrivals[w].wait_recv()
-        g_first.append(relay_out(g.at[0, w], g.at[1, w], g.at[2, w]))
-
-    def forward(copies, slot1, slot2, slot3):
-        upper_half, lower_half = pl.ds(0, half_block), pl.ds(half_block, half_block)
-        copies[0].wait_recv()
-        one = links.push(slot1.at[upper_half], slot3.at[upper_half], y_peer)
-        copies[1].wait_recv()
-        return one, links.push(slot2.at[lower_half], slot3.at[lower_half], x_peer)
-
-    g_second = [forward(g_first[w], g.at[1, w], g.at[2, w], g.at[3, w]) for w in range(4)]
+        g_first.append(relay_out(g.at[0, w], g.at[1, w], g.at[2, w], everything))
+    g_second = [forward(g_first[w], g_first[w], g.at[1, w], g.at[2, w], g.at[3, w]) for w in range(4)]
+    wo_first[0].wait_recv()
+    wo_rows = out_rows(x_peer[0], 0, shard // 2)
+    wo_second = [links.push(wob.at[wo_rows], wob.at[wo_rows], y_peer)]
+    wo_first[1].wait_recv()
+    wo_rows = out_rows(y_peer[0], shard // 2, shard // 2)
+    wo_second.append(links.push(wob.at[wo_rows], wob.at[wo_rows], x_peer))
+    fk_lower = relay_out(fk, fkb.at[0], fkb.at[1], lower_half)
+    arrivals[4].wait_recv()
+    g_first.append(relay_out(g.at[0, 4], g.at[1, 4], g.at[2, 4], everything))
 
     for w in range(4):
         for copy in g_second[w]:
@@ -686,8 +702,7 @@
                 rkv[w, rs] = total.astype(BF)
             else:
                 gate_raw[rs] = total
-    g_second.append(forward(g_first[4], g.at[1, 4], g.at[2, 4], g.at[3, 4]))
-    fk_second = forward(fk_first, fkb.at[0], fkb.at[1], fkb.at[2])
+    fv_upper = relay_out(fv, fvb.at[0], fvb.at[1], upper_half)
 
     low = lax.broadcasted_iota(jnp.int32, (rows, 128), 1) < LANE_WIDTH
     t_square = lax.broadcasted_iota(jnp.int32, (rows, rows), 0)
@@ -729,6 +744,7 @@
             mixed[rs, cols] = gained.astype(BF)
 
     pair_copies = {}
+    own_copies = []
 
     def scatter_start(k, b, source, lanes):
         rs = pl.ds(b * rows, rows)
@@ -785,11 +801,15 @@
         )[:, 0:1]
         return turn(eye8), turn(eye16)
 
-    def gather_start(source, target, lanes, rs):
+    def gather_start(source, target, lanes, rs, keep=None):
         mine = target.at[rs, lanes(m)]
         copies = [links.push(source.at[rs], mine, (d, 2 * other + c)) for other in chips_away]
         copies.append(links.push(source.at[rs], mine, mate))
-        target[rs, lanes(m)] = source[rs]
+        if keep is None:
+            target[rs, lanes(m)] = source[rs]
+        else:
+            own_copies.append(pltpu.make_async_copy(source.at[rs], mine, local.at[keep]))
+            own_copies[-1].start()
         return copies
 
     def gather_middle(target, lanes, rs, first):
@@ -809,7 +829,7 @@
     slices = [pl.ds(b * rows, rows) for b in both]
     all_rows = pl.ds(0, buckets * rows)
 
-    for copy in wo_arrivals:
+    for copy in wo_second:
         copy.wait_recv()
     first1 = []
     for b in both:
@@ -819,7 +839,9 @@
             cols = slice(j * block, (j + 1) * block)
             part[0, rs, cols] = nn(mixed[rs], wob[:, cols]).astype(BF)
         first1.append(scatter_start(0, b, part.at[0], own_lanes))
-    fv_first = relay_out(fv, fvb.at[0], fvb.at[1])
+    g_second.append(forward(g_first[4], g_first[4], g.at[1, 4], g.at[2, 4], g.at[3, 4]))
+    fk_second = forward(fk_upper, fk_lower, fkb.at[0], fkb.at[1], fkb.at[2])
+    fv_lower = relay_out(fv, fvb.at[0], fvb.at[1], lower_half)
     second1 = [scatter_middle(0, b, part.at[0], own_lanes, first1[b]) for b in both]
     gathers = []
     for b in both:
@@ -866,7 +888,7 @@
         hid[rs] = (positive * positive).astype(BF)
         pos[rs] = positive.astype(BF)
     onward = gather_middle(cg, moved_lanes, all_rows, gathers)
-    fv_second = forward(fv_first, fvb.at[0], fvb.at[1], fvb.at[2])
+    fv_second = forward(fv_upper, fv_lower, fvb.at[0], fvb.at[1], fvb.at[2])
     gather_end(gathers, onward)
 
     piece = own
@@ -896,7 +918,13 @@
         for way in range(2):
             second[way].wait_recv()
             total = product_piece(lhs, rhs, way) + ff_got[k, way, 0].astype(F32) + ff_got2[k, way].astype(F32)
-            out[way * piece : (way + 1) * piece] = total.astype(BF)
+            ff_send[k, way, 1] = total.astype(BF)
+            own_copies.append(
+                pltpu.make_async_copy(
+                    ff_send.at[k, way, 1], out.at[pl.ds(way * piece, piece)], local.at[1 + 2 * k + way]
+                )
+            )
+            own_copies[-1].start()
 
     tm_first, tm_second, back_copies = {}, {}, []
 
@@ -940,7 +968,8 @@
                 back_out.at[w, pl.ds(0, parts - 1)],
             )
         )
-        back_out[w, m] = sums[m]
+        own_copies.append(pltpu.make_async_copy(sums.at[m], back_out.at[w, m], local.at[5 + w]))
+        own_copies[-1].start()
 
     fv_grad1 = ff_grad_start(0, cg, hid)
 
@@ -965,7 +994,6 @@
     sens[...] = jnp.zeros_like(sens)
     head_small[...] = jnp.zeros_like(head_small)
     gate_first = []
-    out_first = []
     for b in both:
         rs = bucket_rows(b)
         gate = channel_gate[rs]
@@ -988,15 +1016,15 @@
             normed = hat * gain
             change = normed - roll_rows(normed, 1) * same
             now = jnp.zeros((rows, own), F32)
-            later = jnp.zeros((rows, own), F32)
+            whole = jnp.zeros((rows, own), F32)
             for i, (grad, weight_of) in enumerate(grads):
                 value = nt(grad(rs), weight_of(e))
                 at = slice(sens_row + i, sens_row + i + 1)
                 sens[at, cols] += jnp.sum(value * change, axis=0, keepdims=True)
                 weight = order_vec[mix_row + i : mix_row + i + 1, cols]
                 now = now + value * weight
-                later = later + value * (1.0 - weight)
-            back = now + following * roll_rows(later, -1)
+                whole = whole + value
+            back = now + following * roll_rows(whole - now, -1)
             target[rs, cols] = back.astype(BF)
             scaled = back * gain
             one = one + nt(ones, scaled.astype(BF))
@@ -1095,6 +1123,7 @@
     for copies in first3 + second3:
         for copy in copies:
             links.sent(copy)
+    left, right = pl.ds(0, width // 2), pl.ds(width // 2, width // 2)
     first6, stats6 = [], []
     for b in both:
         gather_end(gathers[b], onward[b])
@@ -1102,10 +1131,12 @@
         if b == 1:
             for j in range(4):
                 wo_part[j] = tn(mixed[:, j * LANE_WIDTH : (j + 1) * LANE_WIDTH], branch[...]).astype(BF)
-            wo_copies = [
-                links.push(wo_part.at[peer[0]], wo_got.at[i], peer)
-                for i, peer in enumerate((x_peer, y_peer, diagonal))
+            wo_first = [
+                links.push(wo_part.at[peer[0], :, lanes], wo_got.at[way, i], way_peer)
+                for way, lanes, way_peer, near in ((0, left, x_peer, x_peer), (1, right, y_peer, y_peer))
+                for i, peer in enumerate((near, diagonal))
             ]
+            out_first = gather_start(out_own, out_full, own_lanes, all_rows, keep=11)
         mixed_grad[rs] = nt(branch[rs], wob[...])
         time_backward(b)
         back_mix(
@@ -1121,11 +1152,18 @@
     for b in both:
         second6.append(scatter_middle(3, b, part.at[1], moved_lanes, first6[b]))
         stats6b.append(stats_middle(1, b, stats6[b]))
-    out_first = gather_start(out_own, out_full, own_lanes, all_rows)
-    ff_grad_end(0, cg, hid, fv_grad2, ffv_out)
     tm_grad_middle(4)
+    for copy in wo_first[:2]:
+        copy.wait_recv()
+    wo_send[0] = (wo_part[y_peer[0], :, left].astype(F32) + wo_got[0, 1].astype(F32)).astype(BF)
+    wo_second = [links.push(wo_send.at[0], wo_got2.at[0], y_peer)]
+    for copy in wo_first[2:]:
+        copy.wait_recv()
+    wo_send[1] = (wo_part[x_peer[0], :, right].astype(F32) + wo_got[1, 1].astype(F32)).astype(BF)
+    wo_second.append(links.push(wo_send.at[1], wo_got2.at[1], x_peer))
     tm_grad_middle(0)
     tm_grad_start(2)
+    tm_grad_end(4)
     out_second = gather_middle(out_full, own_lanes, all_rows, out_first)
     opening = jnp.zeros((1, own), F32)
     for b in both:
@@ -1136,10 +1174,10 @@
         opening = opening + jnp.sum(back * hat, axis=0, keepdims=True)
         value = middle_grad[rs] + norm_back(b, back, hat, OPENING, rstd1, means)
         gin_own[rs] = value.astype(BF)
-    gin_first = gather_start(gin_own, gin_full, own_lanes, all_rows)
+    gin_first = gather_start(gin_own, gin_full, own_lanes, all_rows, keep=10)
     tm_grad_middle(1)
     tm_grad_start(3)
-    tm_grad_end(4)
+    tm_grad_end(0)
 
     vec_copies = links.group(
         [sens.at[:, moved_lanes(other)] for other in others],
@@ -1159,10 +1197,10 @@
     dp_copies = links.group(
         [u2_own] * 3, [u2_got.at[i] for i in range(3)], [x_peer, y_peer, diagonal], u2_got
     )
-    tm_grad_end(0)
     tm_grad_middle(2)
     tm_grad_end(1)
     tm_grad_middle(3)
+    tm_grad_end(2)
     dp_copies.wait_recv()
     u3_own[...] = (u2_own[...] + u2_got[0]) + (u2_got[1] + u2_got[2])
     all_copies = links.group(
@@ -1173,13 +1211,12 @@
     )
     u3_got[m] = u3_own[...]
 
+    ff_grad_end(0, cg, hid, fv_grad2, ffv_out)
     ff_grad_end(1, kin, pre, fk_grad2, ffk_out)
-    tm_grad_end(2)
-    total = wo_part[d].astype(F32)
-    for i, copy in enumerate(wo_copies):
-        copy.wait_recv()
-        total = total + wo_got[i].astype(F32)
-    wo_out[...] = total.astype(BF)
+    for way, lanes in enumerate((left, right)):
+        wo_second[way].wait_recv()
+        total = wo_part[d, :, lanes].astype(F32) + wo_got[way, 0].astype(F32) + wo_got2[way].astype(F32)
+        wo_out[:, lanes] = total.astype(BF)
     tm_grad_end(3)
     all_copies.wait_recv()
     upper_d = lax.rem(d, 2) == 1
@@ -1196,6 +1233,8 @@
     gather_end(out_first, out_second)
     for copy in back_copies:
         copy.wait_recv()
+    for copy in own_copies:
+        copy.wait()
     links.finish()
     assert links.used == COPIES, links.used
 
@@ -1204,12 +1243,14 @@
     out, gin, ffk, ffv, back, wo, vec,
     out_o, gin_o, ffk_o, ffv_o, r_o, k_o, v_o, g_o, c_o, wo_o,
     y0, y1, y2, y3, y4, y5, y6, y7, y8, y9, y10,
-    ffk_v, ffv_v, back_v, wo_v, ffk_f, ffv_f, square, read, write,
+    out_v, gin_v, ffk_v, ffv_v, back_v, wo_v, ffk_f, ffv_f, square, read, write,
 ):
     buckets, rows = out_o.shape[:2]
     reads = [
         pltpu.make_async_copy(a, b, read.at[i])
-        for i, (a, b) in enumerate(((ffv, ffv_v), (ffk, ffk_v), (wo, wo_v), (back, back_v)))
+        for i, (a, b) in enumerate(
+            ((ffv, ffv_v), (ffk, ffk_v), (wo, wo_v), (back, back_v), (out, out_v), (gin, gin_v))
+        )
     ]
     for copy in reads:
         copy.start()
@@ -1220,9 +1261,6 @@
         copy.start()
         writes.append(copy)
 
-    for source, target in ((out, out_o), (gin, gin_o)):
-        for b in range(buckets):
-            store(source.at[pl.ds(b * rows, rows)], target.at[b])
     for i, ref in enumerate((y0, y1, y2, y3, y4, y5, y6, y7, y8, y9, y10)):
         ref[...] = vec[i : i + 1]
     for copy, source, middle, target in zip(reads, (ffv_v, ffk_v, wo_v), (ffv_f, ffk_f, square.at[5]), (ffv_o, ffk_o, wo_o)):
@@ -1248,6 +1286,10 @@
                 start = j * 4 * 128 + u * 128
                 square[w, :, start : start + 128] = tile
         store(square.at[w], target)
+    for copy, source, target in ((reads[4], out_v, out_o), (reads[5], gin_v, gin_o)):
+        copy.wait()
+        for b in range(buckets):
+            store(source.at[pl.ds(b * rows, rows)], target.at[b])
     for copy in writes:
         copy.wait()
 
@@ -1286,10 +1328,11 @@
         v((2, 2, 2, own, hidden), BF), v((2, 2, 2, own, hidden), BF), v((2, 2, own, hidden), BF),
         v((5, 2, 2, own, own), BF), v((5, 2, 2, own, own), BF), v((5, 2, own, own), BF),
         v((parts, shard, own), BF),
-        v((4, shard, width), BF), v((3, shard, width), BF), v((rows, own), BF),
+        v((4, shard, width), BF), v((2, 2, shard, width // 2), BF), v((2, shard, width // 2), BF),
+        v((2, shard, width // 2), BF), v((rows, own), BF),
         v((parts - 1, 8, own), F32), v((16, own), F32), v((3, 16, own), F32), v((16, own), F32),
         v((parts, 16, own), F32),
-        pltpu.SemaphoreType.DMA((COPIES,)), pltpu.SemaphoreType.DMA((COPIES,)), pltpu.SemaphoreType.DMA,
+        pltpu.SemaphoreType.DMA((COPIES,)), pltpu.SemaphoreType.DMA((COPIES,)), pltpu.SemaphoreType.DMA((12,)),
     ]
     out = pl.pallas_call(
         block_kernel,
@@ -1299,7 +1342,7 @@
             struct((16, block), F32),
         ],
         in_specs=[pl.BlockSpec(memory_space=sm), vm, pl.BlockSpec(memory_space=pl.ANY)] + [vm] * 19,
-        out_specs=[vm] * 7,
+        out_specs=[pl.BlockSpec(memory_space=pl.ANY)] * 5 + [vm] * 2,
         scratch_shapes=scratch,
         compiler_params=pltpu.CompilerParams(
             collective_id=0, has_side_effects=True, vmem_limit_bytes=VMEM_LIMIT
@@ -1321,9 +1364,9 @@
         in_specs=[hbm] * 6 + [vm],
         out_specs=[hbm] * 10 + [vm] * 11,
         scratch_shapes=[
-            v(fk.shape, BF), v(fv.shape, BF), v((5, parts, shard, own), BF), v((shard, width), BF),
+            v((rows, width), BF), v((rows, width), BF), v(fk.shape, BF), v(fv.shape, BF), v((5, parts, shard, own), BF), v((shard, width), BF),
             v(fk.shape, F32), v(fv.shape, F32), v((6, shard, width), F32),
-            pltpu.SemaphoreType.DMA((4,)), pltpu.SemaphoreType.DMA((2 * buckets + 8,)),
+            pltpu.SemaphoreType.DMA((6,)), pltpu.SemaphoreType.DMA((2 * buckets + 8,)),
         ],
         compiler_params=pltpu.CompilerParams(vmem_limit_bytes=VMEM_LIMIT),
         name="finish",

time: 337 us -> 272 us (0.81)
  Pallas kernels: 336 us -> 271 us
    pallas_call x1, Pallas kernels: 66.2 us -> 6.28 us  [fast_body(): pl.pallas_call(finish_kernel, out_shape=[struct(block_arguments.shape, BF...]
    pallas_call x1, Pallas kernels: 270 us -> 264 us  [fast_body(): pl.pallas_call(block_kernel, out_shape=[struct((rows, width), BF), struct...]
where the time goes in v4:
time: 272 us; the launch traced here: 271 us
  Pallas kernels  271 us (100%)
    pallas_call x1, Pallas kernels, fast_body(): pl.pallas_call(block_kernel, out_shape=[struct((rows, width), BF), struct...  264 us
    pallas_call x1, Pallas kernels, fast_body(): pl.pallas_call(finish_kernel, out_shape=[struct(block_arguments.shape, BF...  6.28 us

profile of v4, /device:TPU:1, one launch (start us, length us, event | category | flops | bytes accessed | tf_op | source)
XLA Modules:
  0.0 271.4 jit_solution(9347629925001772399)
XLA Ops:
  0.7 264.3 %whole_block.1 = (bf16[256,2048]{1,0:T(8,128)(2,1)}, bf16[256,2048]{1,0:T(8,128)(2,1)}, bf16[512,896]{1,0:T(8,128)(2,1)}, bf16[512,896]{1,0:T(8,128)(2,1)}, bf16...) custom-call(s32[2,8]{1,0:T(2,128)} %bitcast.38, bf16[256,2048]{1,0:T(8,128)(2,1)} %bitcast.25, ...), custom_call_target="tpu_custom_call" | custom-call | tf_op jit(solution)/shard_map/whole_block/pallas_call | solution.py:1337
  265.0 6.3 %finish.1 = (bf16[2,128,2048]{2,1,0:T(8,128)(2,1)}, bf16[2,128,2048]{2,1,0:T(8,128)(2,1)}, f32[512,896]{1,0:T(8,128)}, f32[512,896]{1,0:T(8,128)}, f32[64,2048]{...) custom-call(bf16[256,2048]{1,0:T(8,128)(2,1)} %get-tuple-element.49., ...), custom_call_target="tpu_custom_call" | custom-call | tf_op jit(solution)/shard_map/finish/pallas_call | solution.py:1357

commit v5 on v4

--- a/solution.py
+++ b/solution.py
@@ -558,8 +558,6 @@
                     tile = jnp.where(low16, swap_halves(tiles[0]), tiles[1])
                 blocks[w, to, :, q * 128 : (q + 1) * 128] = tile.astype(BF)
 
-    for w, weight in enumerate((w_recept, w_key, w_value, w_gate)):
-        head_blocks(w, weight)
     pl.semaphore_wait(barrier, len(greeted))
     top_copy.wait()
 
@@ -594,16 +592,19 @@
         return (one, two) + (() if upper_copies is lower_copies else (upper_copies[1], lower_copies[0]))
 
     fk_upper = relay_out(fk, fkb.at[0], fkb.at[1], upper_half)
-    arrivals = [exchange(w) for w in range(4)]
+
+    def out_rows(dp_place, start, size):
+        return pl.ds(pl.multiple_of(dp_place * shard + start, 32), size)
+
+    wo_first = [links.push(w_out, wob.at[out_rows(d, 0, shard)], peer) for peer in (x_peer, y_peer)]
+    arrivals = []
+    for w, weight in enumerate((w_recept, w_key, w_value, w_gate)):
+        head_blocks(w, weight)
+        arrivals.append(exchange(w))
     arrivals.append(exchange(4))
     for w in range(4):
         g[0, w, my_rows] = blocks[w, m]
     g[0, 4, my_rows] = w_channel[:, own_lanes(m)]
-
-    def out_rows(dp_place, start, size):
-        return pl.ds(pl.multiple_of(dp_place * shard + start, 32), size)
-
-    wo_first = [links.push(w_out, wob.at[out_rows(d, 0, shard)], peer) for peer in (x_peer, y_peer)]
     wob[out_rows(d, 0, shard)] = w_out[...]
 
     for j in range(4):
@@ -887,8 +888,8 @@
         positive = jnp.maximum(total, 0.0)
         hid[rs] = (positive * positive).astype(BF)
         pos[rs] = positive.astype(BF)
+    fv_second = forward(fv_upper, fv_lower, fvb.at[0], fvb.at[1], fvb.at[2])
     onward = gather_middle(cg, moved_lanes, all_rows, gathers)
-    fv_second = forward(fv_upper, fv_lower, fvb.at[0], fvb.at[1], fvb.at[2])
     gather_end(gathers, onward)
 
     piece = own
@@ -905,14 +906,17 @@
         )
 
     def ff_grad_middle(k, lhs, rhs, first):
-        first[0].wait_recv()
-        links.sent(first[0])
-        ff_send[k, 0, 0] = (product_piece(lhs, rhs, 4) + ff_got[k, 0, 1].astype(F32)).astype(BF)
-        one = links.push(ff_send.at[k, 0, 0], ff_got2.at[k, 0], y_peer)
-        first[1].wait_recv()
-        links.sent(first[1])
-        ff_send[k, 1, 0] = (product_piece(lhs, rhs, 3) + ff_got[k, 1, 1].astype(F32)).astype(BF)
-        return one, links.push(ff_send.at[k, 1, 0], ff_got2.at[k, 1], x_peer)
+        for way, i in ((0, 4), (1, 3)):
+            value = product_piece(lhs, rhs, i)
+            first[way].wait_recv()
+            links.sent(first[way])
+            ff_send[k, way, 0] = (value + ff_got[k, way, 1].astype(F32)).astype(BF)
+
+    def ff_grad_relay(k):
+        return (
+            links.push(ff_send.at[k, 0, 0], ff_got2.at[k, 0], y_peer),
+            links.push(ff_send.at[k, 1, 0], ff_got2.at[k, 1], x_peer),
+        )
 
     def ff_grad_end(k, lhs, rhs, second, out):
         for way in range(2):
@@ -1063,7 +1067,8 @@
     for b in both:
         second4.append(scatter_middle(2, b, part.at[0], moved_lanes, first4[b]))
         stats4b.append(stats_middle(0, b, stats4[b]))
-    fv_grad2 = ff_grad_middle(0, cg, hid, fv_grad1)
+    ff_grad_middle(0, cg, hid, fv_grad1)
+    fv_grad2 = ff_grad_relay(0)
 
     def norm_back(b, back, hat, gain_row, rstd, means):
         gain = vec[gain_row : gain_row + 1, own_lanes(m)]
@@ -1082,7 +1087,7 @@
         branch_own[rs] = value.astype(BF)
         gathers.append(gather_start(branch_own, branch, own_lanes, slices[b]))
     onward = [gather_middle(branch, own_lanes, slices[b], gathers[b]) for b in both]
-    fk_grad2 = ff_grad_middle(1, kin, pre, fk_grad1)
+    out_first = gather_start(out_own, out_full, own_lanes, all_rows, keep=11)
 
     def time_backward(b):
         rs = bucket_rows(b)
@@ -1123,6 +1128,7 @@
     for copies in first3 + second3:
         for copy in copies:
             links.sent(copy)
+    wo_second = []
     left, right = pl.ds(0, width // 2), pl.ds(width // 2, width // 2)
     first6, stats6 = [], []
     for b in both:
@@ -1136,7 +1142,6 @@
                 for way, lanes, way_peer, near in ((0, left, x_peer, x_peer), (1, right, y_peer, y_peer))
                 for i, peer in enumerate((near, diagonal))
             ]
-            out_first = gather_start(out_own, out_full, own_lanes, all_rows, keep=11)
         mixed_grad[rs] = nt(branch[rs], wob[...])
         time_backward(b)
         back_mix(
@@ -1148,23 +1153,25 @@
 
     for w in (0, 1):
         tm_grad_start(w)
+    vec_copies = links.group(
+        [sens.at[:, moved_lanes(other)] for other in others],
+        [u_got.at[i] for i in range(parts - 1)],
+        [(d, other) for other in others],
+        u_got,
+    )
     second6, stats6b = [], []
     for b in both:
         second6.append(scatter_middle(3, b, part.at[1], moved_lanes, first6[b]))
         stats6b.append(stats_middle(1, b, stats6[b]))
+    out_second = gather_middle(out_full, own_lanes, all_rows, out_first)
     tm_grad_middle(4)
-    for copy in wo_first[:2]:
-        copy.wait_recv()
-    wo_send[0] = (wo_part[y_peer[0], :, left].astype(F32) + wo_got[0, 1].astype(F32)).astype(BF)
-    wo_second = [links.push(wo_send.at[0], wo_got2.at[0], y_peer)]
-    for copy in wo_first[2:]:
-        copy.wait_recv()
-    wo_send[1] = (wo_part[x_peer[0], :, right].astype(F32) + wo_got[1, 1].astype(F32)).astype(BF)
-    wo_second.append(links.push(wo_send.at[1], wo_got2.at[1], x_peer))
-    tm_grad_middle(0)
-    tm_grad_start(2)
-    tm_grad_end(4)
-    out_second = gather_middle(out_full, own_lanes, all_rows, out_first)
+    ff_grad_middle(1, kin, pre, fk_grad1)
+    for way, (lanes, near, peer) in enumerate(((left, y_peer, y_peer), (right, x_peer, x_peer))):
+        for copy in wo_first[2 * way : 2 * way + 2]:
+            copy.wait_recv()
+        value = wo_part[near[0], :, lanes].astype(F32) + wo_got[way, 1].astype(F32)
+        wo_send[way] = value.astype(BF)
+        wo_second.append(links.push(wo_send.at[way], wo_got2.at[way], peer))
     opening = jnp.zeros((1, own), F32)
     for b in both:
         rs = bucket_rows(b)
@@ -1175,17 +1182,13 @@
         value = middle_grad[rs] + norm_back(b, back, hat, OPENING, rstd1, means)
         gin_own[rs] = value.astype(BF)
     gin_first = gather_start(gin_own, gin_full, own_lanes, all_rows, keep=10)
+    tm_grad_middle(0)
+    tm_grad_start(2)
     tm_grad_middle(1)
     tm_grad_start(3)
-    tm_grad_end(0)
-
-    vec_copies = links.group(
-        [sens.at[:, moved_lanes(other)] for other in others],
-        [u_got.at[i] for i in range(parts - 1)],
-        [(d, other) for other in others],
-        u_got,
-    )
+    tm_grad_end(4)
     gin_second = gather_middle(gin_full, own_lanes, all_rows, gin_first)
+
     vec_copies.wait_recv()
     total = sens[:, moved_lanes(m)]
     for i in range(parts - 1):
@@ -1197,10 +1200,12 @@
     dp_copies = links.group(
         [u2_own] * 3, [u2_got.at[i] for i in range(3)], [x_peer, y_peer, diagonal], u2_got
     )
+    tm_grad_end(0)
     tm_grad_middle(2)
+    tm_grad_middle(3)
     tm_grad_end(1)
-    tm_grad_middle(3)
     tm_grad_end(2)
+    fk_grad2 = ff_grad_relay(1)
     dp_copies.wait_recv()
     u3_own[...] = (u2_own[...] + u2_got[0]) + (u2_got[1] + u2_got[2])
     all_copies = links.group(
@@ -1211,13 +1216,13 @@
     )
     u3_got[m] = u3_own[...]
 
+    tm_grad_end(3)
     ff_grad_end(0, cg, hid, fv_grad2, ffv_out)
-    ff_grad_end(1, kin, pre, fk_grad2, ffk_out)
     for way, lanes in enumerate((left, right)):
         wo_second[way].wait_recv()
         total = wo_part[d, :, lanes].astype(F32) + wo_got[way, 0].astype(F32) + wo_got2[way].astype(F32)
         wo_out[:, lanes] = total.astype(BF)
-    tm_grad_end(3)
+    ff_grad_end(1, kin, pre, fk_grad2, ffk_out)
     all_copies.wait_recv()
     upper_d = lax.rem(d, 2) == 1
     low_vec = lax.broadcasted_iota(jnp.int32, (8, 128), 1) < LANE_WIDTH

time: 272 us -> 251 us (0.923)
  Pallas kernels: 271 us -> 249 us
    pallas_call x1, Pallas kernels: 264 us -> 243 us  [fast_body(): pl.pallas_call(block_kernel, out_shape=[struct((rows, width), BF), struct...]
where the time goes in v5:
time: 251 us; the launch traced here: 250 us
  Pallas kernels  249 us (99%)
    pallas_call x1, Pallas kernels, fast_body(): pl.pallas_call(block_kernel, out_shape=[struct((rows, width), BF), struct...  243 us
    pallas_call x1, Pallas kernels, fast_body(): pl.pallas_call(finish_kernel, out_shape=[struct(block_arguments.shape, BF...  6.28 us

profile of v5, /device:TPU:1, one launch (start us, length us, event | category | flops | bytes accessed | tf_op | source)
XLA Modules:
  0.0 250.1 jit_solution(7080554478962831021)
XLA Ops:
  0.7 243.0 %whole_block.1 = (bf16[256,2048]{1,0:T(8,128)(2,1)}, bf16[256,2048]{1,0:T(8,128)(2,1)}, bf16[512,896]{1,0:T(8,128)(2,1)}, bf16[512,896]{1,0:T(8,128)(2,1)}, bf16...) custom-call(s32[2,8]{1,0:T(2,128)} %bitcast.38, bf16[256,2048]{1,0:T(8,128)(2,1)} %bitcast.25, ...), custom_call_target="tpu_custom_call" | custom-call | tf_op jit(solution)/shard_map/whole_block/pallas_call | solution.py:1342
  243.6 6.3 %finish.1 = (bf16[2,128,2048]{2,1,0:T(8,128)(2,1)}, bf16[2,128,2048]{2,1,0:T(8,128)(2,1)}, f32[512,896]{1,0:T(8,128)}, f32[512,896]{1,0:T(8,128)}, f32[64,2048]{...) custom-call(bf16[256,2048]{1,0:T(8,128)(2,1)} %get-tuple-element.49., ...), custom_call_target="tpu_custom_call" | custom-call | tf_op jit(solution)/shard_map/finish/pallas_call | solution.py:1362

commit v6 on v5

--- a/solution.py
+++ b/solution.py
@@ -1204,8 +1204,8 @@
     tm_grad_middle(2)
     tm_grad_middle(3)
     tm_grad_end(1)
+    fk_grad2 = ff_grad_relay(1)
     tm_grad_end(2)
-    fk_grad2 = ff_grad_relay(1)
     dp_copies.wait_recv()
     u3_own[...] = (u2_own[...] + u2_got[0]) + (u2_got[1] + u2_got[2])
     all_copies = links.group(

time: 251 us -> 251 us (level)
  no operation moved by 1% of the time
where the time goes in v6:
time: 251 us; the launch traced here: 250 us
  Pallas kernels  249 us (99%)
    pallas_call x1, Pallas kernels, fast_body(): pl.pallas_call(block_kernel, out_shape=[struct((rows, width), BF), struct...  243 us
    pallas_call x1, Pallas kernels, fast_body(): pl.pallas_call(finish_kernel, out_shape=[struct(block_arguments.shape, BF...  6.28 us

profile of v6, /device:TPU:1, one launch (start us, length us, event | category | flops | bytes accessed | tf_op | source)
XLA Modules:
  0.0 250.1 jit_solution(1911543213331898466)
XLA Ops:
  0.7 243.0 %whole_block.1 = (bf16[256,2048]{1,0:T(8,128)(2,1)}, bf16[256,2048]{1,0:T(8,128)(2,1)}, bf16[512,896]{1,0:T(8,128)(2,1)}, bf16[512,896]{1,0:T(8,128)(2,1)}, bf16...) custom-call(s32[2,8]{1,0:T(2,128)} %bitcast.38, bf16[256,2048]{1,0:T(8,128)(2,1)} %bitcast.25, ...), custom_call_target="tpu_custom_call" | custom-call | tf_op jit(solution)/shard_map/whole_block/pallas_call | solution.py:1342
  243.6 6.3 %finish.1 = (bf16[2,128,2048]{2,1,0:T(8,128)(2,1)}, bf16[2,128,2048]{2,1,0:T(8,128)(2,1)}, f32[512,896]{1,0:T(8,128)}, f32[512,896]{1,0:T(8,128)}, f32[64,2048]{...) custom-call(bf16[256,2048]{1,0:T(8,128)(2,1)} %get-tuple-element.49., ...), custom_call_target="tpu_custom_call" | custom-call | tf_op jit(solution)/shard_map/finish/pallas_call | solution.py:1362
